TPU v7x, 32 devices: a whole 2x2x4 slice. The times are simulated.
32 devices in a mesh: leaf: 8 (over z, y), rows: 4 (over x, core).
Axes of the slice: x: 2, y: 2, z: 4, core: 2. Of those that a mesh axis runs over, the one named last changes fastest.
Arguments:
- factor_zero: bfloat16 [4096, 4096], P('leaf', 'rows'), may hold values from -1 to 3, as said below
- factor_one: bfloat16 [8192, 4096], P('leaf', 'rows'), may hold values from -1 to 3, as said below
- factor_two: bfloat16 [16384, 4096], P('leaf', 'rows'), may hold values from -1 to 3, as said below
- factor_three: bfloat16 [32768, 4096], P('leaf', 'rows'), may hold values from -1 to 3, as said below
- coupling_one: bfloat16 [8192, 1, 4096], P('leaf', None, 'rows'), may hold values from -0.046875 to 0.046875
- coupling_two: bfloat16 [16384, 2, 4096], P('leaf', None, 'rows'), may hold values from -0.046875 to 0.046875
- coupling_three: bfloat16 [32768, 3, 4096], P('leaf', None, 'rows'), may hold values from -0.046875 to 0.046875
- noise_zero: bfloat16 [4096, 128], P('leaf'), may hold values from -6 to 6
- noise_one: bfloat16 [8192, 128], P('leaf'), may hold values from -6 to 6
- noise_two: bfloat16 [16384, 128], P('leaf'), may hold values from -6 to 6
- noise_three: bfloat16 [32768, 128], P('leaf'), may hold values from -6 to 6
- tail_index: int32 [16], replicated, may hold values from 0 to 127
Outputs:
- grad_zero: float32 [4096, 128], P('leaf')
- grad_one: float32 [8192, 128], P('leaf')
- grad_two: float32 [16384, 128], P('leaf')
- grad_three: float32 [32768, 128], P('leaf')
- tail_loss: float32 [], replicated
Inputs may be any that keep to these rules, and one draw needn't show every extreme that they name: `factor_zero`: each 4096 x 4096 node block is lower triangular with a positive diagonal. `factor_one`: each 4096 x 4096 node block is lower triangular with a positive diagonal. `factor_two`: each 4096 x 4096 node block is lower triangular with a positive diagonal. `factor_three`: each 4096 x 4096 node block is lower triangular with a positive diagonal.
All inputs are finite; a program needn't handle non-finite values.
Results may differ from a plain program's by a relative error of at most 0.008.
Values sent between devices are 32-bit elements; how exact they have to be, the bound alone decides.
No kernel may reach another device: no remote copies, remote signals or barrier semaphores. Data moves between devices by JAX's collectives and lax.ppermute only.
A program may use at most 192 MiB of HBM per device.

v0:
```python
import functools

import jax
import jax.numpy as jnp
from jax import lax
from jax.experimental import pallas as pl
from jax.experimental.pallas import tpu as pltpu
from jax.sharding import PartitionSpec as P

LEVELS = 4


tail_level = 0.5


def swapped(x, axis, apart):
    return lax.ppermute(x, axis, [(i, i ^ 1 << apart) for i in range(lax.axis_size(axis))])


def bits_of(axis):
    return lax.axis_size(axis).bit_length() - 1


VMEM = pl.BlockSpec(memory_space=pltpu.VMEM)
HBM = pl.BlockSpec(memory_space=pltpu.HBM)


def in_hbm(array):
    return pltpu.with_memory_space_constraint(array, pltpu.HBM)


def in_vmem(array):
    return pltpu.with_memory_space_constraint(array, pltpu.VMEM)


def kernel_params():
    return pltpu.CompilerParams(vmem_limit_bytes=14 * 1024 * 1024)


def cost(rows, width, scenarios):
    return pl.CostEstimate(flops=scenarios, transcendentals=0, bytes_accessed=scenarios)


def block_rows(rows):
    return min(rows, max(128, rows // 4))


def first_row(chunk, side, count):
    if side is None:
        return chunk * count
    low = lax.axis_index("rows") & 1
    return (2 * chunk + (low if side == 0 else 1 - low)) * count


def block_copy(matrix_ref, plane, first, block, number, buffer_ref, base, sems, sem_base):
    start = pl.multiple_of(first + number * block, block)
    place = pl.multiple_of(base + number * block, block)
    return pltpu.make_async_copy(
        matrix_ref.at[plane, pl.ds(start, block), :],
        buffer_ref.at[pl.ds(place, block), :],
        sems.at[sem_base + number],
    )


def apply_body(plane, chunk, side, count, has_base, matrix_ref, vector_ref, *refs):
    start = first_row(chunk, side, count)
    if plane is None:
        rows = pl.ds(pl.multiple_of(start, count), count)
        product = jnp.dot(matrix_ref[rows, :], vector_ref[...], preferred_element_type=jnp.float32)
        if has_base:
            product = product + refs[0][rows, :]
        refs[-1][...] = product
        return
    out_ref, buffer_ref, sems = refs[-3:]
    block = block_rows(count)
    blocks = count // block
    for number in range(blocks):
        block_copy(matrix_ref, plane, start, block, number, buffer_ref, 0, sems, 0).start()

    def step(number, carry):
        block_copy(matrix_ref, plane, start, block, number, buffer_ref, 0, sems, 0).wait()
        rows = pl.ds(pl.multiple_of(number * block, block), block)
        product = jnp.dot(buffer_ref[rows, :], vector_ref[...], preferred_element_type=jnp.float32)
        if has_base:
            product = product + refs[0][pl.ds(pl.multiple_of(start + number * block, block), block), :]
        out_ref[rows, :] = product
        return carry

    lax.fori_loop(0, blocks, step, 0)


def apply_rows(matrix, plane, vector, base, chunk, side, chunks):
    rows, width = matrix.shape[-2:]
    count = rows // chunks if side is None else rows // chunks // 2
    scenarios = vector.shape[1]
    held = plane is None
    operands = [in_vmem(matrix) if held else in_hbm(matrix), in_vmem(vector)]
    operands += [] if base is None else [in_vmem(base)]
    return pl.pallas_call(
        functools.partial(apply_body, plane, chunk, side, count, base is not None),
        out_shape=pltpu.VMEM((count, scenarios), jnp.float32),
        in_specs=[VMEM if held else HBM] + [VMEM] * (len(operands) - 1),
        out_specs=VMEM,
        scratch_shapes=[]
        if held
        else [
            pltpu.VMEM((count, width), jnp.bfloat16),
            pltpu.SemaphoreType.DMA((count // block_rows(count),)),
        ],
        compiler_params=kernel_params(),
        cost_estimate=cost(count, width, scenarios),
    )(*operands)


def across_body(plane, count, sides, has_noise, has_terms, has_base, old_exact, new_exact, *refs):
    refs = list(refs)
    matrix_ref = refs.pop(0)
    noise_ref = refs.pop(0) if has_noise else None
    terms_refs = [refs.pop(0) for _ in sides] if has_terms else None
    base_ref = refs.pop(0) if has_base else None
    if old_exact:
        refs.pop(0)
    out_ref = refs.pop(0)
    exact_ref = refs.pop(0) if new_exact else None
    total_ref = refs.pop(0)
    streamed = plane is not None
    buffer_ref, sems = (refs.pop(0), refs.pop(0)) if streamed else (None, None)
    right_ref, right_sems = refs[:2] if has_noise else (None, None)
    exact_sems = refs[-1] if new_exact else None
    block = block_rows(count)
    blocks = count // block

    def first(part):
        return first_row(*sides[part], count)

    def noise_copy(part):
        return pltpu.make_async_copy(
            noise_ref.at[pl.ds(pl.multiple_of(first(part), count), count), :],
            right_ref.at[pl.ds(part * count, count), :],
            right_sems.at[part],
        )

    def exact_copy(part):
        return pltpu.make_async_copy(
            terms_refs[part],
            exact_ref.at[pl.ds(pl.multiple_of(first(part), count), count), :],
            exact_sems.at[part],
        )

    def matrix_copy(part, number):
        return block_copy(
            matrix_ref, plane, first(part), block, number, buffer_ref, part * count, sems, part * blocks
        )

    for part in range(len(sides)):
        if has_noise:
            noise_copy(part).start()
        for number in range(blocks if streamed else 0):
            matrix_copy(part, number).start()
    if new_exact:
        for part in range(len(sides)):
            exact_copy(part).start()
    if has_base:
        total_ref[...] = base_ref[...].T
    else:
        total_ref[...] = jnp.zeros_like(total_ref)
    for part in range(len(sides)):
        if has_noise:
            noise_copy(part).wait()

        def step(number, carry):
            if streamed:
                matrix_copy(part, number).wait()
            inner = pl.ds(pl.multiple_of(number * block, block), block)
            held = pl.ds(pl.multiple_of(part * count + number * block, block), block)
            if not has_noise:
                right = terms_refs[part][inner, :].astype(jnp.bfloat16)
            elif not has_terms:
                right = right_ref[held, :]
            else:
                right = right_ref[held, :].astype(jnp.float32) - terms_refs[part][inner, :]
                right = right.astype(jnp.bfloat16)
            if streamed:
                matrix = buffer_ref[held, :]
            else:
                matrix = matrix_ref[pl.ds(pl.multiple_of(first(part) + number * block, block), block), :]
            total_ref[...] += lax.dot_general(
                right, matrix, (((0,), (0,)), ((), ())), preferred_element_type=jnp.float32
            )
            return carry

        lax.fori_loop(0, blocks, step, 0)
    out_ref[...] = total_ref[...].T
    if new_exact:
        for part in range(len(sides)):
            exact_copy(part).wait()


def across_rows(matrix, plane, parts, count, noise=None, base=None, exact=None, give_exact=False):
    rows, width = matrix.shape[-2:]
    scenarios = (parts[0][0] if noise is None else noise).shape[1]
    sides = tuple((chunk, side) for _, chunk, side in parts)
    has_terms = parts[0][0] is not None
    streamed = plane is not None
    operands = [in_hbm(matrix) if streamed else in_vmem(matrix)]
    in_specs = [HBM if streamed else VMEM]
    if noise is not None:
        operands.append(in_hbm(noise))
        in_specs.append(HBM)
    if has_terms:
        operands += [in_vmem(terms) for terms, _, _ in parts]
        in_specs += [VMEM] * len(parts)
    if base is not None:
        operands.append(in_vmem(base))
        in_specs.append(VMEM)
    aliases = {}
    if exact is not None:
        operands.append(in_hbm(exact))
        in_specs.append(HBM)
        aliases = {len(operands) - 1: 1}
    out_shape = [pltpu.VMEM((width, scenarios), jnp.float32)]
    out_specs = [VMEM]
    held = len(parts) * count
    scratch = [pltpu.VMEM((scenarios, width), jnp.float32)]
    if streamed:
        scratch.append(pltpu.VMEM((held, width), jnp.bfloat16))
        scratch.append(pltpu.SemaphoreType.DMA((held // block_rows(count),)))
    if noise is not None:
        scratch += [pltpu.VMEM((held, scenarios), jnp.bfloat16), pltpu.SemaphoreType.DMA((len(parts),))]
    if give_exact:
        out_shape.append(pltpu.HBM((rows, scenarios), jnp.float32))
        out_specs.append(HBM)
        scratch.append(pltpu.SemaphoreType.DMA((len(parts),)))
    results = pl.pallas_call(
        functools.partial(
            across_body, plane, count, sides, noise is not None, has_terms, base is not None,
            exact is not None, give_exact,
        ),
        out_shape=tuple(out_shape),
        in_specs=in_specs,
        out_specs=tuple(out_specs),
        scratch_shapes=scratch,
        input_output_aliases=aliases,
        compiler_params=kernel_params(),
        cost_estimate=cost(held, width, scenarios),
    )(*operands)
    return tuple(results) if give_exact else results[0]


def load_body(plane, matrix_ref, ticket_ref, held_ref, out_ticket_ref, sems):
    copies = []
    block = block_rows(held_ref.shape[0])
    for number in range(held_ref.shape[0] // block):
        rows = pl.ds(number * block, block)
        copies.append(
            pltpu.make_async_copy(matrix_ref.at[plane, rows, :], held_ref.at[rows, :], sems.at[number])
        )
    for copy in copies:
        copy.start()
    out_ticket_ref[...] = ticket_ref[...]
    for copy in copies:
        copy.wait()


def load(matrix, plane, ticket):
    _, rows, width = matrix.shape
    return pl.pallas_call(
        functools.partial(load_body, plane),
        out_shape=(
            pltpu.VMEM((rows, width), matrix.dtype),
            pltpu.VMEM(ticket.shape, ticket.dtype),
        ),
        in_specs=[HBM, VMEM],
        out_specs=(VMEM, VMEM),
        scratch_shapes=[pltpu.SemaphoreType.DMA((rows // block_rows(rows),))],
        compiler_params=kernel_params(),
        cost_estimate=cost(rows, width, ticket.shape[1]),
    )(in_hbm(matrix), ticket)


def place_body(count, own_ref, other_ref, exact_ref, sems):
    copies = []
    for side, terms_ref in enumerate((own_ref, other_ref)):
        start = pl.multiple_of(first_row(0, side, count), count)
        copies.append(
            pltpu.make_async_copy(terms_ref, exact_ref.at[pl.ds(start, count), :], sems.at[side])
        )
    for copy in copies:
        copy.start()
    for copy in copies:
        copy.wait()


def place_rows(own, other):
    count, scenarios = own.shape
    return pl.pallas_call(
        functools.partial(place_body, count),
        out_shape=pltpu.HBM((2 * count, scenarios), jnp.float32),
        in_specs=[VMEM, VMEM],
        out_specs=HBM,
        scratch_shapes=[pltpu.SemaphoreType.DMA((2,))],
        compiler_params=kernel_params(),
    )(in_vmem(own), in_vmem(other))


def tied(first, second):
    return lax.optimization_barrier((first, second))


def run_jobs(jobs, inputs):
    return [job[1](given) for job, given in zip(jobs, inputs)]


def keep_results(jobs, results):
    for job, result in zip(jobs, results):
        job[2](result)


class Waits:
    def __init__(self):
        self.queue = []

    def put(self, *jobs):
        self.queue.append(list(jobs))

    def take(self):
        return self.queue.pop(0) if self.queue else []

    def drain(self):
        for jobs in self.queue:
            for job in jobs:
                job[2](job[1](job[0]()))
        self.queue = []


def exchanges(values, axis_positions, jobs=()):
    inputs = [job[0]() for job in jobs]
    values, inputs = tied(list(values), inputs)
    got = [swapped(value, axis, position) for value, (axis, position) in zip(values, axis_positions)]
    got, results = tied(got, run_jobs(jobs, inputs))
    keep_results(jobs, results)
    return values, got


def exchange(value, axis, position, jobs=()):
    values, got = exchanges([value], [(axis, position)], jobs)
    return values[0], got[0]


def halve(value, position, leaf_index, jobs):
    half_rows = value.shape[0] // 2
    upper = leaf_index >> position & 1
    kept = lax.dynamic_slice_in_dim(value, upper * half_rows, half_rows, 0)
    sent = lax.dynamic_slice_in_dim(value, (1 - upper) * half_rows, half_rows, 0)
    _, got = exchange(sent, "leaf", position, jobs)
    return kept + got


def double(value, position, leaf_index, jobs):
    value, partner = exchange(value, "leaf", position, jobs)
    upper = leaf_index >> position & 1
    return jnp.where(
        upper == 1,
        jnp.concatenate([partner, value], axis=0),
        jnp.concatenate([value, partner], axis=0),
    )


def group_sum(value, group_bits, leaf_index, waits):
    if group_bits == 0:
        return value
    if group_bits == 1:
        value, got = exchange(value, "leaf", 0, waits.take())
        return value + got
    if group_bits == 2:
        middle = value.shape[0] // 2
        parts = [value[:middle], value[middle:]]
        for positions in ((0, 1), (1, 0)):
            parts, got = exchanges(parts, [("leaf", position) for position in positions], waits.take())
            parts = [part + more for part, more in zip(parts, got)]
        return jnp.concatenate(parts, axis=0)
    for position in range(2):
        value = halve(value, position, leaf_index, waits.take())
    for position in range(2, group_bits):
        value, got = exchange(value, "leaf", position, waits.take())
        value = value + got
    for position in reversed(range(2)):
        value = double(value, position, leaf_index, waits.take())
    return value


def chunks_of(rows):
    return 2 if rows >= 4096 else 1


def rows_stage(produce, consume, chunks, waits):
    bits = bits_of("rows")
    owns = []
    for chunk in range(chunks):
        sent = produce(chunk, 1, owns[-1] if owns else None)
        kept = []
        job = (lambda: (), lambda _: produce(chunk, 0, sent), kept.append)
        _, got = exchange(sent, "rows", 0, [job])
        owns.append(kept[0] + got)
    gots = [swapped(own, "rows", 1) for own in owns]
    jobs = waits.take()
    owns[-1], inputs = tied(owns[-1], [job[0]() for job in jobs])
    gots[0], results = tied(gots[0], run_jobs(jobs, inputs))
    keep_results(jobs, results)
    state = None
    for chunk in range(chunks):
        got = gots[chunk]
        if chunk > 0:
            got, state = tied(got, state)
        own = owns[chunk] + got
        for position in range(2, bits):
            own = own + swapped(own, "rows", position)
        owns[chunk] = own
        if chunk + 1 < chunks:
            state = consume([(own, chunk, 0)], state)
    states = [state]
    job = (
        lambda: (owns[-1], state),
        lambda given: consume([(given[0], chunks - 1, 0)], given[1]),
        lambda result: states.append(result),
    )
    owns, others = exchanges(owns, [("rows", 0)] * chunks, [job])
    state = consume([(other, chunk, 1) for chunk, other in enumerate(others)], states[-1])
    parts = [(own, chunk, 0) for chunk, own in enumerate(owns)]
    parts += [(other, chunk, 1) for chunk, other in enumerate(others)]
    return state, parts


def on_device(
    factor_zero,
    factor_one,
    factor_two,
    factor_three,
    coupling_one,
    coupling_two,
    coupling_three,
    noise_zero,
    noise_one,
    noise_two,
    noise_three,
    tail_index,
):
    factors = [factor[None] for factor in (factor_zero, factor_one, factor_two, factor_three)]
    noises = [noise_zero, noise_one, noise_two, noise_three]
    couplings = {
        1: [jnp.transpose(coupling_one, (1, 0, 2))],
        2: [],
        3: [jnp.transpose(coupling_three, (1, 0, 2))],
    }
    leaf_bits = bits_of("leaf")
    leaf_index = lax.axis_index("leaf")
    width = factor_zero.shape[1]
    full_width = width * lax.axis_size("rows")
    scenario_count = noise_zero.shape[1]
    columns = jnp.arange(scenario_count, dtype=jnp.int32)
    counts = jnp.sum((tail_index[:, None] == columns[None, :]).astype(jnp.float32), axis=0)
    weights = 1.0 + counts

    early = {}
    held = {}
    tickets = [jnp.zeros((8, scenario_count), jnp.float32)]

    def load_job(name, plane):
        kind, level = name

        def run(given):
            matrix = factors[level] if kind == "factor" else couplings[level][0]
            held[name], out = load(matrix, plane, given)
            return out

        return (lambda: tickets[-1], run, tickets.append)

    def matrix_of(kind, level, plane):
        if (kind, level) in held:
            return held[kind, level], None
        return (factors[level] if kind == "factor" else couplings[level][0]), plane

    def turn_job():
        return (lambda: coupling_two, lambda given: jnp.transpose(given, (1, 0, 2)), couplings[2].append)

    def early_job(level, plane, vector):
        def run(given):
            return apply_rows(couplings[level][0], plane, given, early.get(level), 0, None, 1)

        return (lambda: vector, run, lambda result: early.__setitem__(level, result))

    def work(*steps):
        waits = Waits()
        for jobs in steps:
            waits.put(*jobs)
        return waits

    samples = []
    for tree_level in range(LEVELS):
        group_bits = leaf_bits - tree_level
        if tree_level == 0:
            part = across_rows(factors[0], 0, [(None, 0, None)], noise_zero.shape[0], noise=noise_zero)
        else:
            plane = tree_level - 1
            last = samples[-1].astype(jnp.bfloat16)
            if tree_level == 1:
                waits = work([turn_job()])
            elif tree_level == 2:
                waits = work([early_job(3, 1, last), load_job(("factor", 2), 0)])
            else:
                waits = work([load_job(("factor", 3), 0)])
            chunks = chunks_of(factors[tree_level].shape[1])

            def produce(chunk, side, after):
                vector = last
                if after is not None:
                    vector, _ = tied(vector, after)
                return apply_rows(
                    *matrix_of("coupling", tree_level, plane), vector, early.get(tree_level), chunk, side, chunks
                )

            factor = factors[tree_level]
            count = factor.shape[1] // chunks // 2

            def consume(parts, state):
                return across_rows(
                    *matrix_of("factor", tree_level, 0), parts, count, noise=noises[tree_level], base=state
                )

            part, _ = rows_stage(produce, consume, chunks, waits)
        if tree_level == 0:
            waits = work([], [], [], [], [load_job(("coupling", 1), 0), load_job(("factor", 1), 0)])
        elif tree_level == 1:
            waits = work(
                [early_job(3, 0, last)],
                [early_job(2, 0, last), load_job(("coupling", 2), 1)],
            )
        elif tree_level == 2:
            waits = work([load_job(("coupling", 3), 2)])
        else:
            waits = work()
        samples.append(group_sum(part, group_bits, leaf_index, waits))
        waits.drain()

    losses = []

    def loss_job(given):
        total = jnp.zeros((8, scenario_count), jnp.float32)
        for tree_level in range(LEVELS):
            group_bits = leaf_bits - tree_level
            piece_rows = given[tree_level].shape[0] >> group_bits
            member = leaf_index & (1 << group_bits) - 1
            own_rows = lax.dynamic_slice_in_dim(given[tree_level], member * piece_rows, piece_rows, 0)
            terms = weights[None, :] * jax.nn.softplus(own_rows - tail_level)
            total = total + jnp.sum(terms.reshape(-1, 8, scenario_count), axis=0)
        return total

    steps = [("leaf", position) for position in range(leaf_bits)]
    steps += [("rows", position) for position in range(bits_of("rows"))]

    def sum_job(count):
        def run(given):
            for _ in range(count):
                if steps:
                    axis, position = steps.pop(0)
                    given = given + swapped(given, axis, position)
            return given

        return (lambda: losses[-1], run, losses.append)

    pending = [None] * LEVELS
    gradients = [None] * LEVELS

    def later_job(level, plane):
        places = [(chunk, side) for _, chunk, side in solved[level]]

        def run(given):
            parts = [(terms, chunk, side) for terms, (chunk, side) in zip(given, places)]
            return across_rows(
                couplings[level][0], plane, parts, given[0].shape[0], base=pending[plane]
            )

        return (
            lambda: [terms for terms, _, _ in solved[level]],
            run,
            lambda result: pending.__setitem__(plane, result),
        )

    solved = {}
    for name in list(held):
        if name != ("factor", 3):
            del held[name]
    loss_start = (lambda: samples, loss_job, losses.append)
    for tree_level in reversed(range(LEVELS)):
        group_bits = leaf_bits - tree_level
        adjoint = weights[None, :] * jax.nn.sigmoid(samples[tree_level] - tail_level)
        if tree_level < LEVELS - 1:
            if tree_level == 2:
                waits = work(
                    [
                        later_job(3, 1), later_job(3, 0), load_job(("factor", 2), 0),
                    ]
                )
            elif tree_level == 1:
                waits = work(
                    [later_job(2, 0)], [load_job(("factor", 1), 0), sum_job(1)]
                )
            else:
                waits = work([sum_job(1)], [], [], [], [load_job(("factor", 0), 0)])
            adjoint = adjoint - group_sum(pending[tree_level], group_bits, leaf_index, waits)
            waits.drain()
        adjoint_round = adjoint.astype(jnp.bfloat16)
        chunks = chunks_of(factors[tree_level].shape[1])
        if tree_level == 3:
            waits = work([load_job(("coupling", 3), 2), loss_start])
        elif tree_level == 2:
            waits = work([load_job(("coupling", 2), 1), sum_job(2)])
        elif tree_level == 1:
            waits = work([load_job(("coupling", 1), 0), sum_job(1)])
        else:
            waits = work()

        def produce(chunk, side, after):
            vector = adjoint_round
            if after is not None:
                vector, _ = tied(vector, after)
            return apply_rows(*matrix_of("factor", tree_level, 0), vector, None, chunk, side, chunks)

        count = factors[tree_level].shape[1] // chunks // 2

        def consume(parts, state):
            if tree_level == 0:
                return ()
            base, exact = (None, None) if state is None else state
            return across_rows(
                *matrix_of("coupling", tree_level, tree_level - 1), parts, count,
                base=base, exact=exact, give_exact=True,
            )

        state, solved[tree_level] = rows_stage(produce, consume, chunks, waits)
        if tree_level == 0:
            gradients[0] = place_rows(*[terms for terms, _, _ in solved[0]])
            continue
        upward, gradients[tree_level] = state
        before = pending[tree_level - 1]
        pending[tree_level - 1] = upward if before is None else before + upward
    while steps:
        last_sum = sum_job(1)
        last_sum[2](last_sum[1](last_sum[0]()))
    tail_loss = jnp.sum(losses[-1] + tickets[-1]) / jnp.float32(
        (2**LEVELS - 1) * full_width * (scenario_count + tail_index.shape[0])
    )
    return (gradients[0], gradients[1], gradients[2], gradients[3], tail_loss)


def solution(mesh):
    in_specs = (
        P("leaf", "rows"),
        P("leaf", "rows"),
        P("leaf", "rows"),
        P("leaf", "rows"),
        P("leaf", None, "rows"),
        P("leaf", None, "rows"),
        P("leaf", None, "rows"),
        P("leaf", None),
        P("leaf", None),
        P("leaf", None),
        P("leaf", None),
        P(),
    )
    out_specs = (P("leaf", None), P("leaf", None), P("leaf", None), P("leaf", None), P())
    return jax.shard_map(
        on_device, mesh=mesh, in_specs=in_specs, out_specs=out_specs, check_vma=False
    )
```

profile of v0, /device:TPU:0, one launch (start us, length us, event | category | flops | bytes accessed | tf_op | source)
XLA Modules:
  0.0 290.0 jit_solution(2402436989515713929)
XLA Ops:
  0.6 2.4 shard_map.155
  3.1 3.0 %collective-permute-start = (f32[512,128]{1,0:T(8,128)S(1)}, f32[512,128]{1,0:T(8,128)S(1)}, u32[]{:S(2)}, u32[]{:S(2)}) collective-permute-start(f32[512,128]{1,0:T(8,128)S(1)} %constant_dynamic-slice_fusion.3), channel_id=1, source_target_pairs={{0,4},{4,0},{8,12},{12,8},{16,20},{20,16},{24,28},{28,24},{1,5},{5... | collective-permute-start | bytes 786440 | tf_op jit(solution)/shard_map/ppermute | solution.py:17
  6.1 6.3 %collective-permute-done = f32[512,128]{1,0:T(8,128)S(1)} collective-permute-done((f32[512,128]{1,0:T(8,128)S(1)}, f32[512,128]{1,0:T(8,128)S(1)}, u32[]{:S(2)}, u32[]{:S(2)}) %collective-permute-start) | collective-permute-done | bytes 262176 | tf_op jit(solution)/shard_map/ppermute | solution.py:17
  14.3 3.2 %collective-permute-done.1 = f32[256,128]{1,0:T(8,128)S(1)} collective-permute-done((f32[256,128]{1,0:T(8,128)S(1)}, f32[256,128]{1,0:T(8,128)S(1)}, u32[]{:S(2)}, u32[]{:S(2)}) %collective-permute-start.1) | collective-permute-done | bytes 131104 | tf_op jit(solution)/shard_map/ppermute | solution.py:17
  17.5 2.9 collective-permute-start.2
  20.4 4.6 %collective-permute-done.2 = f32[256,128]{1,0:T(8,128)S(1)} collective-permute-done((f32[256,128]{1,0:T(8,128)S(1)}, f32[256,128]{1,0:T(8,128)S(1)}, u32[]{:S(2)}, u32[]{:S(2)}) %collective-permute-start.2) | collective-permute-done | bytes 131104 | tf_op jit(solution)/shard_map/ppermute | solution.py:17
  25.8 4.2 %collective-permute-done.3 = f32[256,128]{1,0:T(8,128)S(1)} collective-permute-done((f32[256,128]{1,0:T(8,128)S(1)}, f32[256,128]{1,0:T(8,128)S(1)}, u32[]{:S(2)}, u32[]{:S(2)}) %collective-permute-start.3) | collective-permute-done | bytes 131104 | tf_op jit(solution)/shard_map/ppermute | solution.py:17
  40.4 9.4 %copy.24 = bf16[2048,2,1024]{2,0,1:T(8,128)(2,1)} copy(bf16[2048,2,1024]{2,1,0:T(2,128)(2,1)} %param.17) | data formatting | bytes 16777216 | tf_op jit(solution)/shard_map/optimization_barrier | solution.py:307
  49.9 2.2 shard_map.160.refs_3_
  52.1 2.2 shard_map.161
  56.4 4.5 %shard_map.162.refs_0_ = f32[4096,128]{1,0:T(8,128)S(1)} custom-call(bf16[3,4096,1024]{2,1,0:T(8,128)(2,1)} %bitcast.25, bf16[1024,128]{1,0:T(8,128)(2,1)S(1)} %get-tuple-element.233.vector_ref), custom_call_target="tpu_custom_call" | custom-call | flops 128 | bytes 128 | tf_op jit(solution)/shard_map/pallas_call | solution.py:99
  65.5 3.0 %shard_map.164.refs_0_ = f32[2048,128]{1,0:T(8,128)S(1)} custom-call(bf16[2,2048,1024]{2,1,0:T(8,128)(2,1)} %bitcast.31, bf16[1024,128]{1,0:T(8,128)(2,1)S(1)} %get-tuple-element.233.vector_ref), custom_call_target="tpu_custom_call" | custom-call | flops 128 | bytes 128 | tf_op jit(solution)/shard_map/pallas_call | solution.py:99
  68.5 2.2 shard_map.163
  75.8 4.4 %shard_map.168.refs_0_ = f32[4096,128]{1,0:T(8,128)S(1)} custom-call(bf16[3,4096,1024]{2,1,0:T(8,128)(2,1)} %bitcast.26, bf16[1024,128]{1,0:T(8,128)(2,1)S(1)} %fusion.15.vector_ref, f32[4096,128]{1,0:T(8,128)S(1)} %shard_map.162.refs_0_), custom_call_target="tpu_custom_call" | custom-call | flops 128 | bytes 128 | tf_op jit(solution)/shard_map/pallas_call | solution.py:99
  80.2 2.2 shard_map.167
  82.5 6.8 %collective-permute-done.13 = f32[1024,128]{1,0:T(8,128)S(1)} collective-permute-done((f32[1024,128]{1,0:T(8,128)S(1)}, f32[1024,128]{1,0:T(8,128)S(1)}, u32[]{:S(2)}, u32[]{:S(2)}) %collective-permute-start.13) | collective-permute-done | bytes 524320 | tf_op jit(solution)/shard_map/ppermute | solution.py:17
  89.4 2.2 shard_map.169.refs_3_
  91.6 2.2 shard_map.170
  94.5 3.5 %shard_map.171 = (bf16[4096,1024]{1,0:T(8,128)(2,1)S(1)}, f32[8,128]{1,0:T(8,128)S(1)}) custom-call(bf16[3,4096,1024]{2,1,0:T(8,128)(2,1)} %bitcast.27, f32[8,128]{1,0:T(8,128)S(1)} %get-tuple-element.254.ticket_ref), custom_call_target="tpu_custom_call" | custom-call | flops 128 | bytes 128 | tf_op jit(solution)/shard_map/pallas_call | solution.py:267
  98.0 10.2 %collective-permute-done.15 = f32[1024,128]{1,0:T(8,128)S(1)} collective-permute-done((f32[1024,128]{1,0:T(8,128)S(1)}, f32[1024,128]{1,0:T(8,128)S(1)}, u32[]{:S(2)}, u32[]{:S(2)}) %collective-permute-start.15) | collective-permute-done | bytes 524320 | tf_op jit(solution)/shard_map/ppermute | solution.py:17
  115.7 3.5 %shard_map.176 = (bf16[4096,1024]{1,0:T(8,128)(2,1)S(1)}, f32[8,128]{1,0:T(8,128)S(1)}) custom-call(bf16[1,4096,1024]{2,1,0:T(8,128)(2,1)} %bitcast.37, f32[8,128]{1,0:T(8,128)S(1)} %get-tuple-element.268.ticket_ref), custom_call_target="tpu_custom_call" | custom-call | flops 128 | bytes 128 | tf_op jit(solution)/shard_map/pallas_call | solution.py:267
  119.3 8.3 %collective-permute-done.18 = f32[1024,128]{1,0:T(8,128)S(1)} collective-permute-done((f32[1024,128]{1,0:T(8,128)S(1)}, f32[1024,128]{1,0:T(8,128)S(1)}, u32[]{:S(2)}, u32[]{:S(2)}) %collective-permute-start.18) | collective-permute-done | bytes 524320 | tf_op jit(solution)/shard_map/ppermute | solution.py:17
  127.7 2.2 shard_map.177.refs_3_
  129.9 8.4 %collective-permute-done.19 = f32[1024,128]{1,0:T(8,128)S(1)} collective-permute-done((f32[1024,128]{1,0:T(8,128)S(1)}, f32[1024,128]{1,0:T(8,128)S(1)}, u32[]{:S(2)}, u32[]{:S(2)}) %collective-permute-start.19) | collective-permute-done | bytes 524320 | tf_op jit(solution)/shard_map/ppermute | solution.py:17
  139.0 2.2 shard_map.178.refs_4_
  141.2 3.3 %shard_map.179 = f32[1024,128]{1,0:T(8,128)S(1)} custom-call(bf16[4096,1024]{1,0:T(8,128)(2,1)S(1)} %get-tuple-element.269.refs_0_.matrix_ref, bf16[4096,128]{1,0:T(8,128)(2,1)} %refs_1_.15, f32[1024,128]{1,0:T(8,128)S(1)} %collective-permute-done.20.refs_2_, f32[1024,128]{1,0:T(8,128)S(1)} %collective-permute-done.21.refs_3_, ...), custom_call_target="tpu_custom_call" | custom-call | flops 128 | bytes 128 | tf_op jit(solution)/shard_map/pallas_call | solution.py:234
  148.9 3.4 %copy-done.1 = bf16[4096,1024]{1,0:T(8,128)(2,1)S(1)} copy-done((bf16[4096,1024]{1,0:T(8,128)(2,1)S(1)}, bf16[4096,1024]{1,0:T(8,128)(2,1)}, u32[]{:S(2)}) %copy-start.1) | copy-done | bytes 8388632
  156.7 3.5 %shard_map.184 = (bf16[4096,1024]{1,0:T(8,128)(2,1)S(1)}, f32[8,128]{1,0:T(8,128)S(1)}) custom-call(bf16[3,4096,1024]{2,1,0:T(8,128)(2,1)} %bitcast.28, f32[8,128]{1,0:T(8,128)S(1)} %get-tuple-element.290.ticket_ref), custom_call_target="tpu_custom_call" | custom-call | flops 128 | bytes 128 | tf_op jit(solution)/shard_map/pallas_call | solution.py:267
  160.8 2.3 collective-permute-done.24
  164.4 9.3 %collective-permute-done.25 = f32[1024,128]{1,0:T(8,128)S(1)} collective-permute-done((f32[1024,128]{1,0:T(8,128)S(1)}, f32[1024,128]{1,0:T(8,128)S(1)}, u32[]{:S(2)}, u32[]{:S(2)}) %collective-permute-start.25) | collective-permute-done | bytes 524320 | tf_op jit(solution)/shard_map/ppermute | solution.py:17
  176.6 2.5 shard_map.187
  179.7 2.2 shard_map.190
  181.9 5.6 %shard_map.188 = f32[1024,128]{1,0:T(8,128)S(1)} custom-call(bf16[3,4096,1024]{2,1,0:T(8,128)(2,1)} %bitcast.29, f32[1024,128]{1,0:T(8,128)S(1)} %add.241.refs_1_, f32[1024,128]{1,0:T(8,128)S(1)} %add.242.refs_1_.refs_2_, f32[1024,128]{1,0:T(8,128)S(1)} %collective-permute-done.26.refs_1_.refs_3_, f32[1024,128]{1,0:T(8,128)S(1)} %collective-permute-done.27.refs_2_.refs_4_), custom_call_target="tpu_custom_call" | custom-call | flops 128 | bytes 128 | tf_op jit(solution)/shard_map/pallas_call | solution.py:234
  187.5 5.6 %shard_map.189.refs_3_ = f32[1024,128]{1,0:T(8,128)S(1)} custom-call(bf16[3,4096,1024]{2,1,0:T(8,128)(2,1)} %bitcast.30, f32[1024,128]{1,0:T(8,128)S(1)} %add.241.refs_1_, f32[1024,128]{1,0:T(8,128)S(1)} %add.242.refs_1_.refs_2_, f32[1024,128]{1,0:T(8,128)S(1)} %collective-permute-done.26.refs_1_.refs_3_, f32[1024,128]{1,0:T(8,128)S(1)} %collective-permute-done.27.refs_2_.refs_4_), custom_call_target="tpu_custom_call" | custom-call | flops 128 | bytes 128 | tf_op jit(solution)/shard_map/pallas_call | solution.py:234
  198.0 2.2 collective-permute-done.31
  201.7 2.2 shard_map.193
  203.9 6.1 %collective-permute-done.30 = f32[1024,128]{1,0:T(8,128)S(1)} collective-permute-done((f32[1024,128]{1,0:T(8,128)S(1)}, f32[1024,128]{1,0:T(8,128)S(1)}, u32[]{:S(2)}, u32[]{:S(2)}) %collective-permute-start.30) | collective-permute-done | bytes 524320 | tf_op jit(solution)/shard_map/ppermute | solution.py:17
  216.6 3.4 %shard_map.196 = f32[1024,128]{1,0:T(8,128)S(1)} custom-call(bf16[2,2048,1024]{2,1,0:T(8,128)(2,1)} %bitcast.34, f32[1024,128]{1,0:T(8,128)S(1)} %add.248.refs_1_, f32[1024,128]{1,0:T(8,128)S(1)} %collective-permute-done.33.refs_1_.refs_2_, f32[1024,128]{1,0:T(8,128)S(1)} %shard_map.189.refs_3_), custom_call_target="tpu_custom_call" | custom-call | flops 128 | bytes 128 | tf_op jit(solution)/shard_map/pallas_call | solution.py:234
  225.4 2.6 collective-permute-start.38
  236.2 6.2 %collective-permute-done.40 = f32[512,128]{1,0:T(8,128)S(1)} collective-permute-done((f32[512,128]{1,0:T(8,128)S(1)}, f32[512,128]{1,0:T(8,128)S(1)}, u32[]{:S(2)}, u32[]{:S(2)}) %collective-permute-start.40) | collective-permute-done | bytes 262176 | tf_op jit(solution)/shard_map/ppermute | solution.py:17
  246.8 3.1 %collective-permute-done.44 = f32[8,128]{1,0:T(8,128)S(1)} collective-permute-done((f32[8,128]{1,0:T(8,128)S(1)}, f32[8,128]{1,0:T(8,128)S(1)}, u32[]{:S(2)}, u32[]{:S(2)}) %collective-permute-start.44) | collective-permute-done | bytes 4128 | tf_op jit(solution)/shard_map/ppermute | solution.py:17
  249.9 4.2 %collective-permute-done.43 = f32[512,128]{1,0:T(8,128)S(1)} collective-permute-done((f32[512,128]{1,0:T(8,128)S(1)}, f32[512,128]{1,0:T(8,128)S(1)}, u32[]{:S(2)}, u32[]{:S(2)}) %collective-permute-start.43) | collective-permute-done | bytes 262176 | tf_op jit(solution)/shard_map/ppermute | solution.py:17
  254.2 2.4 collective-permute-start.45
  256.6 3.1 %collective-permute-done.45 = f32[256,128]{1,0:T(8,128)S(1)} collective-permute-done((f32[256,128]{1,0:T(8,128)S(1)}, f32[256,128]{1,0:T(8,128)S(1)}, u32[]{:S(2)}, u32[]{:S(2)}) %collective-permute-start.45) | collective-permute-done | bytes 131104 | tf_op jit(solution)/shard_map/ppermute | solution.py:17
  261.9 5.9 %collective-permute-done.46 = f32[256,128]{1,0:T(8,128)S(1)} collective-permute-done((f32[256,128]{1,0:T(8,128)S(1)}, f32[256,128]{1,0:T(8,128)S(1)}, u32[]{:S(2)}, u32[]{:S(2)}) %collective-permute-start.46) | collective-permute-done | bytes 131104 | tf_op jit(solution)/shard_map/ppermute | solution.py:17
  267.8 5.0 %collective-permute-done.47 = f32[256,128]{1,0:T(8,128)S(1)} collective-permute-done((f32[256,128]{1,0:T(8,128)S(1)}, f32[256,128]{1,0:T(8,128)S(1)}, u32[]{:S(2)}, u32[]{:S(2)}) %collective-permute-start.47) | collective-permute-done | bytes 131104 | tf_op jit(solution)/shard_map/ppermute | solution.py:17
  274.7 4.5 %collective-permute-done.48 = f32[512,128]{1,0:T(8,128)S(1)} collective-permute-done((f32[512,128]{1,0:T(8,128)S(1)}, f32[512,128]{1,0:T(8,128)S(1)}, u32[]{:S(2)}, u32[]{:S(2)}) %collective-permute-start.48) | collective-permute-done | bytes 262176 | tf_op jit(solution)/shard_map/ppermute | solution.py:17
  281.7 5.0 %collective-permute-done.50 = f32[256,128]{1,0:T(8,128)S(1)} collective-permute-done((f32[256,128]{1,0:T(8,128)S(1)}, f32[256,128]{1,0:T(8,128)S(1)}, u32[]{:S(2)}, u32[]{:S(2)}) %collective-permute-start.50) | collective-permute-done | bytes 131104 | tf_op jit(solution)/shard_map/ppermute | solution.py:17
  (178 shorter events, 87.2 us)
Async XLA Ops:
  3.1 9.3 %collective-permute-start = (f32[512,128]{1,0:T(8,128)S(1)}, f32[512,128]{1,0:T(8,128)S(1)}, u32[]{:S(2)}, u32[]{:S(2)}) collective-permute-start(f32[512,128]{1,0:T(8,128)S(1)} %constant_dynamic-slice_fusion.3), channel_id=1, source_target_pairs={{0,4},{4,0},{8,12},{12,8},{16,20},{20,16},{24,28},{28,24},{1,5},{5... | collective-permute-start | bytes 786440 | tf_op jit(solution)/shard_map/ppermute | solution.py:17
  12.5 5.0 %collective-permute-start.1 = (f32[256,128]{1,0:T(8,128)S(1)}, f32[256,128]{1,0:T(8,128)S(1)}, u32[]{:S(2)}, u32[]{:S(2)}) collective-permute-start(f32[256,128]{1,0:T(8,128)S(1)} %constant_dynamic-slice_fusion.2), channel_id=1, source_target_pairs={{0,8},{4,12},{8,0},{12,4},{16,24},{20,28},{24,16},{28,20},{1,9},{5... | collective-permute-start | bytes 393224 | tf_op jit(solution)/shard_map/ppermute | solution.py:17
  17.5 7.4 %collective-permute-start.2 = (f32[256,128]{1,0:T(8,128)S(1)}, f32[256,128]{1,0:T(8,128)S(1)}, u32[]{:S(2)}, u32[]{:S(2)}) collective-permute-start(f32[256,128]{1,0:T(8,128)S(1)} %dynamic-slice_add_fusion.3), channel_id=1, source_target_pairs={{0,16},{4,20},{8,24},{12,28},{16,0},{20,4},{24,8},{28,12},{1,17},{... | collective-permute-start | bytes 393224 | tf_op jit(solution)/shard_map/ppermute | solution.py:17
  25.0 5.0 %collective-permute-start.3 = (f32[256,128]{1,0:T(8,128)S(1)}, f32[256,128]{1,0:T(8,128)S(1)}, u32[]{:S(2)}, u32[]{:S(2)}) collective-permute-start(f32[256,128]{1,0:T(8,128)S(1)} %add.212), channel_id=1, source_target_pairs={{0,8},{4,12},{8,0},{12,4},{16,24},{20,28},{24,16},{28,20},{1,9},{5... | collective-permute-start | bytes 393224 | tf_op jit(solution)/shard_map/ppermute | solution.py:17
  30.0 6.4 %collective-permute-start.4 = (f32[512,128]{1,0:T(8,128)S(1)}, f32[512,128]{1,0:T(8,128)S(1)}, u32[]{:S(2)}, u32[]{:S(2)}) collective-permute-start(f32[512,128]{1,0:T(8,128)S(1)} %maximum_select_fusion.2), channel_id=1, source_target_pairs={{0,4},{4,0},{8,12},{12,8},{16,20},{20,16},{24,28},{28,24},{1,5},{5... | collective-permute-start | bytes 786440 | tf_op jit(solution)/shard_map/ppermute | solution.py:17
  37.0 1.6 collective-permute-start.5
  38.6 11.1 %collective-permute-start.6 = (f32[512,128]{1,0:T(8,128)S(1)}, f32[512,128]{1,0:T(8,128)S(1)}, u32[]{:S(2)}, u32[]{:S(2)}) collective-permute-start(f32[512,128]{1,0:T(8,128)S(1)} %add.213), channel_id=1, source_target_pairs={{0,2},{1,3},{2,0},{3,1},{4,6},{5,7},{6,4},{7,5},{8,10},{9,11},{10,... | collective-permute-start | bytes 786440 | tf_op jit(solution)/shard_map/ppermute | solution.py:17
  49.8 2.2 collective-permute-start.7
  54.3 8.8 %collective-permute-start.8 = (f32[512,128]{1,0:T(8,128)S(1)}, f32[512,128]{1,0:T(8,128)S(1)}, u32[]{:S(2)}, u32[]{:S(2)}) collective-permute-start(f32[512,128]{1,0:T(8,128)S(1)} %get-tuple-element.223), channel_id=1, source_target_pairs={{0,4},{4,0},{8,12},{12,8},{16,20},{20,16},{24,28},{28,24},{1,5},{5... | collective-permute-start | bytes 786440 | tf_op jit(solution)/shard_map/ppermute | solution.py:17
  55.9 8.4 %collective-permute-start.9 = (f32[512,128]{1,0:T(8,128)S(1)}, f32[512,128]{1,0:T(8,128)S(1)}, u32[]{:S(2)}, u32[]{:S(2)}) collective-permute-start(f32[512,128]{1,0:T(8,128)S(1)} %get-tuple-element.224), channel_id=1, source_target_pairs={{0,8},{4,12},{8,0},{12,4},{16,24},{20,28},{24,16},{28,20},{1,9},{5... | collective-permute-start | bytes 786440 | tf_op jit(solution)/shard_map/ppermute | solution.py:17
  64.4 7.7 %collective-permute-start.10 = (f32[512,128]{1,0:T(8,128)S(1)}, f32[512,128]{1,0:T(8,128)S(1)}, u32[]{:S(2)}, u32[]{:S(2)}) collective-permute-start(f32[512,128]{1,0:T(8,128)S(1)} %add.215), channel_id=1, source_target_pairs={{0,8},{4,12},{8,0},{12,4},{16,24},{20,28},{24,16},{28,20},{1,9},{5... | collective-permute-start | bytes 786440 | tf_op jit(solution)/shard_map/ppermute | solution.py:17
  65.0 7.3 %collective-permute-start.11 = (f32[512,128]{1,0:T(8,128)S(1)}, f32[512,128]{1,0:T(8,128)S(1)}, u32[]{:S(2)}, u32[]{:S(2)}) collective-permute-start(f32[512,128]{1,0:T(8,128)S(1)} %add.216), channel_id=1, source_target_pairs={{0,4},{4,0},{8,12},{12,8},{16,20},{20,16},{24,28},{28,24},{1,5},{5... | collective-permute-start | bytes 786440 | tf_op jit(solution)/shard_map/ppermute | solution.py:17
  73.1 2.0 collective-permute-start.12
  75.2 14.0 %collective-permute-start.13 = (f32[1024,128]{1,0:T(8,128)S(1)}, f32[1024,128]{1,0:T(8,128)S(1)}, u32[]{:S(2)}, u32[]{:S(2)}) collective-permute-start(f32[1024,128]{1,0:T(8,128)S(1)} %add.219), channel_id=1, source_target_pairs={{0,2},{1,3},{2,0},{3,1},{4,6},{5,7},{6,4},{7,5},{8,10},{9,11},{10,... | collective-permute-start | bytes 1572872 | tf_op jit(solution)/shard_map/ppermute | solution.py:17
  89.3 2.3 collective-permute-start.14
  93.8 14.4 %collective-permute-start.15 = (f32[1024,128]{1,0:T(8,128)S(1)}, f32[1024,128]{1,0:T(8,128)S(1)}, u32[]{:S(2)}, u32[]{:S(2)}) collective-permute-start(f32[1024,128]{1,0:T(8,128)S(1)} %shard_map.170), channel_id=1, source_target_pairs={{0,4},{4,0},{8,12},{12,8},{16,20},{20,16},{24,28},{28,24},{1,5},{5... | collective-permute-start | bytes 1572872 | tf_op jit(solution)/shard_map/ppermute | solution.py:17
  109.9 2.0 collective-permute-start.16
  112.6 2.0 collective-permute-start.17
  112.8 14.8 %collective-permute-start.18 = (f32[1024,128]{1,0:T(8,128)S(1)}, f32[1024,128]{1,0:T(8,128)S(1)}, u32[]{:S(2)}, u32[]{:S(2)}) collective-permute-start(f32[1024,128]{1,0:T(8,128)S(1)} %add.222), channel_id=1, source_target_pairs={{0,2},{1,3},{2,0},{3,1},{4,6},{5,7},{6,4},{7,5},{8,10},{9,11},{10,... | collective-permute-start | bytes 1572872 | tf_op jit(solution)/shard_map/ppermute | solution.py:17
  114.7 23.6 %collective-permute-start.19 = (f32[1024,128]{1,0:T(8,128)S(1)}, f32[1024,128]{1,0:T(8,128)S(1)}, u32[]{:S(2)}, u32[]{:S(2)}) collective-permute-start(f32[1024,128]{1,0:T(8,128)S(1)} %add.223), channel_id=1, source_target_pairs={{0,2},{1,3},{2,0},{3,1},{4,6},{5,7},{6,4},{7,5},{8,10},{9,11},{10,... | collective-permute-start | bytes 1572872 | tf_op jit(solution)/shard_map/ppermute | solution.py:17
  138.3 2.9 collective-permute-start.20
  138.4 2.8 collective-permute-start.21
  145.4 2.0 collective-permute-start.22
  148.1 4.8 %collective-permute-start.23 = (f32[1024,128]{1,0:T(8,128)S(1)}, f32[1024,128]{1,0:T(8,128)}, u32[]{:S(2)}, u32[]{:S(2)}) collective-permute-start(f32[1024,128]{1,0:T(8,128)S(1)} %shard_map.182), channel_id=1, source_target_pairs={{0,1},{1,0},{2,3},{3,2},{4,5},{5,4},{6,7},{7,6},{8,9},{9,8},{10,11... | collective-permute-start | bytes 1572872 | tf_op jit(solution)/shard_map/ppermute | solution.py:17
  148.3 14.8 %collective-permute-start.24 = (f32[1024,128]{1,0:T(8,128)S(1)}, f32[1024,128]{1,0:T(8,128)S(1)}, u32[]{:S(2)}, u32[]{:S(2)}) collective-permute-start(f32[1024,128]{1,0:T(8,128)S(1)} %add.229), channel_id=1, source_target_pairs={{0,2},{1,3},{2,0},{3,1},{4,6},{5,7},{6,4},{7,5},{8,10},{9,11},{10,... | collective-permute-start | bytes 1572872 | tf_op jit(solution)/shard_map/ppermute | solution.py:17
  154.1 19.7 %collective-permute-start.25 = (f32[1024,128]{1,0:T(8,128)S(1)}, f32[1024,128]{1,0:T(8,128)S(1)}, u32[]{:S(2)}, u32[]{:S(2)}) collective-permute-start(f32[1024,128]{1,0:T(8,128)S(1)} %add.230), channel_id=1, source_target_pairs={{0,2},{1,3},{2,0},{3,1},{4,6},{5,7},{6,4},{7,5},{8,10},{9,11},{10,... | collective-permute-start | bytes 1572872 | tf_op jit(solution)/shard_map/ppermute | solution.py:17
  173.8 2.0 collective-permute-start.26
  173.9 2.6 collective-permute-start.27
  179.0 14.0 %collective-permute-start.28 = (f32[1024,128]{1,0:T(8,128)S(1)}, f32[1024,128]{1,0:T(8,128)S(1)}, u32[]{:S(2)}, u32[]{:S(2)}) collective-permute-start(f32[1024,128]{1,0:T(8,128)S(1)} %get-tuple-element.317), channel_id=1, source_target_pairs={{0,4},{4,0},{8,12},{12,8},{16,20},{20,16},{24,28},{28,24},{1,5},{5... | collective-permute-start | bytes 1572872 | tf_op jit(solution)/shard_map/ppermute | solution.py:17
  194.0 2.0 collective-permute-start.29
  196.0 14.0 %collective-permute-start.30 = (f32[1024,128]{1,0:T(8,128)S(1)}, f32[1024,128]{1,0:T(8,128)S(1)}, u32[]{:S(2)}, u32[]{:S(2)}) collective-permute-start(f32[1024,128]{1,0:T(8,128)S(1)} %add.245), channel_id=1, source_target_pairs={{0,2},{1,3},{2,0},{3,1},{4,6},{5,7},{6,4},{7,5},{8,10},{9,11},{10,... | collective-permute-start | bytes 1572872 | tf_op jit(solution)/shard_map/ppermute | solution.py:17
  196.6 3.6 %collective-permute-start.31 = (f32[8,128]{1,0:T(8,128)S(1)}, f32[8,128]{1,0:T(8,128)S(1)}, u32[]{:S(2)}, u32[]{:S(2)}) collective-permute-start(f32[8,128]{1,0:T(8,128)S(1)} %add_add_fusion), channel_id=1, source_target_pairs={{0,4},{4,0},{8,12},{12,8},{16,20},{20,16},{24,28},{28,24},{1,5},{5... | collective-permute-start | bytes 12296 | tf_op jit(solution)/shard_map/ppermute | solution.py:17
  200.2 3.7 %collective-permute-start.32 = (f32[8,128]{1,0:T(8,128)S(1)}, f32[8,128]{1,0:T(8,128)S(1)}, u32[]{:S(2)}, u32[]{:S(2)}) collective-permute-start(f32[8,128]{1,0:T(8,128)S(1)} %add.246), channel_id=1, source_target_pairs={{0,8},{4,12},{8,0},{12,4},{16,24},{20,28},{24,16},{28,20},{1,9},{5... | collective-permute-start | bytes 12296 | tf_op jit(solution)/shard_map/ppermute | solution.py:17
  210.1 2.0 collective-permute-start.33
  213.6 8.4 %collective-permute-start.34 = (f32[512,128]{1,0:T(8,128)S(1)}, f32[512,128]{1,0:T(8,128)S(1)}, u32[]{:S(2)}, u32[]{:S(2)}) collective-permute-start(f32[512,128]{1,0:T(8,128)S(1)} %get-tuple-element.350), channel_id=1, source_target_pairs={{0,4},{4,0},{8,12},{12,8},{16,20},{20,16},{24,28},{28,24},{1,5},{5... | collective-permute-start | bytes 786440 | tf_op jit(solution)/shard_map/ppermute | solution.py:17
  215.1 8.1 %collective-permute-start.35 = (f32[512,128]{1,0:T(8,128)S(1)}, f32[512,128]{1,0:T(8,128)S(1)}, u32[]{:S(2)}, u32[]{:S(2)}) collective-permute-start(f32[512,128]{1,0:T(8,128)S(1)} %get-tuple-element.351), channel_id=1, source_target_pairs={{0,8},{4,12},{8,0},{12,4},{16,24},{20,28},{24,16},{28,20},{1,9},{5... | collective-permute-start | bytes 786440 | tf_op jit(solution)/shard_map/ppermute | solution.py:17
  223.3 7.3 %collective-permute-start.36 = (f32[512,128]{1,0:T(8,128)S(1)}, f32[512,128]{1,0:T(8,128)S(1)}, u32[]{:S(2)}, u32[]{:S(2)}) collective-permute-start(f32[512,128]{1,0:T(8,128)S(1)} %add.250), channel_id=1, source_target_pairs={{0,8},{4,12},{8,0},{12,4},{16,24},{20,28},{24,16},{28,20},{1,9},{5... | collective-permute-start | bytes 786440 | tf_op jit(solution)/shard_map/ppermute | solution.py:17
  224.8 6.9 %collective-permute-start.37 = (f32[512,128]{1,0:T(8,128)S(1)}, f32[512,128]{1,0:T(8,128)S(1)}, u32[]{:S(2)}, u32[]{:S(2)}) collective-permute-start(f32[512,128]{1,0:T(8,128)S(1)} %add.251), channel_id=1, source_target_pairs={{0,4},{4,0},{8,12},{12,8},{16,20},{20,16},{24,28},{28,24},{1,5},{5... | collective-permute-start | bytes 786440 | tf_op jit(solution)/shard_map/ppermute | solution.py:17
  225.4 4.6 %collective-permute-start.38 = (f32[8,128]{1,0:T(8,128)S(1)}, f32[8,128]{1,0:T(8,128)S(1)}, u32[]{:S(2)}, u32[]{:S(2)}) collective-permute-start(f32[8,128]{1,0:T(8,128)S(1)} %add.247), channel_id=1, source_target_pairs={{0,16},{4,20},{8,24},{12,28},{16,0},{20,4},{24,8},{28,12},{1,17},{... | collective-permute-start | bytes 12296 | tf_op jit(solution)/shard_map/ppermute | solution.py:17
  232.4 1.6 collective-permute-start.39
  234.0 8.4 %collective-permute-start.40 = (f32[512,128]{1,0:T(8,128)S(1)}, f32[512,128]{1,0:T(8,128)S(1)}, u32[]{:S(2)}, u32[]{:S(2)}) collective-permute-start(f32[512,128]{1,0:T(8,128)S(1)} %add.256), channel_id=1, source_target_pairs={{0,2},{1,3},{2,0},{3,1},{4,6},{5,7},{6,4},{7,5},{8,10},{9,11},{10,... | collective-permute-start | bytes 786440 | tf_op jit(solution)/shard_map/ppermute | solution.py:17
  245.6 8.5 %collective-permute-start.43 = (f32[512,128]{1,0:T(8,128)S(1)}, f32[512,128]{1,0:T(8,128)S(1)}, u32[]{:S(2)}, u32[]{:S(2)}) collective-permute-start(f32[512,128]{1,0:T(8,128)S(1)} %constant_dynamic-slice_fusion.1), channel_id=1, source_target_pairs={{0,4},{4,0},{8,12},{12,8},{16,20},{20,16},{24,28},{28,24},{1,5},{5... | collective-permute-start | bytes 786440 | tf_op jit(solution)/shard_map/ppermute | solution.py:17
  246.3 3.6 %collective-permute-start.44 = (f32[8,128]{1,0:T(8,128)S(1)}, f32[8,128]{1,0:T(8,128)S(1)}, u32[]{:S(2)}, u32[]{:S(2)}) collective-permute-start(f32[8,128]{1,0:T(8,128)S(1)} %add.257), channel_id=1, source_target_pairs={{0,2},{1,3},{2,0},{3,1},{4,6},{5,7},{6,4},{7,5},{8,10},{9,11},{10,... | collective-permute-start | bytes 12296 | tf_op jit(solution)/shard_map/ppermute | solution.py:17
  254.2 5.5 %collective-permute-start.45 = (f32[256,128]{1,0:T(8,128)S(1)}, f32[256,128]{1,0:T(8,128)S(1)}, u32[]{:S(2)}, u32[]{:S(2)}) collective-permute-start(f32[256,128]{1,0:T(8,128)S(1)} %constant_dynamic-slice_fusion), channel_id=1, source_target_pairs={{0,8},{4,12},{8,0},{12,4},{16,24},{20,28},{24,16},{28,20},{1,9},{5... | collective-permute-start | bytes 393224 | tf_op jit(solution)/shard_map/ppermute | solution.py:17
  259.7 8.0 %collective-permute-start.46 = (f32[256,128]{1,0:T(8,128)S(1)}, f32[256,128]{1,0:T(8,128)S(1)}, u32[]{:S(2)}, u32[]{:S(2)}) collective-permute-start(f32[256,128]{1,0:T(8,128)S(1)} %dynamic-slice_add_fusion.2), channel_id=1, source_target_pairs={{0,16},{4,20},{8,24},{12,28},{16,0},{20,4},{24,8},{28,12},{1,17},{... | collective-permute-start | bytes 393224 | tf_op jit(solution)/shard_map/ppermute | solution.py:17
  267.7 5.0 %collective-permute-start.47 = (f32[256,128]{1,0:T(8,128)S(1)}, f32[256,128]{1,0:T(8,128)S(1)}, u32[]{:S(2)}, u32[]{:S(2)}) collective-permute-start(f32[256,128]{1,0:T(8,128)S(1)} %add.263), channel_id=1, source_target_pairs={{0,8},{4,12},{8,0},{12,4},{16,24},{20,28},{24,16},{28,20},{1,9},{5... | collective-permute-start | bytes 393224 | tf_op jit(solution)/shard_map/ppermute | solution.py:17
  272.8 6.4 %collective-permute-start.48 = (f32[512,128]{1,0:T(8,128)S(1)}, f32[512,128]{1,0:T(8,128)S(1)}, u32[]{:S(2)}, u32[]{:S(2)}) collective-permute-start(f32[512,128]{1,0:T(8,128)S(1)} %maximum_select_fusion.3), channel_id=1, source_target_pairs={{0,4},{4,0},{8,12},{12,8},{16,20},{20,16},{24,28},{28,24},{1,5},{5... | collective-permute-start | bytes 786440 | tf_op jit(solution)/shard_map/ppermute | solution.py:17
  281.1 5.6 %collective-permute-start.50 = (f32[256,128]{1,0:T(8,128)S(1)}, f32[256,128]{1,0:T(8,128)S(1)}, u32[]{:S(2)}, u32[]{:S(2)}) collective-permute-start(f32[256,128]{1,0:T(8,128)S(1)} %add.265), channel_id=1, source_target_pairs={{0,2},{1,3},{2,0},{3,1},{4,6},{5,7},{6,4},{7,5},{8,10},{9,11},{10,... | collective-permute-start | bytes 393224 | tf_op jit(solution)/shard_map/ppermute | solution.py:17
  (7 other events, 48.8 us)
where the time goes:
time: 291 us; the launch traced here: 290 us
  waiting for transfers between devices  130 us (45%)
  Pallas kernels  94.7 us (33%)
  starting transfers between devices  42.6 us (15%)
  local copies, waits for them, and re-layouts  12.9 us (4%)
  other arithmetic  6.41 us (2%)
  between operations  3.29 us (1%)
    ppermute x52, waiting for transfers between devices, swapped(): lax.ppermute(x, axis, [(i, i ^ 1 << apart) for i in range(lax.axis_size(a...  130 us
    pallas_call x18, Pallas kernels, across_rows(): pl.pallas_call(functools.partial(across_body, plane, count, sides, noise...  43.8 us
    ppermute x52, starting transfers between devices, swapped(): lax.ppermute(x, axis, [(i, i ^ 1 << apart) for i in range(lax.axis_size(a...  42.6 us
    pallas_call x12, Pallas kernels, load(): pl.pallas_call(functools.partial(load_body, plane), out_shape=(pltpu.VMEM...  27.4 us
    pallas_call x21, Pallas kernels, apply_rows(): pl.pallas_call(functools.partial(apply_body, plane, chunk, side, count, b...  22.8 us
    optimization_barrier x1, local copies, waits for them, and re-layouts, tied(): return lax.optimization_barrier((first, second))  9.35 us
  transfers between devices with their start and end apart: 52, of which 42 were waited for; matrix products, arithmetic and copies ran while one was open for 4% of the time, Pallas kernels for 25%

commit v1 on v0

--- a/solution.py
+++ b/solution.py
@@ -112,12 +112,14 @@
     )(*operands)
 
 
-def across_body(plane, count, sides, has_noise, has_terms, has_base, old_exact, new_exact, *refs):
+def across_body(plane, count, sides, noise_held, has_terms, has_base, has_extra, old_exact, new_exact, final, *refs):
     refs = list(refs)
+    has_noise = noise_held is not None
     matrix_ref = refs.pop(0)
     noise_ref = refs.pop(0) if has_noise else None
     terms_refs = [refs.pop(0) for _ in sides] if has_terms else None
     base_ref = refs.pop(0) if has_base else None
+    extra_ref = refs.pop(0) if has_extra else None
     if old_exact:
         refs.pop(0)
     out_ref = refs.pop(0)
@@ -125,7 +127,7 @@
     total_ref = refs.pop(0)
     streamed = plane is not None
     buffer_ref, sems = (refs.pop(0), refs.pop(0)) if streamed else (None, None)
-    right_ref, right_sems = refs[:2] if has_noise else (None, None)
+    right_ref, right_sems = refs[:2] if noise_held is False else (None, None)
     exact_sems = refs[-1] if new_exact else None
     block = block_rows(count)
     blocks = count // block
@@ -153,7 +155,7 @@
         )
 
     for part in range(len(sides)):
-        if has_noise:
+        if noise_held is False:
             noise_copy(part).start()
         for number in range(blocks if streamed else 0):
             matrix_copy(part, number).start()
@@ -161,11 +163,11 @@
         for part in range(len(sides)):
             exact_copy(part).start()
     if has_base:
-        total_ref[...] = base_ref[...].T
+        total_ref[...] = base_ref[...]
     else:
         total_ref[...] = jnp.zeros_like(total_ref)
     for part in range(len(sides)):
-        if has_noise:
+        if noise_held is False:
             noise_copy(part).wait()
 
         def step(number, carry):
@@ -173,30 +175,38 @@
                 matrix_copy(part, number).wait()
             inner = pl.ds(pl.multiple_of(number * block, block), block)
             held = pl.ds(pl.multiple_of(part * count + number * block, block), block)
+            place = pl.ds(pl.multiple_of(first(part) + number * block, block), block)
+            if noise_held:
+                noise = noise_ref[place, :]
+            elif has_noise:
+                noise = right_ref[held, :]
             if not has_noise:
                 right = terms_refs[part][inner, :].astype(jnp.bfloat16)
             elif not has_terms:
-                right = right_ref[held, :]
+                right = noise
             else:
-                right = right_ref[held, :].astype(jnp.float32) - terms_refs[part][inner, :]
-                right = right.astype(jnp.bfloat16)
+                right = (noise.astype(jnp.float32) - terms_refs[part][inner, :]).astype(jnp.bfloat16)
             if streamed:
                 matrix = buffer_ref[held, :]
             else:
-                matrix = matrix_ref[pl.ds(pl.multiple_of(first(part) + number * block, block), block), :]
+                matrix = matrix_ref[place, :]
             total_ref[...] += lax.dot_general(
                 right, matrix, (((0,), (0,)), ((), ())), preferred_element_type=jnp.float32
             )
             return carry
 
         lax.fori_loop(0, blocks, step, 0)
-    out_ref[...] = total_ref[...].T
+    total = total_ref[...].T if final else total_ref[...]
+    out_ref[...] = total + extra_ref[...] if has_extra else total
     if new_exact:
         for part in range(len(sides)):
             exact_copy(part).wait()
 
 
-def across_rows(matrix, plane, parts, count, noise=None, base=None, exact=None, give_exact=False):
+def across_rows(
+    matrix, plane, parts, count, noise=None, noise_held=None, base=None, extra=None, exact=None,
+    give_exact=False, final=True,
+):
     rows, width = matrix.shape[-2:]
     scenarios = (parts[0][0] if noise is None else noise).shape[1]
     sides = tuple((chunk, side) for _, chunk, side in parts)
@@ -205,27 +215,30 @@
     operands = [in_hbm(matrix) if streamed else in_vmem(matrix)]
     in_specs = [HBM if streamed else VMEM]
     if noise is not None:
-        operands.append(in_hbm(noise))
-        in_specs.append(HBM)
+        operands.append(in_vmem(noise) if noise_held else in_hbm(noise))
+        in_specs.append(VMEM if noise_held else HBM)
     if has_terms:
         operands += [in_vmem(terms) for terms, _, _ in parts]
         in_specs += [VMEM] * len(parts)
     if base is not None:
         operands.append(in_vmem(base))
         in_specs.append(VMEM)
+    if extra is not None:
+        operands.append(in_vmem(extra))
+        in_specs.append(VMEM)
     aliases = {}
     if exact is not None:
         operands.append(in_hbm(exact))
         in_specs.append(HBM)
         aliases = {len(operands) - 1: 1}
-    out_shape = [pltpu.VMEM((width, scenarios), jnp.float32)]
+    out_shape = [pltpu.VMEM((width, scenarios) if final else (scenarios, width), jnp.float32)]
     out_specs = [VMEM]
     held = len(parts) * count
     scratch = [pltpu.VMEM((scenarios, width), jnp.float32)]
     if streamed:
         scratch.append(pltpu.VMEM((held, width), jnp.bfloat16))
         scratch.append(pltpu.SemaphoreType.DMA((held // block_rows(count),)))
-    if noise is not None:
+    if noise_held is False:
         scratch += [pltpu.VMEM((held, scenarios), jnp.bfloat16), pltpu.SemaphoreType.DMA((len(parts),))]
     if give_exact:
         out_shape.append(pltpu.HBM((rows, scenarios), jnp.float32))
@@ -233,8 +246,8 @@
         scratch.append(pltpu.SemaphoreType.DMA((len(parts),)))
     results = pl.pallas_call(
         functools.partial(
-            across_body, plane, count, sides, noise is not None, has_terms, base is not None,
-            exact is not None, give_exact,
+            across_body, plane, count, sides, noise_held, has_terms, base is not None,
+            extra is not None, exact is not None, give_exact, final,
         ),
         out_shape=tuple(out_shape),
         in_specs=in_specs,
@@ -247,8 +260,14 @@
     return tuple(results) if give_exact else results[0]
 
 
-def load_body(plane, matrix_ref, ticket_ref, held_ref, out_ticket_ref, sems):
+def load_body(plane, has_noise, matrix_ref, ticket_ref, *refs):
+    refs = list(refs)
+    noise_ref = refs.pop(0) if has_noise else None
+    held_ref, out_ticket_ref = refs[:2]
+    sems = refs[-1]
     copies = []
+    if has_noise:
+        copies.append(pltpu.make_async_copy(noise_ref, refs[2], sems.at[sems.shape[0] - 1]))
     block = block_rows(held_ref.shape[0])
     for number in range(held_ref.shape[0] // block):
         rows = pl.ds(number * block, block)
@@ -262,20 +281,22 @@
         copy.wait()
 
 
-def load(matrix, plane, ticket):
+def load(matrix, plane, ticket, noise):
     _, rows, width = matrix.shape
+    operands = [in_hbm(matrix), ticket]
+    out_shape = [pltpu.VMEM((rows, width), matrix.dtype), pltpu.VMEM(ticket.shape, ticket.dtype)]
+    if noise is not None:
+        operands.append(in_hbm(noise))
+        out_shape.append(pltpu.VMEM(noise.shape, noise.dtype))
     return pl.pallas_call(
-        functools.partial(load_body, plane),
-        out_shape=(
-            pltpu.VMEM((rows, width), matrix.dtype),
-            pltpu.VMEM(ticket.shape, ticket.dtype),
-        ),
-        in_specs=[HBM, VMEM],
-        out_specs=(VMEM, VMEM),
-        scratch_shapes=[pltpu.SemaphoreType.DMA((rows // block_rows(rows),))],
+        functools.partial(load_body, plane, noise is not None),
+        out_shape=tuple(out_shape),
+        in_specs=[HBM, VMEM] + [HBM] * (len(operands) - 2),
+        out_specs=(VMEM,) * len(out_shape),
+        scratch_shapes=[pltpu.SemaphoreType.DMA((rows // block_rows(rows) + 1,))],
         compiler_params=kernel_params(),
         cost_estimate=cost(rows, width, ticket.shape[1]),
-    )(in_hbm(matrix), ticket)
+    )(*operands)
 
 
 def place_body(count, own_ref, other_ref, exact_ref, sems):
@@ -347,17 +368,15 @@
     return values[0], got[0]
 
 
-def halve(value, position, leaf_index, jobs):
+def halves_at(value, position, leaf_index):
     half_rows = value.shape[0] // 2
     upper = leaf_index >> position & 1
     kept = lax.dynamic_slice_in_dim(value, upper * half_rows, half_rows, 0)
     sent = lax.dynamic_slice_in_dim(value, (1 - upper) * half_rows, half_rows, 0)
-    _, got = exchange(sent, "leaf", position, jobs)
-    return kept + got
-
-
-def double(value, position, leaf_index, jobs):
-    value, partner = exchange(value, "leaf", position, jobs)
+    return kept, sent
+
+
+def joined_at(value, partner, position, leaf_index):
     upper = leaf_index >> position & 1
     return jnp.where(
         upper == 1,
@@ -379,14 +398,27 @@
             parts, got = exchanges(parts, [("leaf", position) for position in positions], waits.take())
             parts = [part + more for part, more in zip(parts, got)]
         return jnp.concatenate(parts, axis=0)
-    for position in range(2):
-        value = halve(value, position, leaf_index, waits.take())
+    middle = value.shape[0] // 2
+    parts = [value[:middle], value[middle:]]
+    for positions in ((0, 1), (1, 0)):
+        pairs = [halves_at(part, position, leaf_index) for part, position in zip(parts, positions)]
+        _, got = exchanges(
+            [sent for _, sent in pairs], [("leaf", position) for position in positions], waits.take()
+        )
+        parts = [kept + more for (kept, _), more in zip(pairs, got)]
+    value = jnp.concatenate(parts, axis=0)
     for position in range(2, group_bits):
         value, got = exchange(value, "leaf", position, waits.take())
         value = value + got
-    for position in reversed(range(2)):
-        value = double(value, position, leaf_index, waits.take())
-    return value
+    middle = value.shape[0] // 2
+    parts = [value[:middle], value[middle:]]
+    for positions in ((1, 0), (0, 1)):
+        parts, got = exchanges(parts, [("leaf", position) for position in positions], waits.take())
+        parts = [
+            joined_at(part, more, position, leaf_index)
+            for part, more, position in zip(parts, got, positions)
+        ]
+    return jnp.concatenate(parts, axis=0)
 
 
 def chunks_of(rows):
@@ -417,15 +449,15 @@
             own = own + swapped(own, "rows", position)
         owns[chunk] = own
         if chunk + 1 < chunks:
-            state = consume([(own, chunk, 0)], state)
+            state = consume([(own, chunk, 0)], state, False)
     states = [state]
     job = (
         lambda: (owns[-1], state),
-        lambda given: consume([(given[0], chunks - 1, 0)], given[1]),
+        lambda given: consume([(given[0], chunks - 1, 0)], given[1], False),
         lambda result: states.append(result),
     )
     owns, others = exchanges(owns, [("rows", 0)] * chunks, [job])
-    state = consume([(other, chunk, 1) for chunk, other in enumerate(others)], states[-1])
+    state = consume([(other, chunk, 1) for chunk, other in enumerate(others)], states[-1], True)
     parts = [(own, chunk, 0) for chunk, own in enumerate(owns)]
     parts += [(other, chunk, 1) for chunk, other in enumerate(others)]
     return state, parts
@@ -465,12 +497,15 @@
     held = {}
     tickets = [jnp.zeros((8, scenario_count), jnp.float32)]
 
-    def load_job(name, plane):
+    def load_job(name, plane, forward=False):
         kind, level = name
 
         def run(given):
             matrix = factors[level] if kind == "factor" else couplings[level][0]
-            held[name], out = load(matrix, plane, given)
+            noise = noises[level] if kind == "factor" and forward else None
+            held[name], out, *rest = load(matrix, plane, given, noise)
+            if rest:
+                held["noise", level] = rest[0]
             return out
 
         return (lambda: tickets[-1], run, tickets.append)
@@ -499,16 +534,16 @@
     for tree_level in range(LEVELS):
         group_bits = leaf_bits - tree_level
         if tree_level == 0:
-            part = across_rows(factors[0], 0, [(None, 0, None)], noise_zero.shape[0], noise=noise_zero)
+            part = across_rows(factors[0], 0, [(None, 0, None)], noise_zero.shape[0], noise=noise_zero, noise_held=False)
         else:
             plane = tree_level - 1
             last = samples[-1].astype(jnp.bfloat16)
             if tree_level == 1:
                 waits = work([turn_job()])
             elif tree_level == 2:
-                waits = work([early_job(3, 1, last), load_job(("factor", 2), 0)])
+                waits = work([early_job(3, 1, last), load_job(("factor", 2), 0, True)])
             else:
-                waits = work([load_job(("factor", 3), 0)])
+                waits = work([load_job(("factor", 3), 0, True)])
             chunks = chunks_of(factors[tree_level].shape[1])
 
             def produce(chunk, side, after):
@@ -522,14 +557,17 @@
             factor = factors[tree_level]
             count = factor.shape[1] // chunks // 2
 
-            def consume(parts, state):
+            def consume(parts, state, final):
+                noise_held = ("noise", tree_level) in held
+                noise = held["noise", tree_level] if noise_held else noises[tree_level]
                 return across_rows(
-                    *matrix_of("factor", tree_level, 0), parts, count, noise=noises[tree_level], base=state
+                    *matrix_of("factor", tree_level, 0), parts, count, noise=noise, noise_held=noise_held,
+                    base=state, final=final,
                 )
 
             part, _ = rows_stage(produce, consume, chunks, waits)
         if tree_level == 0:
-            waits = work([], [], [], [], [load_job(("coupling", 1), 0), load_job(("factor", 1), 0)])
+            waits = work([], [], [], [], [load_job(("coupling", 1), 0), load_job(("factor", 1), 0, True)])
         elif tree_level == 1:
             waits = work(
                 [early_job(3, 0, last)],
@@ -577,7 +615,7 @@
         def run(given):
             parts = [(terms, chunk, side) for terms, (chunk, side) in zip(given, places)]
             return across_rows(
-                couplings[level][0], plane, parts, given[0].shape[0], base=pending[plane]
+                couplings[level][0], plane, parts, given[0].shape[0], extra=pending[plane]
             )
 
         return (
@@ -624,26 +662,28 @@
             vector = adjoint_round
             if after is not None:
                 vector, _ = tied(vector, after)
-            return apply_rows(*matrix_of("factor", tree_level, 0), vector, None, chunk, side, chunks)
+            place = matrix_of("factor", tree_level, 0)
+            if chunk > 0 and side == 0:
+                place = (factors[tree_level], 0)
+            return apply_rows(*place, vector, None, chunk, side, chunks)
 
         count = factors[tree_level].shape[1] // chunks // 2
 
-        def consume(parts, state):
+        def consume(parts, state, final):
             if tree_level == 0:
                 return ()
             base, exact = (None, None) if state is None else state
             return across_rows(
                 *matrix_of("coupling", tree_level, tree_level - 1), parts, count,
-                base=base, exact=exact, give_exact=True,
+                base=base, extra=pending[tree_level - 1] if final else None, exact=exact, give_exact=True,
+                final=final,
             )
 
         state, solved[tree_level] = rows_stage(produce, consume, chunks, waits)
         if tree_level == 0:
             gradients[0] = place_rows(*[terms for terms, _, _ in solved[0]])
             continue
-        upward, gradients[tree_level] = state
-        before = pending[tree_level - 1]
-        pending[tree_level - 1] = upward if before is None else before + upward
+        pending[tree_level - 1], gradients[tree_level] = state
     while steps:
         last_sum = sum_job(1)
         last_sum[2](last_sum[1](last_sum[0]()))

time: 291 us -> 280 us (0.962)
  Pallas kernels: 94.7 us -> 88.7 us
  starting transfers between devices: 42.6 us -> 47.5 us
  waiting for transfers between devices: 130 us -> 126 us
  local copies, waits for them, and re-layouts: 12.9 us -> 9.66 us
    pallas_call x30, Pallas kernels: 71.2 us -> 63.7 us  [the longest x18 35.7 us: across_rows(): pl.pallas_call(functools.partial(across_body, plane, count, sides, noise_...]
    ppermute x52 -> x60, starting transfers between devices: 42.6 us -> 47.5 us  [swapped(): lax.ppermute(x, axis, [(i, i ^ 1 << apart) for i in range(lax.axis_size(a...]
    ppermute x52 -> x60, waiting for transfers between devices: 130 us -> 126 us  [swapped(): lax.ppermute(x, axis, [(i, i ^ 1 << apart) for i in range(lax.axis_size(a...]
    unnamed x6 -> x2, local copies, waits for them, and re-layouts: 3.39 us -> 0.01 us
  transfers between devices with their start and end apart: 52 -> 60, of which waited for: 42 -> 52; matrix products, arithmetic and copies ran while one was open for 4% -> 4% of each run, Pallas kernels for 25% -> 25%
where the time goes in v1:
time: 280 us
  waiting for transfers between devices  126 us (45%)
  Pallas kernels  88.7 us (32%)
  starting transfers between devices  47.5 us (17%)
  local copies, waits for them, and re-layouts  9.66 us (3%)
  other arithmetic  4.67 us (2%)
  between operations  3.43 us (1%)
    ppermute x60, waiting for transfers between devices, swapped(): lax.ppermute(x, axis, [(i, i ^ 1 << apart) for i in range(lax.axis_size(a...  126 us
    ppermute x60, starting transfers between devices, swapped(): lax.ppermute(x, axis, [(i, i ^ 1 << apart) for i in range(lax.axis_size(a...  47.5 us
    pallas_call x18, Pallas kernels, across_rows(): pl.pallas_call(functools.partial(across_body, plane, count, sides, noise_...  35.7 us
    pallas_call x12, Pallas kernels, load(): pl.pallas_call(functools.partial(load_body, plane, noise is not None), ou...  28 us
    pallas_call x21, Pallas kernels, apply_rows(): pl.pallas_call(functools.partial(apply_body, plane, chunk, side, count, b...  24.3 us
    optimization_barrier x1, local copies, waits for them, and re-layouts, tied(): return lax.optimization_barrier((first, second))  9.36 us
  transfers between devices with their start and end apart: 60, of which 52 were waited for; matrix products, arithmetic and copies ran while one was open for 4% of the time, Pallas kernels for 25%

profile of v1, /device:TPU:0, one launch (start us, length us, event | category | flops | bytes accessed | tf_op | source)
XLA Modules:
  0.0 279.5 jit_solution(2597582148241277419)
XLA Ops:
  0.6 2.4 shard_map.155
  3.1 3.0 %collective-permute-start = (f32[256,128]{1,0:T(8,128)S(1)}, f32[256,128]{1,0:T(8,128)S(1)}, u32[]{:S(2)}, u32[]{:S(2)}) collective-permute-start(f32[256,128]{1,0:T(8,128)S(1)} %constant_dynamic-slice_fusion.7), channel_id=1, source_target_pairs={{0,4},{4,0},{8,12},{12,8},{16,20},{20,16},{24,28},{28,24},{1,5},{5... | collective-permute-start | bytes 393224 | tf_op jit(solution)/shard_map/ppermute | solution.py:17
  6.2 1.6 collective-permute-start.1
  7.7 1.9 collective-permute-done
  11.2 1.6 collective-permute-start.2
  13.4 2.2 collective-permute-done.2
  15.5 1.6 collective-permute-done.3
  17.2 2.7 collective-permute-start.4
  19.8 4.7 %collective-permute-done.4 = f32[256,128]{1,0:T(8,128)S(1)} collective-permute-done((f32[256,128]{1,0:T(8,128)S(1)}, f32[256,128]{1,0:T(8,128)S(1)}, u32[]{:S(2)}, u32[]{:S(2)}) %collective-permute-start.4) | collective-permute-done | bytes 131104 | tf_op jit(solution)/shard_map/ppermute | solution.py:17
  25.0 4.5 %collective-permute-done.5 = f32[128,128]{1,0:T(8,128)S(1)} collective-permute-done((f32[128,128]{1,0:T(8,128)S(1)}, f32[128,128]{1,0:T(8,128)S(1)}, u32[]{:S(2)}, u32[]{:S(2)}) %collective-permute-start.5) | collective-permute-done | bytes 65568 | tf_op jit(solution)/shard_map/ppermute | solution.py:17
  31.3 2.2 shard_map.156
  33.5 1.6 shard_map.157
  37.4 1.7 collective-permute-start.10
  39.1 9.4 %copy.24 = bf16[2048,2,1024]{2,0,1:T(8,128)(2,1)} copy(bf16[2048,2,1024]{2,1,0:T(2,128)(2,1)} %param.17) | data formatting | bytes 16777216 | tf_op jit(solution)/shard_map/optimization_barrier | solution.py:328
  51.4 1.6 collective-permute-start.12
  54.1 4.5 %shard_map.162.refs_0_ = f32[4096,128]{1,0:T(8,128)S(1)} custom-call(bf16[3,4096,1024]{2,1,0:T(8,128)(2,1)} %bitcast.25, bf16[1024,128]{1,0:T(8,128)(2,1)S(1)} %fusion.15.vector_ref), custom_call_target="tpu_custom_call" | custom-call | flops 128 | bytes 128 | tf_op jit(solution)/shard_map/pallas_call | solution.py:99
  62.8 3.0 %shard_map.164.refs_0_ = f32[2048,128]{1,0:T(8,128)S(1)} custom-call(bf16[2,2048,1024]{2,1,0:T(8,128)(2,1)} %bitcast.31, bf16[1024,128]{1,0:T(8,128)(2,1)S(1)} %fusion.15.vector_ref), custom_call_target="tpu_custom_call" | custom-call | flops 128 | bytes 128 | tf_op jit(solution)/shard_map/pallas_call | solution.py:99
  65.8 2.2 shard_map.163
  72.7 4.5 %shard_map.168.refs_0_ = f32[4096,128]{1,0:T(8,128)S(1)} custom-call(bf16[3,4096,1024]{2,1,0:T(8,128)(2,1)} %bitcast.26, bf16[1024,128]{1,0:T(8,128)(2,1)S(1)} %fusion.14.vector_ref, f32[4096,128]{1,0:T(8,128)S(1)} %shard_map.162.refs_0_), custom_call_target="tpu_custom_call" | custom-call | flops 128 | bytes 128 | tf_op jit(solution)/shard_map/pallas_call | solution.py:99
  77.2 2.4 shard_map.167
  79.6 6.6 %collective-permute-done.17 = f32[1024,128]{1,0:T(8,128)S(1)} collective-permute-done((f32[1024,128]{1,0:T(8,128)S(1)}, f32[1024,128]{1,0:T(8,128)S(1)}, u32[]{:S(2)}, u32[]{:S(2)}) %collective-permute-start.17) | collective-permute-done | bytes 524320 | tf_op jit(solution)/shard_map/ppermute | solution.py:17
  90.1 3.5 %shard_map.171 = (bf16[4096,1024]{1,0:T(8,128)(2,1)S(1)}, f32[8,128]{1,0:T(8,128)S(1)}) custom-call(bf16[3,4096,1024]{2,1,0:T(8,128)(2,1)} %bitcast.27, f32[8,128]{1,0:T(8,128)S(1)} %get-tuple-element.299.ticket_ref), custom_call_target="tpu_custom_call" | custom-call | flops 128 | bytes 128 | tf_op jit(solution)/shard_map/pallas_call | solution.py:291
  93.6 9.8 %collective-permute-done.19 = f32[1024,128]{1,0:T(8,128)S(1)} collective-permute-done((f32[1024,128]{1,0:T(8,128)S(1)}, f32[1024,128]{1,0:T(8,128)S(1)}, u32[]{:S(2)}, u32[]{:S(2)}) %collective-permute-start.19) | collective-permute-done | bytes 524320 | tf_op jit(solution)/shard_map/ppermute | solution.py:17
  110.2 3.8 %shard_map.176 = (bf16[4096,1024]{1,0:T(8,128)(2,1)S(1)}, f32[8,128]{1,0:T(8,128)S(1)}, bf16[4096,128]{1,0:T(8,128)(2,1)S(1)}) custom-call(bf16[1,4096,1024]{2,1,0:T(8,128)(2,1)} %bitcast.35, f32[8,128]{1,0:T(8,128)S(1)} %get-tuple-element.313.ticket_ref, bf16[4096,128]{1,0:T(8,128)(2,1)} %refs_0_.5), custom_call_target="tpu_custom_call" | custom-call | flops 128 | bytes 128 | tf_op jit(solution)/shard_map/pallas_call | solution.py:291
  114.0 8.0 %collective-permute-done.22 = f32[1024,128]{1,0:T(8,128)S(1)} collective-permute-done((f32[1024,128]{1,0:T(8,128)S(1)}, f32[1024,128]{1,0:T(8,128)S(1)}, u32[]{:S(2)}, u32[]{:S(2)}) %collective-permute-start.22) | collective-permute-done | bytes 524320 | tf_op jit(solution)/shard_map/ppermute | solution.py:17
  123.2 9.5 %collective-permute-done.23 = f32[1024,128]{1,0:T(8,128)S(1)} collective-permute-done((f32[1024,128]{1,0:T(8,128)S(1)}, f32[1024,128]{1,0:T(8,128)S(1)}, u32[]{:S(2)}, u32[]{:S(2)}) %collective-permute-start.23) | collective-permute-done | bytes 524320 | tf_op jit(solution)/shard_map/ppermute | solution.py:17
  135.5 2.3 shard_map.179
  142.4 2.3 shard_map.183
  147.5 3.5 %shard_map.184 = (bf16[4096,1024]{1,0:T(8,128)(2,1)S(1)}, f32[8,128]{1,0:T(8,128)S(1)}) custom-call(bf16[3,4096,1024]{2,1,0:T(8,128)(2,1)} %bitcast.28, f32[8,128]{1,0:T(8,128)S(1)} %get-tuple-element.336.ticket_ref), custom_call_target="tpu_custom_call" | custom-call | flops 128 | bytes 128 | tf_op jit(solution)/shard_map/pallas_call | solution.py:291
  151.5 5.1 %collective-permute-done.28 = f32[1024,128]{1,0:T(8,128)S(1)} collective-permute-done((f32[1024,128]{1,0:T(8,128)S(1)}, f32[1024,128]{1,0:T(8,128)S(1)}, u32[]{:S(2)}, u32[]{:S(2)}) %collective-permute-start.28) | collective-permute-done | bytes 524320 | tf_op jit(solution)/shard_map/ppermute | solution.py:17
  157.7 9.5 %collective-permute-done.29 = f32[1024,128]{1,0:T(8,128)S(1)} collective-permute-done((f32[1024,128]{1,0:T(8,128)S(1)}, f32[1024,128]{1,0:T(8,128)S(1)}, u32[]{:S(2)}, u32[]{:S(2)}) %collective-permute-start.29) | collective-permute-done | bytes 524320 | tf_op jit(solution)/shard_map/ppermute | solution.py:17
  170.0 2.3 shard_map.187
  173.0 2.2 shard_map.188
  175.2 5.6 %shard_map.189.refs_3_ = f32[1024,128]{1,0:T(8,128)S(1)} custom-call(bf16[3,4096,1024]{2,1,0:T(8,128)(2,1)} %bitcast.29, f32[1024,128]{1,0:T(8,128)S(1)} %add.269.refs_1_, f32[1024,128]{1,0:T(8,128)S(1)} %add.270.refs_1_.refs_2_, f32[1024,128]{1,0:T(8,128)S(1)} %collective-permute-done.30.refs_1_.refs_3_, f32[1024,128]{1,0:T(8,128)S(1)} %collective-permute-done.31.refs_2_.refs_4_), custom_call_target="tpu_custom_call" | custom-call | flops 128 | bytes 128 | tf_op jit(solution)/shard_map/pallas_call | solution.py:247
  180.8 5.6 %shard_map.190.refs_3_ = f32[1024,128]{1,0:T(8,128)S(1)} custom-call(bf16[3,4096,1024]{2,1,0:T(8,128)(2,1)} %bitcast.30, f32[1024,128]{1,0:T(8,128)S(1)} %add.269.refs_1_, f32[1024,128]{1,0:T(8,128)S(1)} %add.270.refs_1_.refs_2_, f32[1024,128]{1,0:T(8,128)S(1)} %collective-permute-done.30.refs_1_.refs_3_, f32[1024,128]{1,0:T(8,128)S(1)} %collective-permute-done.31.refs_2_.refs_4_), custom_call_target="tpu_custom_call" | custom-call | flops 128 | bytes 128 | tf_op jit(solution)/shard_map/pallas_call | solution.py:247
  191.3 2.2 collective-permute-done.35
  194.4 2.2 shard_map.193
  197.1 6.2 %collective-permute-done.34 = f32[1024,128]{1,0:T(8,128)S(1)} collective-permute-done((f32[1024,128]{1,0:T(8,128)S(1)}, f32[1024,128]{1,0:T(8,128)S(1)}, u32[]{:S(2)}, u32[]{:S(2)}) %collective-permute-start.34) | collective-permute-done | bytes 524320 | tf_op jit(solution)/shard_map/ppermute | solution.py:17
  209.1 3.4 %shard_map.196.refs_3_ = f32[1024,128]{1,0:T(8,128)S(1)} custom-call(bf16[2,2048,1024]{2,1,0:T(8,128)(2,1)} %bitcast.34, f32[1024,128]{1,0:T(8,128)S(1)} %add.276.refs_1_, f32[1024,128]{1,0:T(8,128)S(1)} %collective-permute-done.37.refs_1_.refs_2_, f32[1024,128]{1,0:T(8,128)S(1)} %shard_map.190.refs_3_), custom_call_target="tpu_custom_call" | custom-call | flops 128 | bytes 128 | tf_op jit(solution)/shard_map/pallas_call | solution.py:247
  212.5 2.6 collective-permute-done.38
  217.9 1.9 collective-permute-start.42
  227.1 1.6 shard_map.200
  228.7 6.2 %collective-permute-done.44 = f32[512,128]{1,0:T(8,128)S(1)} collective-permute-done((f32[512,128]{1,0:T(8,128)S(1)}, f32[512,128]{1,0:T(8,128)S(1)}, u32[]{:S(2)}, u32[]{:S(2)}) %collective-permute-start.44) | collective-permute-done | bytes 262176 | tf_op jit(solution)/shard_map/ppermute | solution.py:17
  240.5 3.1 %collective-permute-done.49 = f32[8,128]{1,0:T(8,128)S(1)} collective-permute-done((f32[8,128]{1,0:T(8,128)S(1)}, f32[8,128]{1,0:T(8,128)S(1)}, u32[]{:S(2)}, u32[]{:S(2)}) %collective-permute-start.49) | collective-permute-done | bytes 4128 | tf_op jit(solution)/shard_map/ppermute | solution.py:17
  249.7 1.7 collective-permute-start.52
  251.4 5.7 %collective-permute-done.52 = f32[256,128]{1,0:T(8,128)S(1)} collective-permute-done((f32[256,128]{1,0:T(8,128)S(1)}, f32[256,128]{1,0:T(8,128)S(1)}, u32[]{:S(2)}, u32[]{:S(2)}) %collective-permute-start.52) | collective-permute-done | bytes 131104 | tf_op jit(solution)/shard_map/ppermute | solution.py:17
  258.7 2.9 %collective-permute-done.53 = f32[128,128]{1,0:T(8,128)S(1)} collective-permute-done((f32[128,128]{1,0:T(8,128)S(1)}, f32[128,128]{1,0:T(8,128)S(1)}, u32[]{:S(2)}, u32[]{:S(2)}) %collective-permute-start.53) | collective-permute-done | bytes 65568 | tf_op jit(solution)/shard_map/ppermute | solution.py:17
  271.2 5.0 %collective-permute-done.58 = f32[256,128]{1,0:T(8,128)S(1)} collective-permute-done((f32[256,128]{1,0:T(8,128)S(1)}, f32[256,128]{1,0:T(8,128)S(1)}, u32[]{:S(2)}, u32[]{:S(2)}) %collective-permute-start.58) | collective-permute-done | bytes 131104 | tf_op jit(solution)/shard_map/ppermute | solution.py:17
  (209 shorter events, 92.7 us)
Async XLA Ops:
  3.1 6.5 %collective-permute-start = (f32[256,128]{1,0:T(8,128)S(1)}, f32[256,128]{1,0:T(8,128)S(1)}, u32[]{:S(2)}, u32[]{:S(2)}) collective-permute-start(f32[256,128]{1,0:T(8,128)S(1)} %constant_dynamic-slice_fusion.7), channel_id=1, source_target_pairs={{0,4},{4,0},{8,12},{12,8},{16,20},{20,16},{24,28},{28,24},{1,5},{5... | collective-permute-start | bytes 393224 | tf_op jit(solution)/shard_map/ppermute | solution.py:17
  6.2 5.0 %collective-permute-start.1 = (f32[256,128]{1,0:T(8,128)S(1)}, f32[256,128]{1,0:T(8,128)S(1)}, u32[]{:S(2)}, u32[]{:S(2)}) collective-permute-start(f32[256,128]{1,0:T(8,128)S(1)} %constant_dynamic-slice_fusion.6), channel_id=1, source_target_pairs={{0,8},{4,12},{8,0},{12,4},{16,24},{20,28},{24,16},{28,20},{1,9},{5... | collective-permute-start | bytes 393224 | tf_op jit(solution)/shard_map/ppermute | solution.py:17
  11.2 4.3 %collective-permute-start.2 = (f32[128,128]{1,0:T(8,128)S(1)}, f32[128,128]{1,0:T(8,128)S(1)}, u32[]{:S(2)}, u32[]{:S(2)}) collective-permute-start(f32[128,128]{1,0:T(8,128)S(1)} %constant_dynamic-slice_fusion.5), channel_id=1, source_target_pairs={{0,8},{4,12},{8,0},{12,4},{16,24},{20,28},{24,16},{28,20},{1,9},{5... | collective-permute-start | bytes 196616 | tf_op jit(solution)/shard_map/ppermute | solution.py:17
  12.9 4.3 %collective-permute-start.3 = (f32[128,128]{1,0:T(8,128)S(1)}, f32[128,128]{1,0:T(8,128)S(1)}, u32[]{:S(2)}, u32[]{:S(2)}) collective-permute-start(f32[128,128]{1,0:T(8,128)S(1)} %constant_dynamic-slice_fusion.4), channel_id=1, source_target_pairs={{0,4},{4,0},{8,12},{12,8},{16,20},{20,16},{24,28},{28,24},{1,5},{5... | collective-permute-start | bytes 196616 | tf_op jit(solution)/shard_map/ppermute | solution.py:17
  17.2 7.3 %collective-permute-start.4 = (f32[256,128]{1,0:T(8,128)S(1)}, f32[256,128]{1,0:T(8,128)S(1)}, u32[]{:S(2)}, u32[]{:S(2)}) collective-permute-start(f32[256,128]{1,0:T(8,128)S(1)} %pad_maximum_fusion.2), channel_id=1, source_target_pairs={{0,16},{4,20},{8,24},{12,28},{16,0},{20,4},{24,8},{28,12},{1,17},{... | collective-permute-start | bytes 393224 | tf_op jit(solution)/shard_map/ppermute | solution.py:17
  24.5 5.0 %collective-permute-start.5 = (f32[128,128]{1,0:T(8,128)S(1)}, f32[128,128]{1,0:T(8,128)S(1)}, u32[]{:S(2)}, u32[]{:S(2)}) collective-permute-start(f32[128,128]{1,0:T(8,128)S(1)} %get-tuple-element.242), channel_id=1, source_target_pairs={{0,8},{4,12},{8,0},{12,4},{16,24},{20,28},{24,16},{28,20},{1,9},{5... | collective-permute-start | bytes 196616 | tf_op jit(solution)/shard_map/ppermute | solution.py:17
  24.6 5.0 %collective-permute-start.6 = (f32[128,128]{1,0:T(8,128)S(1)}, f32[128,128]{1,0:T(8,128)S(1)}, u32[]{:S(2)}, u32[]{:S(2)}) collective-permute-start(f32[128,128]{1,0:T(8,128)S(1)} %get-tuple-element.243), channel_id=1, source_target_pairs={{0,4},{4,0},{8,12},{12,8},{16,20},{20,16},{24,28},{28,24},{1,5},{5... | collective-permute-start | bytes 196616 | tf_op jit(solution)/shard_map/ppermute | solution.py:17
  29.6 5.5 %collective-permute-start.7 = (f32[256,128]{1,0:T(8,128)S(1)}, f32[256,128]{1,0:T(8,128)S(1)}, u32[]{:S(2)}, u32[]{:S(2)}) collective-permute-start(f32[256,128]{1,0:T(8,128)S(1)} %maximum_select_fusion.4), channel_id=1, source_target_pairs={{0,4},{4,0},{8,12},{12,8},{16,20},{20,16},{24,28},{28,24},{1,5},{5... | collective-permute-start | bytes 393224 | tf_op jit(solution)/shard_map/ppermute | solution.py:17
  30.0 5.1 %collective-permute-start.8 = (f32[256,128]{1,0:T(8,128)S(1)}, f32[256,128]{1,0:T(8,128)S(1)}, u32[]{:S(2)}, u32[]{:S(2)}) collective-permute-start(f32[256,128]{1,0:T(8,128)S(1)} %maximum_select_fusion.5), channel_id=1, source_target_pairs={{0,8},{4,12},{8,0},{12,4},{16,24},{20,28},{24,16},{28,20},{1,9},{5... | collective-permute-start | bytes 393224 | tf_op jit(solution)/shard_map/ppermute | solution.py:17
  37.4 11.1 %collective-permute-start.10 = (f32[512,128]{1,0:T(8,128)S(1)}, f32[512,128]{1,0:T(8,128)S(1)}, u32[]{:S(2)}, u32[]{:S(2)}) collective-permute-start(f32[512,128]{1,0:T(8,128)S(1)} %add.241), channel_id=1, source_target_pairs={{0,2},{1,3},{2,0},{3,1},{4,6},{5,7},{6,4},{7,5},{8,10},{9,11},{10,... | collective-permute-start | bytes 786440 | tf_op jit(solution)/shard_map/ppermute | solution.py:17
  51.4 8.4 %collective-permute-start.12 = (f32[512,128]{1,0:T(8,128)S(1)}, f32[512,128]{1,0:T(8,128)S(1)}, u32[]{:S(2)}, u32[]{:S(2)}) collective-permute-start(f32[512,128]{1,0:T(8,128)S(1)} %get-tuple-element.267), channel_id=1, source_target_pairs={{0,4},{4,0},{8,12},{12,8},{16,20},{20,16},{24,28},{28,24},{1,5},{5... | collective-permute-start | bytes 786440 | tf_op jit(solution)/shard_map/ppermute | solution.py:17
  53.0 8.1 %collective-permute-start.13 = (f32[512,128]{1,0:T(8,128)S(1)}, f32[512,128]{1,0:T(8,128)S(1)}, u32[]{:S(2)}, u32[]{:S(2)}) collective-permute-start(f32[512,128]{1,0:T(8,128)S(1)} %get-tuple-element.268), channel_id=1, source_target_pairs={{0,8},{4,12},{8,0},{12,4},{16,24},{20,28},{24,16},{28,20},{1,9},{5... | collective-permute-start | bytes 786440 | tf_op jit(solution)/shard_map/ppermute | solution.py:17
  61.1 7.3 %collective-permute-start.14 = (f32[512,128]{1,0:T(8,128)S(1)}, f32[512,128]{1,0:T(8,128)S(1)}, u32[]{:S(2)}, u32[]{:S(2)}) collective-permute-start(f32[512,128]{1,0:T(8,128)S(1)} %add.243), channel_id=1, source_target_pairs={{0,8},{4,12},{8,0},{12,4},{16,24},{20,28},{24,16},{28,20},{1,9},{5... | collective-permute-start | bytes 786440 | tf_op jit(solution)/shard_map/ppermute | solution.py:17
  62.3 6.9 %collective-permute-start.15 = (f32[512,128]{1,0:T(8,128)S(1)}, f32[512,128]{1,0:T(8,128)S(1)}, u32[]{:S(2)}, u32[]{:S(2)}) collective-permute-start(f32[512,128]{1,0:T(8,128)S(1)} %add.244), channel_id=1, source_target_pairs={{0,4},{4,0},{8,12},{12,8},{16,20},{20,16},{24,28},{28,24},{1,5},{5... | collective-permute-start | bytes 786440 | tf_op jit(solution)/shard_map/ppermute | solution.py:17
  70.1 2.0 collective-permute-start.16
  72.1 14.0 %collective-permute-start.17 = (f32[1024,128]{1,0:T(8,128)S(1)}, f32[1024,128]{1,0:T(8,128)S(1)}, u32[]{:S(2)}, u32[]{:S(2)}) collective-permute-start(f32[1024,128]{1,0:T(8,128)S(1)} %add.247), channel_id=1, source_target_pairs={{0,2},{1,3},{2,0},{3,1},{4,6},{5,7},{6,4},{7,5},{8,10},{9,11},{10,... | collective-permute-start | bytes 1572872 | tf_op jit(solution)/shard_map/ppermute | solution.py:17
  89.5 14.0 %collective-permute-start.19 = (f32[1024,128]{1,0:T(8,128)S(1)}, f32[1024,128]{1,0:T(8,128)S(1)}, u32[]{:S(2)}, u32[]{:S(2)}) collective-permute-start(f32[1024,128]{1,0:T(8,128)S(1)} %shard_map.170), channel_id=1, source_target_pairs={{0,4},{4,0},{8,12},{12,8},{16,20},{20,16},{24,28},{28,24},{1,5},{5... | collective-permute-start | bytes 1572872 | tf_op jit(solution)/shard_map/ppermute | solution.py:17
  104.3 2.0 collective-permute-start.20
  107.1 2.0 collective-permute-start.21
  107.3 14.8 %collective-permute-start.22 = (f32[1024,128]{1,0:T(8,128)S(1)}, f32[1024,128]{1,0:T(8,128)S(1)}, u32[]{:S(2)}, u32[]{:S(2)}) collective-permute-start(f32[1024,128]{1,0:T(8,128)S(1)} %add.250), channel_id=1, source_target_pairs={{0,2},{1,3},{2,0},{3,1},{4,6},{5,7},{6,4},{7,5},{8,10},{9,11},{10,... | collective-permute-start | bytes 1572872 | tf_op jit(solution)/shard_map/ppermute | solution.py:17
  109.1 23.6 %collective-permute-start.23 = (f32[1024,128]{1,0:T(8,128)S(1)}, f32[1024,128]{1,0:T(8,128)S(1)}, u32[]{:S(2)}, u32[]{:S(2)}) collective-permute-start(f32[1024,128]{1,0:T(8,128)S(1)} %add.251), channel_id=1, source_target_pairs={{0,2},{1,3},{2,0},{3,1},{4,6},{5,7},{6,4},{7,5},{8,10},{9,11},{10,... | collective-permute-start | bytes 1572872 | tf_op jit(solution)/shard_map/ppermute | solution.py:17
  132.8 2.0 collective-permute-start.24
  132.8 2.6 collective-permute-start.25
  141.5 3.2 %collective-permute-start.27 = (f32[1024,128]{1,0:T(8,128)S(1)}, f32[1024,128]{1,0:T(8,128)}, u32[]{:S(2)}, u32[]{:S(2)}) collective-permute-start(f32[1024,128]{1,0:T(8,128)S(1)} %shard_map.182), channel_id=1, source_target_pairs={{0,1},{1,0},{2,3},{3,2},{4,5},{5,4},{6,7},{7,6},{8,9},{9,8},{10,11... | collective-permute-start | bytes 1572872 | tf_op jit(solution)/shard_map/ppermute | solution.py:17
  141.8 14.8 %collective-permute-start.28 = (f32[1024,128]{1,0:T(8,128)S(1)}, f32[1024,128]{1,0:T(8,128)S(1)}, u32[]{:S(2)}, u32[]{:S(2)}) collective-permute-start(f32[1024,128]{1,0:T(8,128)S(1)} %add.257), channel_id=1, source_target_pairs={{0,2},{1,3},{2,0},{3,1},{4,6},{5,7},{6,4},{7,5},{8,10},{9,11},{10,... | collective-permute-start | bytes 1572872 | tf_op jit(solution)/shard_map/ppermute | solution.py:17
  145.7 21.5 %collective-permute-start.29 = (f32[1024,128]{1,0:T(8,128)S(1)}, f32[1024,128]{1,0:T(8,128)S(1)}, u32[]{:S(2)}, u32[]{:S(2)}) collective-permute-start(f32[1024,128]{1,0:T(8,128)S(1)} %add.258), channel_id=1, source_target_pairs={{0,2},{1,3},{2,0},{3,1},{4,6},{5,7},{6,4},{7,5},{8,10},{9,11},{10,... | collective-permute-start | bytes 1572872 | tf_op jit(solution)/shard_map/ppermute | solution.py:17
  167.4 2.6 collective-permute-start.31
  172.3 14.0 %collective-permute-start.32 = (f32[1024,128]{1,0:T(8,128)S(1)}, f32[1024,128]{1,0:T(8,128)S(1)}, u32[]{:S(2)}, u32[]{:S(2)}) collective-permute-start(f32[1024,128]{1,0:T(8,128)S(1)} %get-tuple-element.365), channel_id=1, source_target_pairs={{0,4},{4,0},{8,12},{12,8},{16,20},{20,16},{24,28},{28,24},{1,5},{5... | collective-permute-start | bytes 1572872 | tf_op jit(solution)/shard_map/ppermute | solution.py:17
  189.3 14.0 %collective-permute-start.34 = (f32[1024,128]{1,0:T(8,128)S(1)}, f32[1024,128]{1,0:T(8,128)S(1)}, u32[]{:S(2)}, u32[]{:S(2)}) collective-permute-start(f32[1024,128]{1,0:T(8,128)S(1)} %add.273), channel_id=1, source_target_pairs={{0,2},{1,3},{2,0},{3,1},{4,6},{5,7},{6,4},{7,5},{8,10},{9,11},{10,... | collective-permute-start | bytes 1572872 | tf_op jit(solution)/shard_map/ppermute | solution.py:17
  189.9 3.6 %collective-permute-start.35 = (f32[8,128]{1,0:T(8,128)S(1)}, f32[8,128]{1,0:T(8,128)S(1)}, u32[]{:S(2)}, u32[]{:S(2)}) collective-permute-start(f32[8,128]{1,0:T(8,128)S(1)} %add_add_fusion), channel_id=1, source_target_pairs={{0,4},{4,0},{8,12},{12,8},{16,20},{20,16},{24,28},{28,24},{1,5},{5... | collective-permute-start | bytes 12296 | tf_op jit(solution)/shard_map/ppermute | solution.py:17
  193.5 3.6 %collective-permute-start.36 = (f32[8,128]{1,0:T(8,128)S(1)}, f32[8,128]{1,0:T(8,128)S(1)}, u32[]{:S(2)}, u32[]{:S(2)}) collective-permute-start(f32[8,128]{1,0:T(8,128)S(1)} %add.274), channel_id=1, source_target_pairs={{0,8},{4,12},{8,0},{12,4},{16,24},{20,28},{24,16},{28,20},{1,9},{5... | collective-permute-start | bytes 12296 | tf_op jit(solution)/shard_map/ppermute | solution.py:17
  206.7 8.4 %collective-permute-start.38 = (f32[512,128]{1,0:T(8,128)S(1)}, f32[512,128]{1,0:T(8,128)S(1)}, u32[]{:S(2)}, u32[]{:S(2)}) collective-permute-start(f32[512,128]{1,0:T(8,128)S(1)} %get-tuple-element.396), channel_id=1, source_target_pairs={{0,4},{4,0},{8,12},{12,8},{16,20},{20,16},{24,28},{28,24},{1,5},{5... | collective-permute-start | bytes 786440 | tf_op jit(solution)/shard_map/ppermute | solution.py:17
  208.2 8.1 %collective-permute-start.39 = (f32[512,128]{1,0:T(8,128)S(1)}, f32[512,128]{1,0:T(8,128)S(1)}, u32[]{:S(2)}, u32[]{:S(2)}) collective-permute-start(f32[512,128]{1,0:T(8,128)S(1)} %get-tuple-element.397), channel_id=1, source_target_pairs={{0,8},{4,12},{8,0},{12,4},{16,24},{20,28},{24,16},{28,20},{1,9},{5... | collective-permute-start | bytes 786440 | tf_op jit(solution)/shard_map/ppermute | solution.py:17
  216.3 7.3 %collective-permute-start.40 = (f32[512,128]{1,0:T(8,128)S(1)}, f32[512,128]{1,0:T(8,128)S(1)}, u32[]{:S(2)}, u32[]{:S(2)}) collective-permute-start(f32[512,128]{1,0:T(8,128)S(1)} %add.277), channel_id=1, source_target_pairs={{0,8},{4,12},{8,0},{12,4},{16,24},{20,28},{24,16},{28,20},{1,9},{5... | collective-permute-start | bytes 786440 | tf_op jit(solution)/shard_map/ppermute | solution.py:17
  217.3 6.9 %collective-permute-start.41 = (f32[512,128]{1,0:T(8,128)S(1)}, f32[512,128]{1,0:T(8,128)S(1)}, u32[]{:S(2)}, u32[]{:S(2)}) collective-permute-start(f32[512,128]{1,0:T(8,128)S(1)} %add.278), channel_id=1, source_target_pairs={{0,4},{4,0},{8,12},{12,8},{16,20},{20,16},{24,28},{28,24},{1,5},{5... | collective-permute-start | bytes 786440 | tf_op jit(solution)/shard_map/ppermute | solution.py:17
  217.9 4.6 %collective-permute-start.42 = (f32[8,128]{1,0:T(8,128)S(1)}, f32[8,128]{1,0:T(8,128)S(1)}, u32[]{:S(2)}, u32[]{:S(2)}) collective-permute-start(f32[8,128]{1,0:T(8,128)S(1)} %add.275), channel_id=1, source_target_pairs={{0,16},{4,20},{8,24},{12,28},{16,0},{20,4},{24,8},{28,12},{1,17},{... | collective-permute-start | bytes 12296 | tf_op jit(solution)/shard_map/ppermute | solution.py:17
  226.5 8.4 %collective-permute-start.44 = (f32[512,128]{1,0:T(8,128)S(1)}, f32[512,128]{1,0:T(8,128)S(1)}, u32[]{:S(2)}, u32[]{:S(2)}) collective-permute-start(f32[512,128]{1,0:T(8,128)S(1)} %add.283), channel_id=1, source_target_pairs={{0,2},{1,3},{2,0},{3,1},{4,6},{5,7},{6,4},{7,5},{8,10},{9,11},{10,... | collective-permute-start | bytes 786440 | tf_op jit(solution)/shard_map/ppermute | solution.py:17
  237.9 5.7 %collective-permute-start.47 = (f32[256,128]{1,0:T(8,128)S(1)}, f32[256,128]{1,0:T(8,128)S(1)}, u32[]{:S(2)}, u32[]{:S(2)}) collective-permute-start(f32[256,128]{1,0:T(8,128)S(1)} %constant_dynamic-slice_fusion.3), channel_id=1, source_target_pairs={{0,4},{4,0},{8,12},{12,8},{16,20},{20,16},{24,28},{28,24},{1,5},{5... | collective-permute-start | bytes 393224 | tf_op jit(solution)/shard_map/ppermute | solution.py:17
  238.6 5.3 %collective-permute-start.48 = (f32[256,128]{1,0:T(8,128)S(1)}, f32[256,128]{1,0:T(8,128)S(1)}, u32[]{:S(2)}, u32[]{:S(2)}) collective-permute-start(f32[256,128]{1,0:T(8,128)S(1)} %constant_dynamic-slice_fusion.2), channel_id=1, source_target_pairs={{0,8},{4,12},{8,0},{12,4},{16,24},{20,28},{24,16},{28,20},{1,9},{5... | collective-permute-start | bytes 393224 | tf_op jit(solution)/shard_map/ppermute | solution.py:17
  240.0 3.6 %collective-permute-start.49 = (f32[8,128]{1,0:T(8,128)S(1)}, f32[8,128]{1,0:T(8,128)S(1)}, u32[]{:S(2)}, u32[]{:S(2)}) collective-permute-start(f32[8,128]{1,0:T(8,128)S(1)} %add.284), channel_id=1, source_target_pairs={{0,2},{1,3},{2,0},{3,1},{4,6},{5,7},{6,4},{7,5},{8,10},{9,11},{10,... | collective-permute-start | bytes 12296 | tf_op jit(solution)/shard_map/ppermute | solution.py:17
  243.9 4.3 %collective-permute-start.50 = (f32[128,128]{1,0:T(8,128)S(1)}, f32[128,128]{1,0:T(8,128)S(1)}, u32[]{:S(2)}, u32[]{:S(2)}) collective-permute-start(f32[128,128]{1,0:T(8,128)S(1)} %constant_dynamic-slice_fusion.1), channel_id=1, source_target_pairs={{0,8},{4,12},{8,0},{12,4},{16,24},{20,28},{24,16},{28,20},{1,9},{5... | collective-permute-start | bytes 196616 | tf_op jit(solution)/shard_map/ppermute | solution.py:17
  245.4 4.3 %collective-permute-start.51 = (f32[128,128]{1,0:T(8,128)S(1)}, f32[128,128]{1,0:T(8,128)S(1)}, u32[]{:S(2)}, u32[]{:S(2)}) collective-permute-start(f32[128,128]{1,0:T(8,128)S(1)} %constant_dynamic-slice_fusion), channel_id=1, source_target_pairs={{0,4},{4,0},{8,12},{12,8},{16,20},{20,16},{24,28},{28,24},{1,5},{5... | collective-permute-start | bytes 196616 | tf_op jit(solution)/shard_map/ppermute | solution.py:17
  249.7 7.4 %collective-permute-start.52 = (f32[256,128]{1,0:T(8,128)S(1)}, f32[256,128]{1,0:T(8,128)S(1)}, u32[]{:S(2)}, u32[]{:S(2)}) collective-permute-start(f32[256,128]{1,0:T(8,128)S(1)} %pad_maximum_fusion.3), channel_id=1, source_target_pairs={{0,16},{4,20},{8,24},{12,28},{16,0},{20,4},{24,8},{28,12},{1,17},{... | collective-permute-start | bytes 393224 | tf_op jit(solution)/shard_map/ppermute | solution.py:17
  257.2 4.5 %collective-permute-start.53 = (f32[128,128]{1,0:T(8,128)S(1)}, f32[128,128]{1,0:T(8,128)S(1)}, u32[]{:S(2)}, u32[]{:S(2)}) collective-permute-start(f32[128,128]{1,0:T(8,128)S(1)} %get-tuple-element.443), channel_id=1, source_target_pairs={{0,8},{4,12},{8,0},{12,4},{16,24},{20,28},{24,16},{28,20},{1,9},{5... | collective-permute-start | bytes 196616 | tf_op jit(solution)/shard_map/ppermute | solution.py:17
  257.2 5.0 %collective-permute-start.54 = (f32[128,128]{1,0:T(8,128)S(1)}, f32[128,128]{1,0:T(8,128)S(1)}, u32[]{:S(2)}, u32[]{:S(2)}) collective-permute-start(f32[128,128]{1,0:T(8,128)S(1)} %get-tuple-element.444), channel_id=1, source_target_pairs={{0,4},{4,0},{8,12},{12,8},{16,20},{20,16},{24,28},{28,24},{1,5},{5... | collective-permute-start | bytes 196616 | tf_op jit(solution)/shard_map/ppermute | solution.py:17
  262.3 5.0 %collective-permute-start.55 = (f32[256,128]{1,0:T(8,128)S(1)}, f32[256,128]{1,0:T(8,128)S(1)}, u32[]{:S(2)}, u32[]{:S(2)}) collective-permute-start(f32[256,128]{1,0:T(8,128)S(1)} %maximum_select_fusion.6), channel_id=1, source_target_pairs={{0,4},{4,0},{8,12},{12,8},{16,20},{20,16},{24,28},{28,24},{1,5},{5... | collective-permute-start | bytes 393224 | tf_op jit(solution)/shard_map/ppermute | solution.py:17
  263.7 5.0 %collective-permute-start.56 = (f32[256,128]{1,0:T(8,128)S(1)}, f32[256,128]{1,0:T(8,128)S(1)}, u32[]{:S(2)}, u32[]{:S(2)}) collective-permute-start(f32[256,128]{1,0:T(8,128)S(1)} %maximum_select_fusion.7), channel_id=1, source_target_pairs={{0,8},{4,12},{8,0},{12,4},{16,24},{20,28},{24,16},{28,20},{1,9},{5... | collective-permute-start | bytes 393224 | tf_op jit(solution)/shard_map/ppermute | solution.py:17
  270.6 5.6 %collective-permute-start.58 = (f32[256,128]{1,0:T(8,128)S(1)}, f32[256,128]{1,0:T(8,128)S(1)}, u32[]{:S(2)}, u32[]{:S(2)}) collective-permute-start(f32[256,128]{1,0:T(8,128)S(1)} %add.293), channel_id=1, source_target_pairs={{0,2},{1,3},{2,0},{3,1},{4,6},{5,7},{6,4},{7,5},{8,10},{9,11},{10,... | collective-permute-start | bytes 393224 | tf_op jit(solution)/shard_map/ppermute | solution.py:17
  (13 other events, 31.9 us)

commit v2 on v1

--- a/solution.py
+++ b/solution.py
@@ -13,8 +13,12 @@
 tail_level = 0.5
 
 
+def moved(x, axis, flips):
+    return lax.ppermute(x, axis, [(i, i ^ flips) for i in range(lax.axis_size(axis))])
+
+
 def swapped(x, axis, apart):
-    return lax.ppermute(x, axis, [(i, i ^ 1 << apart) for i in range(lax.axis_size(axis))])
+    return moved(x, axis, 1 << apart)
 
 
 def bits_of(axis):
@@ -354,26 +358,18 @@
         self.queue = []
 
 
-def exchanges(values, axis_positions, jobs=()):
+def exchanges(values, axis_flips, jobs=()):
     inputs = [job[0]() for job in jobs]
     values, inputs = tied(list(values), inputs)
-    got = [swapped(value, axis, position) for value, (axis, position) in zip(values, axis_positions)]
+    got = [moved(value, axis, flips) for value, (axis, flips) in zip(values, axis_flips)]
     got, results = tied(got, run_jobs(jobs, inputs))
     keep_results(jobs, results)
     return values, got
 
 
 def exchange(value, axis, position, jobs=()):
-    values, got = exchanges([value], [(axis, position)], jobs)
+    values, got = exchanges([value], [(axis, 1 << position)], jobs)
     return values[0], got[0]
-
-
-def halves_at(value, position, leaf_index):
-    half_rows = value.shape[0] // 2
-    upper = leaf_index >> position & 1
-    kept = lax.dynamic_slice_in_dim(value, upper * half_rows, half_rows, 0)
-    sent = lax.dynamic_slice_in_dim(value, (1 - upper) * half_rows, half_rows, 0)
-    return kept, sent
 
 
 def joined_at(value, partner, position, leaf_index):
@@ -395,30 +391,24 @@
         middle = value.shape[0] // 2
         parts = [value[:middle], value[middle:]]
         for positions in ((0, 1), (1, 0)):
-            parts, got = exchanges(parts, [("leaf", position) for position in positions], waits.take())
+            parts, got = exchanges(parts, [("leaf", 1 << position) for position in positions], waits.take())
             parts = [part + more for part, more in zip(parts, got)]
         return jnp.concatenate(parts, axis=0)
-    middle = value.shape[0] // 2
-    parts = [value[:middle], value[middle:]]
-    for positions in ((0, 1), (1, 0)):
-        pairs = [halves_at(part, position, leaf_index) for part, position in zip(parts, positions)]
-        _, got = exchanges(
-            [sent for _, sent in pairs], [("leaf", position) for position in positions], waits.take()
-        )
-        parts = [kept + more for (kept, _), more in zip(pairs, got)]
-    value = jnp.concatenate(parts, axis=0)
+    quarter = value.shape[0] // 4
+    member = leaf_index & 3
+    pieces = [
+        lax.dynamic_slice_in_dim(value, (member ^ flips) * quarter, quarter, 0) for flips in range(4)
+    ]
+    routes = [("leaf", flips) for flips in (1, 2, 3)]
+    _, got = exchanges(pieces[1:], routes, waits.take())
+    value = (pieces[0] + got[0]) + (got[1] + got[2])
     for position in range(2, group_bits):
         value, got = exchange(value, "leaf", position, waits.take())
         value = value + got
-    middle = value.shape[0] // 2
-    parts = [value[:middle], value[middle:]]
-    for positions in ((1, 0), (0, 1)):
-        parts, got = exchanges(parts, [("leaf", position) for position in positions], waits.take())
-        parts = [
-            joined_at(part, more, position, leaf_index)
-            for part, more, position in zip(parts, got, positions)
-        ]
-    return jnp.concatenate(parts, axis=0)
+    values, got = exchanges([value] * 3, routes, waits.take())
+    near = joined_at(values[0], got[0], 0, leaf_index)
+    far = joined_at(got[1], got[2], 0, leaf_index)
+    return joined_at(near, far, 1, leaf_index)
 
 
 def chunks_of(rows):
@@ -456,7 +446,7 @@
         lambda given: consume([(given[0], chunks - 1, 0)], given[1], False),
         lambda result: states.append(result),
     )
-    owns, others = exchanges(owns, [("rows", 0)] * chunks, [job])
+    owns, others = exchanges(owns, [("rows", 1)] * chunks, [job])
     state = consume([(other, chunk, 1) for chunk, other in enumerate(others)], states[-1], True)
     parts = [(own, chunk, 0) for chunk, own in enumerate(owns)]
     parts += [(other, chunk, 1) for chunk, other in enumerate(others)]
@@ -567,7 +557,7 @@
 
             part, _ = rows_stage(produce, consume, chunks, waits)
         if tree_level == 0:
-            waits = work([], [], [], [], [load_job(("coupling", 1), 0), load_job(("factor", 1), 0, True)])
+            waits = work([], [], [load_job(("coupling", 1), 0), load_job(("factor", 1), 0, True)])
         elif tree_level == 1:
             waits = work(
                 [early_job(3, 0, last)],
@@ -644,7 +634,7 @@
                     [later_job(2, 0)], [load_job(("factor", 1), 0), sum_job(1)]
                 )
             else:
-                waits = work([sum_job(1)], [], [], [], [load_job(("factor", 0), 0)])
+                waits = work([sum_job(1)], [], [load_job(("factor", 0), 0)])
             adjoint = adjoint - group_sum(pending[tree_level], group_bits, leaf_index, waits)
             waits.drain()
         adjoint_round = adjoint.astype(jnp.bfloat16)

time: 280 us -> 272 us (0.971)
  waiting for transfers between devices: 126 us -> 120 us
    ppermute x60 -> x56, waiting for transfers between devices: 126 us -> 120 us  [moved(): lax.ppermute(x, axis, [(i, i ^ flips) for i in range(lax.axis_size(axis))])]
    ppermute x60 -> x56, starting transfers between devices: 47.5 us -> 45.8 us  [moved(): lax.ppermute(x, axis, [(i, i ^ flips) for i in range(lax.axis_size(axis))])]
  transfers between devices with their start and end apart: 60 -> 56, of which waited for: 52 -> 48; matrix products, arithmetic and copies ran while one was open for 4% -> 4% of each run, Pallas kernels for 25% -> 26%
where the time goes in v2:
time: 272 us
  waiting for transfers between devices  120 us (44%)
  Pallas kernels  88.7 us (33%)
  starting transfers between devices  45.8 us (17%)
  local copies, waits for them, and re-layouts  9.5 us (3%)
  other arithmetic  4.6 us (2%)
  between operations  3.25 us (1%)
    ppermute x56, waiting for transfers between devices, moved(): lax.ppermute(x, axis, [(i, i ^ flips) for i in range(lax.axis_size(axis))])  120 us
    ppermute x56, starting transfers between devices, moved(): lax.ppermute(x, axis, [(i, i ^ flips) for i in range(lax.axis_size(axis))])  45.8 us
    pallas_call x18, Pallas kernels, across_rows(): pl.pallas_call(functools.partial(across_body, plane, count, sides, noise_...  35.6 us
    pallas_call x12, Pallas kernels, load(): pl.pallas_call(functools.partial(load_body, plane, noise is not None), ou...  28 us
    pallas_call x21, Pallas kernels, apply_rows(): pl.pallas_call(functools.partial(apply_body, plane, chunk, side, count, b...  24.3 us
    optimization_barrier x1, local copies, waits for them, and re-layouts, tied(): return lax.optimization_barrier((first, second))  9.35 us
  transfers between devices with their start and end apart: 56, of which 48 were waited for; matrix products, arithmetic and copies ran while one was open for 4% of the time, Pallas kernels for 26%

profile of v2, /device:TPU:0, one launch (start us, length us, event | category | flops | bytes accessed | tf_op | source)
XLA Modules:
  0.0 271.8 jit_solution(14660971798296797974)
XLA Ops:
  0.7 2.4 shard_map.155
  3.1 3.0 %collective-permute-start = (f32[256,128]{1,0:T(8,128)S(1)}, f32[256,128]{1,0:T(8,128)S(1)}, u32[]{:S(2)}, u32[]{:S(2)}) collective-permute-start(f32[256,128]{1,0:T(8,128)S(1)} %get-tuple-element.226), channel_id=1, source_target_pairs={{0,4},{4,0},{8,12},{12,8},{16,20},{20,16},{24,28},{28,24},{1,5},{5... | collective-permute-start | bytes 393224 | tf_op jit(solution)/shard_map/ppermute | solution.py:17
  7.7 1.9 collective-permute-done
  9.6 2.9 %collective-permute-done.1 = f32[256,128]{1,0:T(8,128)S(1)} collective-permute-done((f32[256,128]{1,0:T(8,128)S(1)}, f32[256,128]{1,0:T(8,128)S(1)}, u32[]{:S(2)}, u32[]{:S(2)}) %collective-permute-start.1) | collective-permute-done | bytes 131104 | tf_op jit(solution)/shard_map/ppermute | solution.py:17
  13.7 2.8 %collective-permute-start.3 = (f32[256,128]{1,0:T(8,128)S(1)}, f32[256,128]{1,0:T(8,128)S(1)}, u32[]{:S(2)}, u32[]{:S(2)}) collective-permute-start(f32[256,128]{1,0:T(8,128)S(1)} %add_add_fusion.1), channel_id=1, source_target_pairs={{0,16},{4,20},{8,24},{12,28},{16,0},{20,4},{24,8},{28,12},{1,17},{... | collective-permute-start | bytes 393224 | tf_op jit(solution)/shard_map/ppermute | solution.py:17
  16.5 5.4 %collective-permute-done.3 = f32[256,128]{1,0:T(8,128)S(1)} collective-permute-done((f32[256,128]{1,0:T(8,128)S(1)}, f32[256,128]{1,0:T(8,128)S(1)}, u32[]{:S(2)}, u32[]{:S(2)}) %collective-permute-start.3) | collective-permute-done | bytes 131104 | tf_op jit(solution)/shard_map/ppermute | solution.py:17
  22.2 2.2 collective-permute-start.6
  25.5 2.2 shard_map.156
  27.7 1.6 shard_map.157
  34.4 9.3 %copy.24 = bf16[2048,2,1024]{2,0,1:T(8,128)(2,1)} copy(bf16[2048,2,1024]{2,1,0:T(2,128)(2,1)} %param.17) | data formatting | bytes 16777216 | tf_op jit(solution)/shard_map/optimization_barrier | solution.py:332
  46.7 2.0 collective-permute-start.10
  49.0 4.5 %shard_map.162.refs_0_ = f32[4096,128]{1,0:T(8,128)S(1)} custom-call(bf16[3,4096,1024]{2,1,0:T(8,128)(2,1)} %bitcast.25, bf16[1024,128]{1,0:T(8,128)(2,1)S(1)} %get-tuple-element.265.vector_ref), custom_call_target="tpu_custom_call" | custom-call | flops 128 | bytes 128 | tf_op jit(solution)/shard_map/pallas_call | solution.py:103
  53.4 1.9 collective-permute-done.10
  58.3 3.0 %shard_map.164.refs_0_ = f32[2048,128]{1,0:T(8,128)S(1)} custom-call(bf16[2,2048,1024]{2,1,0:T(8,128)(2,1)} %bitcast.31, bf16[1024,128]{1,0:T(8,128)(2,1)S(1)} %get-tuple-element.265.vector_ref), custom_call_target="tpu_custom_call" | custom-call | flops 128 | bytes 128 | tf_op jit(solution)/shard_map/pallas_call | solution.py:103
  61.3 2.2 shard_map.163
  67.6 4.5 %shard_map.168.refs_0_ = f32[4096,128]{1,0:T(8,128)S(1)} custom-call(bf16[3,4096,1024]{2,1,0:T(8,128)(2,1)} %bitcast.26, bf16[1024,128]{1,0:T(8,128)(2,1)S(1)} %fusion.15.vector_ref, f32[4096,128]{1,0:T(8,128)S(1)} %shard_map.162.refs_0_), custom_call_target="tpu_custom_call" | custom-call | flops 128 | bytes 128 | tf_op jit(solution)/shard_map/pallas_call | solution.py:103
  72.1 2.4 shard_map.167
  74.5 6.6 %collective-permute-done.15 = f32[1024,128]{1,0:T(8,128)S(1)} collective-permute-done((f32[1024,128]{1,0:T(8,128)S(1)}, f32[1024,128]{1,0:T(8,128)S(1)}, u32[]{:S(2)}, u32[]{:S(2)}) %collective-permute-start.15) | collective-permute-done | bytes 524320 | tf_op jit(solution)/shard_map/ppermute | solution.py:17
  85.5 3.5 %shard_map.171 = (bf16[4096,1024]{1,0:T(8,128)(2,1)S(1)}, f32[8,128]{1,0:T(8,128)S(1)}) custom-call(bf16[3,4096,1024]{2,1,0:T(8,128)(2,1)} %bitcast.27, f32[8,128]{1,0:T(8,128)S(1)} %get-tuple-element.287.ticket_ref), custom_call_target="tpu_custom_call" | custom-call | flops 128 | bytes 128 | tf_op jit(solution)/shard_map/pallas_call | solution.py:295
  89.0 9.4 %collective-permute-done.17 = f32[1024,128]{1,0:T(8,128)S(1)} collective-permute-done((f32[1024,128]{1,0:T(8,128)S(1)}, f32[1024,128]{1,0:T(8,128)S(1)}, u32[]{:S(2)}, u32[]{:S(2)}) %collective-permute-start.17) | collective-permute-done | bytes 524320 | tf_op jit(solution)/shard_map/ppermute | solution.py:17
  105.1 3.8 %shard_map.176 = (bf16[4096,1024]{1,0:T(8,128)(2,1)S(1)}, f32[8,128]{1,0:T(8,128)S(1)}, bf16[4096,128]{1,0:T(8,128)(2,1)S(1)}) custom-call(bf16[1,4096,1024]{2,1,0:T(8,128)(2,1)} %bitcast.35, f32[8,128]{1,0:T(8,128)S(1)} %get-tuple-element.301.ticket_ref, bf16[4096,128]{1,0:T(8,128)(2,1)} %refs_0_.5), custom_call_target="tpu_custom_call" | custom-call | flops 128 | bytes 128 | tf_op jit(solution)/shard_map/pallas_call | solution.py:295
  108.9 8.0 %collective-permute-done.20 = f32[1024,128]{1,0:T(8,128)S(1)} collective-permute-done((f32[1024,128]{1,0:T(8,128)S(1)}, f32[1024,128]{1,0:T(8,128)S(1)}, u32[]{:S(2)}, u32[]{:S(2)}) %collective-permute-start.20) | collective-permute-done | bytes 524320 | tf_op jit(solution)/shard_map/ppermute | solution.py:17
  118.2 9.5 %collective-permute-done.21 = f32[1024,128]{1,0:T(8,128)S(1)} collective-permute-done((f32[1024,128]{1,0:T(8,128)S(1)}, f32[1024,128]{1,0:T(8,128)S(1)}, u32[]{:S(2)}, u32[]{:S(2)}) %collective-permute-start.21) | collective-permute-done | bytes 524320 | tf_op jit(solution)/shard_map/ppermute | solution.py:17
  130.4 2.5 shard_map.179
  137.4 2.2 shard_map.183
  142.5 3.5 %shard_map.184 = (bf16[4096,1024]{1,0:T(8,128)(2,1)S(1)}, f32[8,128]{1,0:T(8,128)S(1)}) custom-call(bf16[3,4096,1024]{2,1,0:T(8,128)(2,1)} %bitcast.28, f32[8,128]{1,0:T(8,128)S(1)} %get-tuple-element.324.ticket_ref), custom_call_target="tpu_custom_call" | custom-call | flops 128 | bytes 128 | tf_op jit(solution)/shard_map/pallas_call | solution.py:295
  146.6 5.1 %collective-permute-done.26 = f32[1024,128]{1,0:T(8,128)S(1)} collective-permute-done((f32[1024,128]{1,0:T(8,128)S(1)}, f32[1024,128]{1,0:T(8,128)S(1)}, u32[]{:S(2)}, u32[]{:S(2)}) %collective-permute-start.26) | collective-permute-done | bytes 524320 | tf_op jit(solution)/shard_map/ppermute | solution.py:17
  152.8 9.5 %collective-permute-done.27 = f32[1024,128]{1,0:T(8,128)S(1)} collective-permute-done((f32[1024,128]{1,0:T(8,128)S(1)}, f32[1024,128]{1,0:T(8,128)S(1)}, u32[]{:S(2)}, u32[]{:S(2)}) %collective-permute-start.27) | collective-permute-done | bytes 524320 | tf_op jit(solution)/shard_map/ppermute | solution.py:17
  165.1 2.3 shard_map.187
  168.5 2.2 shard_map.188
  170.7 5.6 %shard_map.189.refs_3_ = f32[1024,128]{1,0:T(8,128)S(1)} custom-call(bf16[3,4096,1024]{2,1,0:T(8,128)(2,1)} %bitcast.29, f32[1024,128]{1,0:T(8,128)S(1)} %add.239.refs_1_, f32[1024,128]{1,0:T(8,128)S(1)} %add.240.refs_1_.refs_2_, f32[1024,128]{1,0:T(8,128)S(1)} %collective-permute-done.28.refs_1_.refs_3_, f32[1024,128]{1,0:T(8,128)S(1)} %collective-permute-done.29.refs_2_.refs_4_), custom_call_target="tpu_custom_call" | custom-call | flops 128 | bytes 128 | tf_op jit(solution)/shard_map/pallas_call | solution.py:251
  176.3 5.6 %shard_map.190.refs_3_ = f32[1024,128]{1,0:T(8,128)S(1)} custom-call(bf16[3,4096,1024]{2,1,0:T(8,128)(2,1)} %bitcast.30, f32[1024,128]{1,0:T(8,128)S(1)} %add.239.refs_1_, f32[1024,128]{1,0:T(8,128)S(1)} %add.240.refs_1_.refs_2_, f32[1024,128]{1,0:T(8,128)S(1)} %collective-permute-done.28.refs_1_.refs_3_, f32[1024,128]{1,0:T(8,128)S(1)} %collective-permute-done.29.refs_2_.refs_4_), custom_call_target="tpu_custom_call" | custom-call | flops 128 | bytes 128 | tf_op jit(solution)/shard_map/pallas_call | solution.py:251
  186.4 2.6 collective-permute-done.33
  190.3 2.2 shard_map.193
  192.6 6.2 %collective-permute-done.32 = f32[1024,128]{1,0:T(8,128)S(1)} collective-permute-done((f32[1024,128]{1,0:T(8,128)S(1)}, f32[1024,128]{1,0:T(8,128)S(1)}, u32[]{:S(2)}, u32[]{:S(2)}) %collective-permute-start.32) | collective-permute-done | bytes 524320 | tf_op jit(solution)/shard_map/ppermute | solution.py:17
  203.3 1.7 collective-permute-start.37
  204.9 3.4 %shard_map.196.refs_3_ = f32[1024,128]{1,0:T(8,128)S(1)} custom-call(bf16[2,2048,1024]{2,1,0:T(8,128)(2,1)} %bitcast.34, f32[1024,128]{1,0:T(8,128)S(1)} %add.246.refs_1_, f32[1024,128]{1,0:T(8,128)S(1)} %collective-permute-done.35.refs_1_.refs_2_, f32[1024,128]{1,0:T(8,128)S(1)} %shard_map.190.refs_3_), custom_call_target="tpu_custom_call" | custom-call | flops 128 | bytes 128 | tf_op jit(solution)/shard_map/pallas_call | solution.py:251
  208.3 2.3 collective-permute-done.36
  211.4 1.7 collective-permute-start.38
  213.7 2.1 collective-permute-start.40
  224.6 6.2 %collective-permute-done.42 = f32[512,128]{1,0:T(8,128)S(1)} collective-permute-done((f32[512,128]{1,0:T(8,128)S(1)}, f32[512,128]{1,0:T(8,128)S(1)}, u32[]{:S(2)}, u32[]{:S(2)}) %collective-permute-start.42) | collective-permute-done | bytes 262176 | tf_op jit(solution)/shard_map/ppermute | solution.py:17
  234.4 2.1 collective-permute-start.46
  237.8 3.1 %collective-permute-done.48 = f32[8,128]{1,0:T(8,128)S(1)} collective-permute-done((f32[8,128]{1,0:T(8,128)S(1)}, f32[8,128]{1,0:T(8,128)S(1)}, u32[]{:S(2)}, u32[]{:S(2)}) %collective-permute-start.48) | collective-permute-done | bytes 4128 | tf_op jit(solution)/shard_map/ppermute | solution.py:17
  240.9 2.4 collective-permute-done.47
  244.9 6.7 %collective-permute-done.49 = f32[256,128]{1,0:T(8,128)S(1)} collective-permute-done((f32[256,128]{1,0:T(8,128)S(1)}, f32[256,128]{1,0:T(8,128)S(1)}, u32[]{:S(2)}, u32[]{:S(2)}) %collective-permute-start.49) | collective-permute-done | bytes 131104 | tf_op jit(solution)/shard_map/ppermute | solution.py:17
  251.7 2.6 collective-permute-start.52
  257.7 2.0 collective-permute-done.52
  263.5 5.0 %collective-permute-done.54 = f32[256,128]{1,0:T(8,128)S(1)} collective-permute-done((f32[256,128]{1,0:T(8,128)S(1)}, f32[256,128]{1,0:T(8,128)S(1)}, u32[]{:S(2)}, u32[]{:S(2)}) %collective-permute-start.54) | collective-permute-done | bytes 131104 | tf_op jit(solution)/shard_map/ppermute | solution.py:17
  (178 shorter events, 82.9 us)
Async XLA Ops:
  3.1 6.5 %collective-permute-start = (f32[256,128]{1,0:T(8,128)S(1)}, f32[256,128]{1,0:T(8,128)S(1)}, u32[]{:S(2)}, u32[]{:S(2)}) collective-permute-start(f32[256,128]{1,0:T(8,128)S(1)} %get-tuple-element.226), channel_id=1, source_target_pairs={{0,4},{4,0},{8,12},{12,8},{16,20},{20,16},{24,28},{28,24},{1,5},{5... | collective-permute-start | bytes 393224 | tf_op jit(solution)/shard_map/ppermute | solution.py:17
  6.1 6.4 %collective-permute-start.1 = (f32[256,128]{1,0:T(8,128)S(1)}, f32[256,128]{1,0:T(8,128)S(1)}, u32[]{:S(2)}, u32[]{:S(2)}) collective-permute-start(f32[256,128]{1,0:T(8,128)S(1)} %get-tuple-element.227), channel_id=1, source_target_pairs={{0,8},{4,12},{8,0},{12,4},{16,24},{20,28},{24,16},{28,20},{1,9},{5... | collective-permute-start | bytes 393224 | tf_op jit(solution)/shard_map/ppermute | solution.py:17
  7.7 6.0 %collective-permute-start.2 = (f32[256,128]{1,0:T(8,128)S(1)}, f32[256,128]{1,0:T(8,128)S(1)}, u32[]{:S(2)}, u32[]{:S(2)}) collective-permute-start(f32[256,128]{1,0:T(8,128)S(1)} %get-tuple-element.228), channel_id=1, source_target_pairs={{0,12},{4,8},{8,4},{12,0},{16,28},{20,24},{24,20},{28,16},{1,13},{... | collective-permute-start | bytes 393224 | tf_op jit(solution)/shard_map/ppermute | solution.py:17
  13.7 8.2 %collective-permute-start.3 = (f32[256,128]{1,0:T(8,128)S(1)}, f32[256,128]{1,0:T(8,128)S(1)}, u32[]{:S(2)}, u32[]{:S(2)}) collective-permute-start(f32[256,128]{1,0:T(8,128)S(1)} %add_add_fusion.1), channel_id=1, source_target_pairs={{0,16},{4,20},{8,24},{12,28},{16,0},{20,4},{24,8},{28,12},{1,17},{... | collective-permute-start | bytes 393224 | tf_op jit(solution)/shard_map/ppermute | solution.py:17
  21.9 7.4 %collective-permute-start.5 = (f32[256,128]{1,0:T(8,128)S(1)}, f32[256,128]{1,0:T(8,128)S(1)}, u32[]{:S(2)}, u32[]{:S(2)}) collective-permute-start(f32[256,128]{1,0:T(8,128)S(1)} %add.211), channel_id=1, source_target_pairs={{0,8},{4,12},{8,0},{12,4},{16,24},{20,28},{24,16},{28,20},{1,9},{5... | collective-permute-start | bytes 393224 | tf_op jit(solution)/shard_map/ppermute | solution.py:17
  22.2 7.1 %collective-permute-start.6 = (f32[256,128]{1,0:T(8,128)S(1)}, f32[256,128]{1,0:T(8,128)S(1)}, u32[]{:S(2)}, u32[]{:S(2)}) collective-permute-start(f32[256,128]{1,0:T(8,128)S(1)} %add.211), channel_id=1, source_target_pairs={{0,12},{4,8},{8,4},{12,0},{16,28},{20,24},{24,20},{28,16},{1,13},{... | collective-permute-start | bytes 393224 | tf_op jit(solution)/shard_map/ppermute | solution.py:17
  24.5 6.2 %collective-permute-start.4 = (f32[256,128]{1,0:T(8,128)S(1)}, f32[256,128]{1,0:T(8,128)S(1)}, u32[]{:S(2)}, u32[]{:S(2)}) collective-permute-start(f32[256,128]{1,0:T(8,128)S(1)} %add.211), channel_id=1, source_target_pairs={{0,4},{4,0},{8,12},{12,8},{16,20},{20,16},{24,28},{28,24},{1,5},{5... | collective-permute-start | bytes 393224 | tf_op jit(solution)/shard_map/ppermute | solution.py:17
  32.9 10.9 %collective-permute-start.8 = (f32[512,128]{1,0:T(8,128)S(1)}, f32[512,128]{1,0:T(8,128)S(1)}, u32[]{:S(2)}, u32[]{:S(2)}) collective-permute-start(f32[512,128]{1,0:T(8,128)S(1)} %add.212), channel_id=1, source_target_pairs={{0,2},{1,3},{2,0},{3,1},{4,6},{5,7},{6,4},{7,5},{8,10},{9,11},{10,... | collective-permute-start | bytes 786440 | tf_op jit(solution)/shard_map/ppermute | solution.py:17
  46.7 8.6 %collective-permute-start.10 = (f32[512,128]{1,0:T(8,128)S(1)}, f32[512,128]{1,0:T(8,128)S(1)}, u32[]{:S(2)}, u32[]{:S(2)}) collective-permute-start(f32[512,128]{1,0:T(8,128)S(1)} %get-tuple-element.255), channel_id=1, source_target_pairs={{0,4},{4,0},{8,12},{12,8},{16,20},{20,16},{24,28},{28,24},{1,5},{5... | collective-permute-start | bytes 786440 | tf_op jit(solution)/shard_map/ppermute | solution.py:17
  48.7 8.1 %collective-permute-start.11 = (f32[512,128]{1,0:T(8,128)S(1)}, f32[512,128]{1,0:T(8,128)S(1)}, u32[]{:S(2)}, u32[]{:S(2)}) collective-permute-start(f32[512,128]{1,0:T(8,128)S(1)} %get-tuple-element.256), channel_id=1, source_target_pairs={{0,8},{4,12},{8,0},{12,4},{16,24},{20,28},{24,16},{28,20},{1,9},{5... | collective-permute-start | bytes 786440 | tf_op jit(solution)/shard_map/ppermute | solution.py:17
  56.8 7.3 %collective-permute-start.12 = (f32[512,128]{1,0:T(8,128)S(1)}, f32[512,128]{1,0:T(8,128)S(1)}, u32[]{:S(2)}, u32[]{:S(2)}) collective-permute-start(f32[512,128]{1,0:T(8,128)S(1)} %add.214), channel_id=1, source_target_pairs={{0,8},{4,12},{8,0},{12,4},{16,24},{20,28},{24,16},{28,20},{1,9},{5... | collective-permute-start | bytes 786440 | tf_op jit(solution)/shard_map/ppermute | solution.py:17
  57.2 7.0 %collective-permute-start.13 = (f32[512,128]{1,0:T(8,128)S(1)}, f32[512,128]{1,0:T(8,128)S(1)}, u32[]{:S(2)}, u32[]{:S(2)}) collective-permute-start(f32[512,128]{1,0:T(8,128)S(1)} %add.215), channel_id=1, source_target_pairs={{0,4},{4,0},{8,12},{12,8},{16,20},{20,16},{24,28},{28,24},{1,5},{5... | collective-permute-start | bytes 786440 | tf_op jit(solution)/shard_map/ppermute | solution.py:17
  65.0 2.0 collective-permute-start.14
  67.0 14.0 %collective-permute-start.15 = (f32[1024,128]{1,0:T(8,128)S(1)}, f32[1024,128]{1,0:T(8,128)S(1)}, u32[]{:S(2)}, u32[]{:S(2)}) collective-permute-start(f32[1024,128]{1,0:T(8,128)S(1)} %add.218), channel_id=1, source_target_pairs={{0,2},{1,3},{2,0},{3,1},{4,6},{5,7},{6,4},{7,5},{8,10},{9,11},{10,... | collective-permute-start | bytes 1572872 | tf_op jit(solution)/shard_map/ppermute | solution.py:17
  81.1 2.0 collective-permute-start.16
  84.4 14.0 %collective-permute-start.17 = (f32[1024,128]{1,0:T(8,128)S(1)}, f32[1024,128]{1,0:T(8,128)S(1)}, u32[]{:S(2)}, u32[]{:S(2)}) collective-permute-start(f32[1024,128]{1,0:T(8,128)S(1)} %shard_map.170), channel_id=1, source_target_pairs={{0,4},{4,0},{8,12},{12,8},{16,20},{20,16},{24,28},{28,24},{1,5},{5... | collective-permute-start | bytes 1572872 | tf_op jit(solution)/shard_map/ppermute | solution.py:17
  99.2 2.0 collective-permute-start.18
  102.0 2.0 collective-permute-start.19
  102.2 14.8 %collective-permute-start.20 = (f32[1024,128]{1,0:T(8,128)S(1)}, f32[1024,128]{1,0:T(8,128)S(1)}, u32[]{:S(2)}, u32[]{:S(2)}) collective-permute-start(f32[1024,128]{1,0:T(8,128)S(1)} %add.221), channel_id=1, source_target_pairs={{0,2},{1,3},{2,0},{3,1},{4,6},{5,7},{6,4},{7,5},{8,10},{9,11},{10,... | collective-permute-start | bytes 1572872 | tf_op jit(solution)/shard_map/ppermute | solution.py:17
  104.0 23.6 %collective-permute-start.21 = (f32[1024,128]{1,0:T(8,128)S(1)}, f32[1024,128]{1,0:T(8,128)S(1)}, u32[]{:S(2)}, u32[]{:S(2)}) collective-permute-start(f32[1024,128]{1,0:T(8,128)S(1)} %add.222), channel_id=1, source_target_pairs={{0,2},{1,3},{2,0},{3,1},{4,6},{5,7},{6,4},{7,5},{8,10},{9,11},{10,... | collective-permute-start | bytes 1572872 | tf_op jit(solution)/shard_map/ppermute | solution.py:17
  127.7 2.0 collective-permute-start.22
  127.8 2.6 collective-permute-start.23
  133.8 2.0 collective-permute-start.24
  136.6 3.1 %collective-permute-start.25 = (f32[1024,128]{1,0:T(8,128)S(1)}, f32[1024,128]{1,0:T(8,128)}, u32[]{:S(2)}, u32[]{:S(2)}) collective-permute-start(f32[1024,128]{1,0:T(8,128)S(1)} %shard_map.182), channel_id=1, source_target_pairs={{0,1},{1,0},{2,3},{3,2},{4,5},{5,4},{6,7},{7,6},{8,9},{9,8},{10,11... | collective-permute-start | bytes 1572872 | tf_op jit(solution)/shard_map/ppermute | solution.py:17
  136.8 14.8 %collective-permute-start.26 = (f32[1024,128]{1,0:T(8,128)S(1)}, f32[1024,128]{1,0:T(8,128)S(1)}, u32[]{:S(2)}, u32[]{:S(2)}) collective-permute-start(f32[1024,128]{1,0:T(8,128)S(1)} %add.228), channel_id=1, source_target_pairs={{0,2},{1,3},{2,0},{3,1},{4,6},{5,7},{6,4},{7,5},{8,10},{9,11},{10,... | collective-permute-start | bytes 1572872 | tf_op jit(solution)/shard_map/ppermute | solution.py:17
  140.8 21.5 %collective-permute-start.27 = (f32[1024,128]{1,0:T(8,128)S(1)}, f32[1024,128]{1,0:T(8,128)S(1)}, u32[]{:S(2)}, u32[]{:S(2)}) collective-permute-start(f32[1024,128]{1,0:T(8,128)S(1)} %add.229), channel_id=1, source_target_pairs={{0,2},{1,3},{2,0},{3,1},{4,6},{5,7},{6,4},{7,5},{8,10},{9,11},{10,... | collective-permute-start | bytes 1572872 | tf_op jit(solution)/shard_map/ppermute | solution.py:17
  162.4 2.0 collective-permute-start.28
  162.5 2.6 collective-permute-start.29
  167.4 14.4 %collective-permute-start.30 = (f32[1024,128]{1,0:T(8,128)S(1)}, f32[1024,128]{1,0:T(8,128)S(1)}, u32[]{:S(2)}, u32[]{:S(2)}) collective-permute-start(f32[1024,128]{1,0:T(8,128)S(1)} %get-tuple-element.353), channel_id=1, source_target_pairs={{0,4},{4,0},{8,12},{12,8},{16,20},{20,16},{24,28},{28,24},{1,5},{5... | collective-permute-start | bytes 1572872 | tf_op jit(solution)/shard_map/ppermute | solution.py:17
  184.8 14.0 %collective-permute-start.32 = (f32[1024,128]{1,0:T(8,128)S(1)}, f32[1024,128]{1,0:T(8,128)S(1)}, u32[]{:S(2)}, u32[]{:S(2)}) collective-permute-start(f32[1024,128]{1,0:T(8,128)S(1)} %add.243), channel_id=1, source_target_pairs={{0,2},{1,3},{2,0},{3,1},{4,6},{5,7},{6,4},{7,5},{8,10},{9,11},{10,... | collective-permute-start | bytes 1572872 | tf_op jit(solution)/shard_map/ppermute | solution.py:17
  185.4 3.6 %collective-permute-start.33 = (f32[8,128]{1,0:T(8,128)S(1)}, f32[8,128]{1,0:T(8,128)S(1)}, u32[]{:S(2)}, u32[]{:S(2)}) collective-permute-start(f32[8,128]{1,0:T(8,128)S(1)} %add_add_fusion.2), channel_id=1, source_target_pairs={{0,4},{4,0},{8,12},{12,8},{16,20},{20,16},{24,28},{28,24},{1,5},{5... | collective-permute-start | bytes 12296 | tf_op jit(solution)/shard_map/ppermute | solution.py:17
  189.0 3.6 %collective-permute-start.34 = (f32[8,128]{1,0:T(8,128)S(1)}, f32[8,128]{1,0:T(8,128)S(1)}, u32[]{:S(2)}, u32[]{:S(2)}) collective-permute-start(f32[8,128]{1,0:T(8,128)S(1)} %add.244), channel_id=1, source_target_pairs={{0,8},{4,12},{8,0},{12,4},{16,24},{20,28},{24,16},{28,20},{1,9},{5... | collective-permute-start | bytes 12296 | tf_op jit(solution)/shard_map/ppermute | solution.py:17
  198.9 2.0 collective-permute-start.35
  202.2 8.4 %collective-permute-start.36 = (f32[512,128]{1,0:T(8,128)S(1)}, f32[512,128]{1,0:T(8,128)S(1)}, u32[]{:S(2)}, u32[]{:S(2)}) collective-permute-start(f32[512,128]{1,0:T(8,128)S(1)} %get-tuple-element.384), channel_id=1, source_target_pairs={{0,4},{4,0},{8,12},{12,8},{16,20},{20,16},{24,28},{28,24},{1,5},{5... | collective-permute-start | bytes 786440 | tf_op jit(solution)/shard_map/ppermute | solution.py:17
  203.3 8.1 %collective-permute-start.37 = (f32[512,128]{1,0:T(8,128)S(1)}, f32[512,128]{1,0:T(8,128)S(1)}, u32[]{:S(2)}, u32[]{:S(2)}) collective-permute-start(f32[512,128]{1,0:T(8,128)S(1)} %get-tuple-element.385), channel_id=1, source_target_pairs={{0,8},{4,12},{8,0},{12,4},{16,24},{20,28},{24,16},{28,20},{1,9},{5... | collective-permute-start | bytes 786440 | tf_op jit(solution)/shard_map/ppermute | solution.py:17
  211.4 7.4 %collective-permute-start.38 = (f32[512,128]{1,0:T(8,128)S(1)}, f32[512,128]{1,0:T(8,128)S(1)}, u32[]{:S(2)}, u32[]{:S(2)}) collective-permute-start(f32[512,128]{1,0:T(8,128)S(1)} %add.247), channel_id=1, source_target_pairs={{0,8},{4,12},{8,0},{12,4},{16,24},{20,28},{24,16},{28,20},{1,9},{5... | collective-permute-start | bytes 786440 | tf_op jit(solution)/shard_map/ppermute | solution.py:17
  213.1 6.9 %collective-permute-start.39 = (f32[512,128]{1,0:T(8,128)S(1)}, f32[512,128]{1,0:T(8,128)S(1)}, u32[]{:S(2)}, u32[]{:S(2)}) collective-permute-start(f32[512,128]{1,0:T(8,128)S(1)} %add.248), channel_id=1, source_target_pairs={{0,4},{4,0},{8,12},{12,8},{16,20},{20,16},{24,28},{28,24},{1,5},{5... | collective-permute-start | bytes 786440 | tf_op jit(solution)/shard_map/ppermute | solution.py:17
  213.7 4.6 %collective-permute-start.40 = (f32[8,128]{1,0:T(8,128)S(1)}, f32[8,128]{1,0:T(8,128)S(1)}, u32[]{:S(2)}, u32[]{:S(2)}) collective-permute-start(f32[8,128]{1,0:T(8,128)S(1)} %add.245), channel_id=1, source_target_pairs={{0,16},{4,20},{8,24},{12,28},{16,0},{20,4},{24,8},{28,12},{1,17},{... | collective-permute-start | bytes 12296 | tf_op jit(solution)/shard_map/ppermute | solution.py:17
  222.4 8.4 %collective-permute-start.42 = (f32[512,128]{1,0:T(8,128)S(1)}, f32[512,128]{1,0:T(8,128)S(1)}, u32[]{:S(2)}, u32[]{:S(2)}) collective-permute-start(f32[512,128]{1,0:T(8,128)S(1)} %add.253), channel_id=1, source_target_pairs={{0,2},{1,3},{2,0},{3,1},{4,6},{5,7},{6,4},{7,5},{8,10},{9,11},{10,... | collective-permute-start | bytes 786440 | tf_op jit(solution)/shard_map/ppermute | solution.py:17
  233.7 7.2 %collective-permute-start.45 = (f32[256,128]{1,0:T(8,128)S(1)}, f32[256,128]{1,0:T(8,128)S(1)}, u32[]{:S(2)}, u32[]{:S(2)}) collective-permute-start(f32[256,128]{1,0:T(8,128)S(1)} %get-tuple-element.422), channel_id=1, source_target_pairs={{0,4},{4,0},{8,12},{12,8},{16,20},{20,16},{24,28},{28,24},{1,5},{5... | collective-permute-start | bytes 393224 | tf_op jit(solution)/shard_map/ppermute | solution.py:17
  234.4 6.5 %collective-permute-start.46 = (f32[256,128]{1,0:T(8,128)S(1)}, f32[256,128]{1,0:T(8,128)S(1)}, u32[]{:S(2)}, u32[]{:S(2)}) collective-permute-start(f32[256,128]{1,0:T(8,128)S(1)} %get-tuple-element.423), channel_id=1, source_target_pairs={{0,8},{4,12},{8,0},{12,4},{16,24},{20,28},{24,16},{28,20},{1,9},{5... | collective-permute-start | bytes 393224 | tf_op jit(solution)/shard_map/ppermute | solution.py:17
  236.4 6.9 %collective-permute-start.47 = (f32[256,128]{1,0:T(8,128)S(1)}, f32[256,128]{1,0:T(8,128)S(1)}, u32[]{:S(2)}, u32[]{:S(2)}) collective-permute-start(f32[256,128]{1,0:T(8,128)S(1)} %get-tuple-element.424), channel_id=1, source_target_pairs={{0,12},{4,8},{8,4},{12,0},{16,28},{20,24},{24,20},{28,16},{1,13},{... | collective-permute-start | bytes 393224 | tf_op jit(solution)/shard_map/ppermute | solution.py:17
  237.3 3.6 %collective-permute-start.48 = (f32[8,128]{1,0:T(8,128)S(1)}, f32[8,128]{1,0:T(8,128)S(1)}, u32[]{:S(2)}, u32[]{:S(2)}) collective-permute-start(f32[8,128]{1,0:T(8,128)S(1)} %add.254), channel_id=1, source_target_pairs={{0,2},{1,3},{2,0},{3,1},{4,6},{5,7},{6,4},{7,5},{8,10},{9,11},{10,... | collective-permute-start | bytes 12296 | tf_op jit(solution)/shard_map/ppermute | solution.py:17
  243.3 8.3 %collective-permute-start.49 = (f32[256,128]{1,0:T(8,128)S(1)}, f32[256,128]{1,0:T(8,128)S(1)}, u32[]{:S(2)}, u32[]{:S(2)}) collective-permute-start(f32[256,128]{1,0:T(8,128)S(1)} %add_add_fusion), channel_id=1, source_target_pairs={{0,16},{4,20},{8,24},{12,28},{16,0},{20,4},{24,8},{28,12},{1,17},{... | collective-permute-start | bytes 393224 | tf_op jit(solution)/shard_map/ppermute | solution.py:17
  251.6 6.1 %collective-permute-start.51 = (f32[256,128]{1,0:T(8,128)S(1)}, f32[256,128]{1,0:T(8,128)S(1)}, u32[]{:S(2)}, u32[]{:S(2)}) collective-permute-start(f32[256,128]{1,0:T(8,128)S(1)} %add.260), channel_id=1, source_target_pairs={{0,8},{4,12},{8,0},{12,4},{16,24},{20,28},{24,16},{28,20},{1,9},{5... | collective-permute-start | bytes 393224 | tf_op jit(solution)/shard_map/ppermute | solution.py:17
  251.7 8.0 %collective-permute-start.52 = (f32[256,128]{1,0:T(8,128)S(1)}, f32[256,128]{1,0:T(8,128)S(1)}, u32[]{:S(2)}, u32[]{:S(2)}) collective-permute-start(f32[256,128]{1,0:T(8,128)S(1)} %add.260), channel_id=1, source_target_pairs={{0,12},{4,8},{8,4},{12,0},{16,28},{20,24},{24,20},{28,16},{1,13},{... | collective-permute-start | bytes 393224 | tf_op jit(solution)/shard_map/ppermute | solution.py:17
  254.3 6.7 %collective-permute-start.50 = (f32[256,128]{1,0:T(8,128)S(1)}, f32[256,128]{1,0:T(8,128)S(1)}, u32[]{:S(2)}, u32[]{:S(2)}) collective-permute-start(f32[256,128]{1,0:T(8,128)S(1)} %add.260), channel_id=1, source_target_pairs={{0,4},{4,0},{8,12},{12,8},{16,20},{20,16},{24,28},{28,24},{1,5},{5... | collective-permute-start | bytes 393224 | tf_op jit(solution)/shard_map/ppermute | solution.py:17
  262.9 5.6 %collective-permute-start.54 = (f32[256,128]{1,0:T(8,128)S(1)}, f32[256,128]{1,0:T(8,128)S(1)}, u32[]{:S(2)}, u32[]{:S(2)}) collective-permute-start(f32[256,128]{1,0:T(8,128)S(1)} %add.262), channel_id=1, source_target_pairs={{0,2},{1,3},{2,0},{3,1},{4,6},{5,7},{6,4},{7,5},{8,10},{9,11},{10,... | collective-permute-start | bytes 393224 | tf_op jit(solution)/shard_map/ppermute | solution.py:17
  (9 other events, 24.0 us)

commit v3 on v2

--- a/solution.py
+++ b/solution.py
@@ -415,15 +415,25 @@
     return 2 if rows >= 4096 else 1
 
 
-def rows_stage(produce, consume, chunks, waits):
+def rows_stage(produce, consume, chunks, waits, ahead):
     bits = bits_of("rows")
     owns = []
+    sents = [produce(0, 1, None)]
     for chunk in range(chunks):
-        sent = produce(chunk, 1, owns[-1] if owns else None)
+        if len(sents) == chunk:
+            sents.append(produce(chunk, 1, owns[-1]))
+        sent = sents[chunk]
         kept = []
-        job = (lambda: (), lambda _: produce(chunk, 0, sent), kept.append)
-        _, got = exchange(sent, "rows", 0, [job])
+
+        def beneath(_):
+            parts = [produce(chunk, 0, sent)]
+            if ahead and chunk + 1 < chunks:
+                parts.append(produce(chunk + 1, 1, sent))
+            return parts
+
+        _, got = exchange(sent, "rows", 0, [(lambda: (), beneath, kept.extend)])
         owns.append(kept[0] + got)
+        sents += kept[1:]
     gots = [swapped(own, "rows", 1) for own in owns]
     jobs = waits.take()
     owns[-1], inputs = tied(owns[-1], [job[0]() for job in jobs])
@@ -555,7 +565,7 @@
                     base=state, final=final,
                 )
 
-            part, _ = rows_stage(produce, consume, chunks, waits)
+            part, _ = rows_stage(produce, consume, chunks, waits, True)
         if tree_level == 0:
             waits = work([], [], [load_job(("coupling", 1), 0), load_job(("factor", 1), 0, True)])
         elif tree_level == 1:
@@ -614,11 +624,19 @@
             lambda result: pending.__setitem__(plane, result),
         )
 
+    def tail_run(given):
+        rows, ticket = given
+        total = jnp.sum(sum_job(len(steps))[1](rows) + ticket)
+        return total / jnp.float32(
+            (2**LEVELS - 1) * full_width * (scenario_count + tail_index.shape[0])
+        )
+
+    tail_job = (lambda: (losses[-1], tickets[-1]), tail_run, losses.append)
     solved = {}
     for name in list(held):
         if name != ("factor", 3):
             del held[name]
-    loss_start = (lambda: samples, loss_job, losses.append)
+    loss_start = (lambda: samples, lambda given: sum_job(2)[1](loss_job(given)), losses.append)
     for tree_level in reversed(range(LEVELS)):
         group_bits = leaf_bits - tree_level
         adjoint = weights[None, :] * jax.nn.sigmoid(samples[tree_level] - tail_level)
@@ -626,15 +644,15 @@
             if tree_level == 2:
                 waits = work(
                     [
-                        later_job(3, 1), later_job(3, 0), load_job(("factor", 2), 0),
+                        later_job(3, 1), load_job(("factor", 2), 0),
                     ]
                 )
             elif tree_level == 1:
                 waits = work(
-                    [later_job(2, 0)], [load_job(("factor", 1), 0), sum_job(1)]
+                    [later_job(2, 0)], [load_job(("factor", 1), 0)]
                 )
             else:
-                waits = work([sum_job(1)], [], [load_job(("factor", 0), 0)])
+                waits = work([], [], [load_job(("factor", 0), 0)])
             adjoint = adjoint - group_sum(pending[tree_level], group_bits, leaf_index, waits)
             waits.drain()
         adjoint_round = adjoint.astype(jnp.bfloat16)
@@ -642,11 +660,11 @@
         if tree_level == 3:
             waits = work([load_job(("coupling", 3), 2), loss_start])
         elif tree_level == 2:
-            waits = work([load_job(("coupling", 2), 1), sum_job(2)])
+            waits = work([later_job(3, 0), load_job(("coupling", 2), 1), sum_job(2)])
         elif tree_level == 1:
             waits = work([load_job(("coupling", 1), 0), sum_job(1)])
         else:
-            waits = work()
+            waits = work([tail_job])
 
         def produce(chunk, side, after):
             vector = adjoint_round
@@ -669,18 +687,12 @@
                 final=final,
             )
 
-        state, solved[tree_level] = rows_stage(produce, consume, chunks, waits)
+        state, solved[tree_level] = rows_stage(produce, consume, chunks, waits, False)
         if tree_level == 0:
             gradients[0] = place_rows(*[terms for terms, _, _ in solved[0]])
             continue
         pending[tree_level - 1], gradients[tree_level] = state
-    while steps:
-        last_sum = sum_job(1)
-        last_sum[2](last_sum[1](last_sum[0]()))
-    tail_loss = jnp.sum(losses[-1] + tickets[-1]) / jnp.float32(
-        (2**LEVELS - 1) * full_width * (scenario_count + tail_index.shape[0])
-    )
-    return (gradients[0], gradients[1], gradients[2], gradients[3], tail_loss)
+    return (gradients[0], gradients[1], gradients[2], gradients[3], losses[-1])
 
 
 def solution(mesh):

time: 272 us -> 271 us (level)
  waiting for transfers between devices: 120 us -> 116 us
  starting transfers between devices: 45.8 us -> 48.9 us
    ppermute x56, waiting for transfers between devices: 120 us -> 116 us  [moved(): lax.ppermute(x, axis, [(i, i ^ flips) for i in range(lax.axis_size(axis))])]
    ppermute x56, starting transfers between devices: 45.8 us -> 48.9 us  [moved(): lax.ppermute(x, axis, [(i, i ^ flips) for i in range(lax.axis_size(axis))])]
where the time goes in v3:
time: 271 us
  waiting for transfers between devices  116 us (43%)
  Pallas kernels  88.7 us (33%)
  starting transfers between devices  48.9 us (18%)
  local copies, waits for them, and re-layouts  9.5 us (4%)
  other arithmetic  4.67 us (2%)
  between operations  3.23 us (1%)
    ppermute x56, waiting for transfers between devices, moved(): lax.ppermute(x, axis, [(i, i ^ flips) for i in range(lax.axis_size(axis))])  116 us
    ppermute x56, starting transfers between devices, moved(): lax.ppermute(x, axis, [(i, i ^ flips) for i in range(lax.axis_size(axis))])  48.9 us
    pallas_call x18, Pallas kernels, across_rows(): pl.pallas_call(functools.partial(across_body, plane, count, sides, noise_...  35.6 us
    pallas_call x12, Pallas kernels, load(): pl.pallas_call(functools.partial(load_body, plane, noise is not None), ou...  28 us
    pallas_call x21, Pallas kernels, apply_rows(): pl.pallas_call(functools.partial(apply_body, plane, chunk, side, count, b...  24.3 us
    optimization_barrier x1, local copies, waits for them, and re-layouts, tied(): return lax.optimization_barrier((first, second))  9.35 us
  transfers between devices with their start and end apart: 56, of which 48 were waited for; matrix products, arithmetic and copies ran while one was open for 4% of the time, Pallas kernels for 26%

profile of v3, /device:TPU:0, one launch (start us, length us, event | category | flops | bytes accessed | tf_op | source)
XLA Modules:
  0.0 270.8 jit_solution(5264585080371685663)
XLA Ops:
  0.7 2.4 shard_map.155
  3.1 3.0 %collective-permute-start = (f32[256,128]{1,0:T(8,128)S(1)}, f32[256,128]{1,0:T(8,128)S(1)}, u32[]{:S(2)}, u32[]{:S(2)}) collective-permute-start(f32[256,128]{1,0:T(8,128)S(1)} %get-tuple-element.227), channel_id=1, source_target_pairs={{0,4},{4,0},{8,12},{12,8},{16,20},{20,16},{24,28},{28,24},{1,5},{5... | collective-permute-start | bytes 393224 | tf_op jit(solution)/shard_map/ppermute | solution.py:17
  7.7 1.9 collective-permute-done
  9.6 2.9 %collective-permute-done.1 = f32[256,128]{1,0:T(8,128)S(1)} collective-permute-done((f32[256,128]{1,0:T(8,128)S(1)}, f32[256,128]{1,0:T(8,128)S(1)}, u32[]{:S(2)}, u32[]{:S(2)}) %collective-permute-start.1) | collective-permute-done | bytes 131104 | tf_op jit(solution)/shard_map/ppermute | solution.py:17
  13.7 2.8 %collective-permute-start.3 = (f32[256,128]{1,0:T(8,128)S(1)}, f32[256,128]{1,0:T(8,128)S(1)}, u32[]{:S(2)}, u32[]{:S(2)}) collective-permute-start(f32[256,128]{1,0:T(8,128)S(1)} %add_add_fusion.1), channel_id=1, source_target_pairs={{0,16},{4,20},{8,24},{12,28},{16,0},{20,4},{24,8},{28,12},{1,17},{... | collective-permute-start | bytes 393224 | tf_op jit(solution)/shard_map/ppermute | solution.py:17
  16.5 5.4 %collective-permute-done.3 = f32[256,128]{1,0:T(8,128)S(1)} collective-permute-done((f32[256,128]{1,0:T(8,128)S(1)}, f32[256,128]{1,0:T(8,128)S(1)}, u32[]{:S(2)}, u32[]{:S(2)}) %collective-permute-start.3) | collective-permute-done | bytes 131104 | tf_op jit(solution)/shard_map/ppermute | solution.py:17
  22.2 2.2 collective-permute-start.6
  25.5 2.2 shard_map.156
  34.4 9.3 %copy.24 = bf16[2048,2,1024]{2,0,1:T(8,128)(2,1)} copy(bf16[2048,2,1024]{2,1,0:T(2,128)(2,1)} %param.17) | data formatting | bytes 16777216 | tf_op jit(solution)/shard_map/optimization_barrier | solution.py:332
  46.7 2.0 collective-permute-start.10
  49.0 4.5 %shard_map.162.refs_0_ = f32[4096,128]{1,0:T(8,128)S(1)} custom-call(bf16[3,4096,1024]{2,1,0:T(8,128)(2,1)} %bitcast.25, bf16[1024,128]{1,0:T(8,128)(2,1)S(1)} %get-tuple-element.266.vector_ref), custom_call_target="tpu_custom_call" | custom-call | flops 128 | bytes 128 | tf_op jit(solution)/shard_map/pallas_call | solution.py:103
  53.4 1.9 collective-permute-done.10
  58.3 3.0 %shard_map.164.refs_0_ = f32[2048,128]{1,0:T(8,128)S(1)} custom-call(bf16[2,2048,1024]{2,1,0:T(8,128)(2,1)} %bitcast.31, bf16[1024,128]{1,0:T(8,128)(2,1)S(1)} %get-tuple-element.266.vector_ref), custom_call_target="tpu_custom_call" | custom-call | flops 128 | bytes 128 | tf_op jit(solution)/shard_map/pallas_call | solution.py:103
  61.3 2.2 shard_map.163
  67.6 4.5 %shard_map.168.refs_0_ = f32[4096,128]{1,0:T(8,128)S(1)} custom-call(bf16[3,4096,1024]{2,1,0:T(8,128)(2,1)} %bitcast.26, bf16[1024,128]{1,0:T(8,128)(2,1)S(1)} %fusion.15.vector_ref, f32[4096,128]{1,0:T(8,128)S(1)} %shard_map.162.refs_0_), custom_call_target="tpu_custom_call" | custom-call | flops 128 | bytes 128 | tf_op jit(solution)/shard_map/pallas_call | solution.py:103
  72.1 2.4 shard_map.167
  74.5 6.6 %collective-permute-done.15 = f32[1024,128]{1,0:T(8,128)S(1)} collective-permute-done((f32[1024,128]{1,0:T(8,128)S(1)}, f32[1024,128]{1,0:T(8,128)S(1)}, u32[]{:S(2)}, u32[]{:S(2)}) %collective-permute-start.15) | collective-permute-done | bytes 524320 | tf_op jit(solution)/shard_map/ppermute | solution.py:17
  85.5 3.5 %shard_map.171 = (bf16[4096,1024]{1,0:T(8,128)(2,1)S(1)}, f32[8,128]{1,0:T(8,128)S(1)}) custom-call(bf16[3,4096,1024]{2,1,0:T(8,128)(2,1)} %bitcast.27, f32[8,128]{1,0:T(8,128)S(1)} %get-tuple-element.288.ticket_ref), custom_call_target="tpu_custom_call" | custom-call | flops 128 | bytes 128 | tf_op jit(solution)/shard_map/pallas_call | solution.py:295
  89.0 9.4 %collective-permute-done.17 = f32[1024,128]{1,0:T(8,128)S(1)} collective-permute-done((f32[1024,128]{1,0:T(8,128)S(1)}, f32[1024,128]{1,0:T(8,128)S(1)}, u32[]{:S(2)}, u32[]{:S(2)}) %collective-permute-start.17) | collective-permute-done | bytes 524320 | tf_op jit(solution)/shard_map/ppermute | solution.py:17
  104.4 3.8 %shard_map.176 = (bf16[4096,1024]{1,0:T(8,128)(2,1)S(1)}, f32[8,128]{1,0:T(8,128)S(1)}, bf16[4096,128]{1,0:T(8,128)(2,1)S(1)}) custom-call(bf16[1,4096,1024]{2,1,0:T(8,128)(2,1)} %bitcast.35, f32[8,128]{1,0:T(8,128)S(1)} %get-tuple-element.300.ticket_ref, bf16[4096,128]{1,0:T(8,128)(2,1)} %refs_0_.5), custom_call_target="tpu_custom_call" | custom-call | flops 128 | bytes 128 | tf_op jit(solution)/shard_map/pallas_call | solution.py:295
  108.2 8.0 %collective-permute-done.20 = f32[1024,128]{1,0:T(8,128)S(1)} collective-permute-done((f32[1024,128]{1,0:T(8,128)S(1)}, f32[1024,128]{1,0:T(8,128)S(1)}, u32[]{:S(2)}, u32[]{:S(2)}) %collective-permute-start.20) | collective-permute-done | bytes 524320 | tf_op jit(solution)/shard_map/ppermute | solution.py:17
  117.4 9.5 %collective-permute-done.21 = f32[1024,128]{1,0:T(8,128)S(1)} collective-permute-done((f32[1024,128]{1,0:T(8,128)S(1)}, f32[1024,128]{1,0:T(8,128)S(1)}, u32[]{:S(2)}, u32[]{:S(2)}) %collective-permute-start.21) | collective-permute-done | bytes 524320 | tf_op jit(solution)/shard_map/ppermute | solution.py:17
  129.7 2.5 shard_map.179
  136.7 2.3 shard_map.183
  143.4 2.6 collective-permute-done.27
  147.7 3.5 %shard_map.184 = (bf16[4096,1024]{1,0:T(8,128)(2,1)S(1)}, f32[8,128]{1,0:T(8,128)S(1)}) custom-call(bf16[3,4096,1024]{2,1,0:T(8,128)(2,1)} %bitcast.28, f32[8,128]{1,0:T(8,128)S(1)} %get-tuple-element.325.ticket_ref), custom_call_target="tpu_custom_call" | custom-call | flops 128 | bytes 128 | tf_op jit(solution)/shard_map/pallas_call | solution.py:295
  152.4 9.2 %collective-permute-done.29 = f32[1024,128]{1,0:T(8,128)S(1)} collective-permute-done((f32[1024,128]{1,0:T(8,128)S(1)}, f32[1024,128]{1,0:T(8,128)S(1)}, u32[]{:S(2)}, u32[]{:S(2)}) %collective-permute-start.29) | collective-permute-done | bytes 524320 | tf_op jit(solution)/shard_map/ppermute | solution.py:17
  164.4 2.3 shard_map.187
  167.8 2.2 shard_map.188
  170.0 5.5 %shard_map.189.refs_3_ = f32[1024,128]{1,0:T(8,128)S(1)} custom-call(bf16[3,4096,1024]{2,1,0:T(8,128)(2,1)} %bitcast.29, f32[1024,128]{1,0:T(8,128)S(1)} %add.241.refs_1_, f32[1024,128]{1,0:T(8,128)S(1)} %add.242.refs_1_.refs_2_, f32[1024,128]{1,0:T(8,128)S(1)} %collective-permute-done.30.refs_1_.refs_3_, f32[1024,128]{1,0:T(8,128)S(1)} %collective-permute-done.31.refs_2_.refs_4_), custom_call_target="tpu_custom_call" | custom-call | flops 128 | bytes 128 | tf_op jit(solution)/shard_map/pallas_call | solution.py:251
  175.6 5.2 %collective-permute-done.32 = f32[1024,128]{1,0:T(8,128)S(1)} collective-permute-done((f32[1024,128]{1,0:T(8,128)S(1)}, f32[1024,128]{1,0:T(8,128)S(1)}, u32[]{:S(2)}, u32[]{:S(2)}) %collective-permute-start.32) | collective-permute-done | bytes 524320 | tf_op jit(solution)/shard_map/ppermute | solution.py:17
  184.3 2.6 collective-permute-start.35
  186.9 1.9 collective-permute-done.35
  188.8 2.2 shard_map.192
  191.1 5.5 %shard_map.193.refs_3_ = f32[1024,128]{1,0:T(8,128)S(1)} custom-call(bf16[3,4096,1024]{2,1,0:T(8,128)(2,1)} %bitcast.30, f32[1024,128]{1,0:T(8,128)S(1)} %add.241.refs_1_, f32[1024,128]{1,0:T(8,128)S(1)} %add.242.refs_1_.refs_2_, f32[1024,128]{1,0:T(8,128)S(1)} %collective-permute-done.30.refs_1_.refs_3_, f32[1024,128]{1,0:T(8,128)S(1)} %collective-permute-done.31.refs_2_.refs_4_), custom_call_target="tpu_custom_call" | custom-call | flops 128 | bytes 128 | tf_op jit(solution)/shard_map/pallas_call | solution.py:251
  203.4 3.4 %shard_map.196.refs_3_ = f32[1024,128]{1,0:T(8,128)S(1)} custom-call(bf16[2,2048,1024]{2,1,0:T(8,128)(2,1)} %bitcast.34, f32[1024,128]{1,0:T(8,128)S(1)} %add.248.refs_1_, f32[1024,128]{1,0:T(8,128)S(1)} %collective-permute-done.37.refs_1_.refs_2_, f32[1024,128]{1,0:T(8,128)S(1)} %shard_map.193.refs_3_), custom_call_target="tpu_custom_call" | custom-call | flops 128 | bytes 128 | tf_op jit(solution)/shard_map/pallas_call | solution.py:251
  206.8 2.7 collective-permute-done.38
  214.6 3.0 %collective-permute-done.40 = f32[512,128]{1,0:T(8,128)S(1)} collective-permute-done((f32[512,128]{1,0:T(8,128)S(1)}, f32[512,128]{1,0:T(8,128)S(1)}, u32[]{:S(2)}, u32[]{:S(2)}) %collective-permute-start.40) | collective-permute-done | bytes 262176 | tf_op jit(solution)/shard_map/ppermute | solution.py:17
  224.5 4.8 %collective-permute-done.44 = f32[8,128]{1,0:T(8,128)S(1)} collective-permute-done((f32[8,128]{1,0:T(8,128)S(1)}, f32[8,128]{1,0:T(8,128)S(1)}, u32[]{:S(2)}, u32[]{:S(2)}) %collective-permute-start.44) | collective-permute-done | bytes 4128 | tf_op jit(solution)/shard_map/ppermute | solution.py:17
  234.1 1.7 collective-permute-start.48
  235.9 2.0 collective-permute-done.46
  237.9 2.2 collective-permute-done.47
  240.2 1.8 collective-permute-done.48
  241.9 2.2 collective-permute-start.49
  244.1 6.0 %collective-permute-done.49 = f32[256,128]{1,0:T(8,128)S(1)} collective-permute-done((f32[256,128]{1,0:T(8,128)S(1)}, f32[256,128]{1,0:T(8,128)S(1)}, u32[]{:S(2)}, u32[]{:S(2)}) %collective-permute-start.49) | collective-permute-done | bytes 131104 | tf_op jit(solution)/shard_map/ppermute | solution.py:17
  250.4 2.5 collective-permute-start.52
  256.4 2.2 collective-permute-done.52
  264.2 3.4 %collective-permute-done.54 = f32[256,128]{1,0:T(8,128)S(1)} collective-permute-done((f32[256,128]{1,0:T(8,128)S(1)}, f32[256,128]{1,0:T(8,128)S(1)}, u32[]{:S(2)}, u32[]{:S(2)}) %collective-permute-start.54) | collective-permute-done | bytes 131104 | tf_op jit(solution)/shard_map/ppermute | solution.py:17
  (178 shorter events, 88.9 us)
Async XLA Ops:
  3.1 6.5 %collective-permute-start = (f32[256,128]{1,0:T(8,128)S(1)}, f32[256,128]{1,0:T(8,128)S(1)}, u32[]{:S(2)}, u32[]{:S(2)}) collective-permute-start(f32[256,128]{1,0:T(8,128)S(1)} %get-tuple-element.227), channel_id=1, source_target_pairs={{0,4},{4,0},{8,12},{12,8},{16,20},{20,16},{24,28},{28,24},{1,5},{5... | collective-permute-start | bytes 393224 | tf_op jit(solution)/shard_map/ppermute | solution.py:17
  6.1 6.4 %collective-permute-start.1 = (f32[256,128]{1,0:T(8,128)S(1)}, f32[256,128]{1,0:T(8,128)S(1)}, u32[]{:S(2)}, u32[]{:S(2)}) collective-permute-start(f32[256,128]{1,0:T(8,128)S(1)} %get-tuple-element.228), channel_id=1, source_target_pairs={{0,8},{4,12},{8,0},{12,4},{16,24},{20,28},{24,16},{28,20},{1,9},{5... | collective-permute-start | bytes 393224 | tf_op jit(solution)/shard_map/ppermute | solution.py:17
  7.7 6.0 %collective-permute-start.2 = (f32[256,128]{1,0:T(8,128)S(1)}, f32[256,128]{1,0:T(8,128)S(1)}, u32[]{:S(2)}, u32[]{:S(2)}) collective-permute-start(f32[256,128]{1,0:T(8,128)S(1)} %get-tuple-element.229), channel_id=1, source_target_pairs={{0,12},{4,8},{8,4},{12,0},{16,28},{20,24},{24,20},{28,16},{1,13},{... | collective-permute-start | bytes 393224 | tf_op jit(solution)/shard_map/ppermute | solution.py:17
  13.7 8.2 %collective-permute-start.3 = (f32[256,128]{1,0:T(8,128)S(1)}, f32[256,128]{1,0:T(8,128)S(1)}, u32[]{:S(2)}, u32[]{:S(2)}) collective-permute-start(f32[256,128]{1,0:T(8,128)S(1)} %add_add_fusion.1), channel_id=1, source_target_pairs={{0,16},{4,20},{8,24},{12,28},{16,0},{20,4},{24,8},{28,12},{1,17},{... | collective-permute-start | bytes 393224 | tf_op jit(solution)/shard_map/ppermute | solution.py:17
  21.9 7.4 %collective-permute-start.5 = (f32[256,128]{1,0:T(8,128)S(1)}, f32[256,128]{1,0:T(8,128)S(1)}, u32[]{:S(2)}, u32[]{:S(2)}) collective-permute-start(f32[256,128]{1,0:T(8,128)S(1)} %add.211), channel_id=1, source_target_pairs={{0,8},{4,12},{8,0},{12,4},{16,24},{20,28},{24,16},{28,20},{1,9},{5... | collective-permute-start | bytes 393224 | tf_op jit(solution)/shard_map/ppermute | solution.py:17
  22.2 7.1 %collective-permute-start.6 = (f32[256,128]{1,0:T(8,128)S(1)}, f32[256,128]{1,0:T(8,128)S(1)}, u32[]{:S(2)}, u32[]{:S(2)}) collective-permute-start(f32[256,128]{1,0:T(8,128)S(1)} %add.211), channel_id=1, source_target_pairs={{0,12},{4,8},{8,4},{12,0},{16,28},{20,24},{24,20},{28,16},{1,13},{... | collective-permute-start | bytes 393224 | tf_op jit(solution)/shard_map/ppermute | solution.py:17
  24.5 6.2 %collective-permute-start.4 = (f32[256,128]{1,0:T(8,128)S(1)}, f32[256,128]{1,0:T(8,128)S(1)}, u32[]{:S(2)}, u32[]{:S(2)}) collective-permute-start(f32[256,128]{1,0:T(8,128)S(1)} %add.211), channel_id=1, source_target_pairs={{0,4},{4,0},{8,12},{12,8},{16,20},{20,16},{24,28},{28,24},{1,5},{5... | collective-permute-start | bytes 393224 | tf_op jit(solution)/shard_map/ppermute | solution.py:17
  32.9 10.9 %collective-permute-start.8 = (f32[512,128]{1,0:T(8,128)S(1)}, f32[512,128]{1,0:T(8,128)S(1)}, u32[]{:S(2)}, u32[]{:S(2)}) collective-permute-start(f32[512,128]{1,0:T(8,128)S(1)} %add.212), channel_id=1, source_target_pairs={{0,2},{1,3},{2,0},{3,1},{4,6},{5,7},{6,4},{7,5},{8,10},{9,11},{10,... | collective-permute-start | bytes 786440 | tf_op jit(solution)/shard_map/ppermute | solution.py:17
  46.7 8.6 %collective-permute-start.10 = (f32[512,128]{1,0:T(8,128)S(1)}, f32[512,128]{1,0:T(8,128)S(1)}, u32[]{:S(2)}, u32[]{:S(2)}) collective-permute-start(f32[512,128]{1,0:T(8,128)S(1)} %get-tuple-element.256), channel_id=1, source_target_pairs={{0,4},{4,0},{8,12},{12,8},{16,20},{20,16},{24,28},{28,24},{1,5},{5... | collective-permute-start | bytes 786440 | tf_op jit(solution)/shard_map/ppermute | solution.py:17
  48.7 8.1 %collective-permute-start.11 = (f32[512,128]{1,0:T(8,128)S(1)}, f32[512,128]{1,0:T(8,128)S(1)}, u32[]{:S(2)}, u32[]{:S(2)}) collective-permute-start(f32[512,128]{1,0:T(8,128)S(1)} %get-tuple-element.257), channel_id=1, source_target_pairs={{0,8},{4,12},{8,0},{12,4},{16,24},{20,28},{24,16},{28,20},{1,9},{5... | collective-permute-start | bytes 786440 | tf_op jit(solution)/shard_map/ppermute | solution.py:17
  56.8 7.3 %collective-permute-start.12 = (f32[512,128]{1,0:T(8,128)S(1)}, f32[512,128]{1,0:T(8,128)S(1)}, u32[]{:S(2)}, u32[]{:S(2)}) collective-permute-start(f32[512,128]{1,0:T(8,128)S(1)} %add.214), channel_id=1, source_target_pairs={{0,8},{4,12},{8,0},{12,4},{16,24},{20,28},{24,16},{28,20},{1,9},{5... | collective-permute-start | bytes 786440 | tf_op jit(solution)/shard_map/ppermute | solution.py:17
  57.2 7.0 %collective-permute-start.13 = (f32[512,128]{1,0:T(8,128)S(1)}, f32[512,128]{1,0:T(8,128)S(1)}, u32[]{:S(2)}, u32[]{:S(2)}) collective-permute-start(f32[512,128]{1,0:T(8,128)S(1)} %add.215), channel_id=1, source_target_pairs={{0,4},{4,0},{8,12},{12,8},{16,20},{20,16},{24,28},{28,24},{1,5},{5... | collective-permute-start | bytes 786440 | tf_op jit(solution)/shard_map/ppermute | solution.py:17
  65.0 2.0 collective-permute-start.14
  67.0 14.0 %collective-permute-start.15 = (f32[1024,128]{1,0:T(8,128)S(1)}, f32[1024,128]{1,0:T(8,128)S(1)}, u32[]{:S(2)}, u32[]{:S(2)}) collective-permute-start(f32[1024,128]{1,0:T(8,128)S(1)} %add.218), channel_id=1, source_target_pairs={{0,2},{1,3},{2,0},{3,1},{4,6},{5,7},{6,4},{7,5},{8,10},{9,11},{10,... | collective-permute-start | bytes 1572872 | tf_op jit(solution)/shard_map/ppermute | solution.py:17
  81.1 2.0 collective-permute-start.16
  84.4 14.0 %collective-permute-start.17 = (f32[1024,128]{1,0:T(8,128)S(1)}, f32[1024,128]{1,0:T(8,128)S(1)}, u32[]{:S(2)}, u32[]{:S(2)}) collective-permute-start(f32[1024,128]{1,0:T(8,128)S(1)} %shard_map.170), channel_id=1, source_target_pairs={{0,4},{4,0},{8,12},{12,8},{16,20},{20,16},{24,28},{28,24},{1,5},{5... | collective-permute-start | bytes 1572872 | tf_op jit(solution)/shard_map/ppermute | solution.py:17
  99.2 2.0 collective-permute-start.18
  101.4 14.8 %collective-permute-start.20 = (f32[1024,128]{1,0:T(8,128)S(1)}, f32[1024,128]{1,0:T(8,128)S(1)}, u32[]{:S(2)}, u32[]{:S(2)}) collective-permute-start(f32[1024,128]{1,0:T(8,128)S(1)} %add.224), channel_id=1, source_target_pairs={{0,2},{1,3},{2,0},{3,1},{4,6},{5,7},{6,4},{7,5},{8,10},{9,11},{10,... | collective-permute-start | bytes 1572872 | tf_op jit(solution)/shard_map/ppermute | solution.py:17
  103.2 23.7 %collective-permute-start.21 = (f32[1024,128]{1,0:T(8,128)S(1)}, f32[1024,128]{1,0:T(8,128)S(1)}, u32[]{:S(2)}, u32[]{:S(2)}) collective-permute-start(f32[1024,128]{1,0:T(8,128)S(1)} %add.221), channel_id=1, source_target_pairs={{0,2},{1,3},{2,0},{3,1},{4,6},{5,7},{6,4},{7,5},{8,10},{9,11},{10,... | collective-permute-start | bytes 1572872 | tf_op jit(solution)/shard_map/ppermute | solution.py:17
  127.0 2.0 collective-permute-start.22
  127.0 2.6 collective-permute-start.23
  133.1 2.0 collective-permute-start.24
  135.8 3.1 %collective-permute-start.25 = (f32[1024,128]{1,0:T(8,128)S(1)}, f32[1024,128]{1,0:T(8,128)}, u32[]{:S(2)}, u32[]{:S(2)}) collective-permute-start(f32[1024,128]{1,0:T(8,128)S(1)} %shard_map.182), channel_id=1, source_target_pairs={{0,1},{1,0},{2,3},{3,2},{4,5},{5,4},{6,7},{7,6},{8,9},{9,8},{10,11... | collective-permute-start | bytes 1572872 | tf_op jit(solution)/shard_map/ppermute | solution.py:17
  136.1 15.1 %collective-permute-start.26 = (f32[1024,128]{1,0:T(8,128)S(1)}, f32[1024,128]{1,0:T(8,128)S(1)}, u32[]{:S(2)}, u32[]{:S(2)}) collective-permute-start(f32[1024,128]{1,0:T(8,128)S(1)} %add.228), channel_id=1, source_target_pairs={{0,2},{1,3},{2,0},{3,1},{4,6},{5,7},{6,4},{7,5},{8,10},{9,11},{10,... | collective-permute-start | bytes 1572872 | tf_op jit(solution)/shard_map/ppermute | solution.py:17
  140.1 21.5 %collective-permute-start.29 = (f32[1024,128]{1,0:T(8,128)S(1)}, f32[1024,128]{1,0:T(8,128)S(1)}, u32[]{:S(2)}, u32[]{:S(2)}) collective-permute-start(f32[1024,128]{1,0:T(8,128)S(1)} %add.229), channel_id=1, source_target_pairs={{0,2},{1,3},{2,0},{3,1},{4,6},{5,7},{6,4},{7,5},{8,10},{9,11},{10,... | collective-permute-start | bytes 1572872 | tf_op jit(solution)/shard_map/ppermute | solution.py:17
  142.3 3.7 %collective-permute-start.27 = (f32[8,128]{1,0:T(8,128)S(1)}, f32[8,128]{1,0:T(8,128)S(1)}, u32[]{:S(2)}, u32[]{:S(2)}) collective-permute-start(f32[8,128]{1,0:T(8,128)S(1)} %add_add_fusion.2), channel_id=1, source_target_pairs={{0,4},{4,0},{8,12},{12,8},{16,20},{20,16},{24,28},{28,24},{1,5},{5... | collective-permute-start | bytes 12296 | tf_op jit(solution)/shard_map/ppermute | solution.py:17
  146.0 5.2 %collective-permute-start.28 = (f32[8,128]{1,0:T(8,128)S(1)}, f32[8,128]{1,0:T(8,128)S(1)}, u32[]{:S(2)}, u32[]{:S(2)}) collective-permute-start(f32[8,128]{1,0:T(8,128)S(1)} %add.239), channel_id=1, source_target_pairs={{0,8},{4,12},{8,0},{12,4},{16,24},{20,28},{24,16},{28,20},{1,9},{5... | collective-permute-start | bytes 12296 | tf_op jit(solution)/shard_map/ppermute | solution.py:17
  161.7 2.0 collective-permute-start.30
  161.7 2.6 collective-permute-start.31
  166.7 14.0 %collective-permute-start.32 = (f32[1024,128]{1,0:T(8,128)S(1)}, f32[1024,128]{1,0:T(8,128)S(1)}, u32[]{:S(2)}, u32[]{:S(2)}) collective-permute-start(f32[1024,128]{1,0:T(8,128)S(1)} %get-tuple-element.354), channel_id=1, source_target_pairs={{0,4},{4,0},{8,12},{12,8},{16,20},{20,16},{24,28},{28,24},{1,5},{5... | collective-permute-start | bytes 1572872 | tf_op jit(solution)/shard_map/ppermute | solution.py:17
  183.7 14.0 %collective-permute-start.34 = (f32[1024,128]{1,0:T(8,128)S(1)}, f32[1024,128]{1,0:T(8,128)S(1)}, u32[]{:S(2)}, u32[]{:S(2)}) collective-permute-start(f32[1024,128]{1,0:T(8,128)S(1)} %add.245), channel_id=1, source_target_pairs={{0,2},{1,3},{2,0},{3,1},{4,6},{5,7},{6,4},{7,5},{8,10},{9,11},{10,... | collective-permute-start | bytes 1572872 | tf_op jit(solution)/shard_map/ppermute | solution.py:17
  184.3 4.5 %collective-permute-start.35 = (f32[8,128]{1,0:T(8,128)S(1)}, f32[8,128]{1,0:T(8,128)S(1)}, u32[]{:S(2)}, u32[]{:S(2)}) collective-permute-start(f32[8,128]{1,0:T(8,128)S(1)} %add.240), channel_id=1, source_target_pairs={{0,16},{4,20},{8,24},{12,28},{16,0},{20,4},{24,8},{28,12},{1,17},{... | collective-permute-start | bytes 12296 | tf_op jit(solution)/shard_map/ppermute | solution.py:17
  188.8 7.8 %collective-permute-start.36 = (f32[8,128]{1,0:T(8,128)S(1)}, f32[8,128]{1,0:T(8,128)S(1)}, u32[]{:S(2)}, u32[]{:S(2)}) collective-permute-start(f32[8,128]{1,0:T(8,128)S(1)} %add.246), channel_id=1, source_target_pairs={{0,1},{1,0},{2,3},{3,2},{4,5},{5,4},{6,7},{7,6},{8,9},{9,8},{10,11... | collective-permute-start | bytes 12296 | tf_op jit(solution)/shard_map/ppermute | solution.py:17
  197.8 2.0 collective-permute-start.37
  201.1 8.4 %collective-permute-start.38 = (f32[512,128]{1,0:T(8,128)S(1)}, f32[512,128]{1,0:T(8,128)S(1)}, u32[]{:S(2)}, u32[]{:S(2)}) collective-permute-start(f32[512,128]{1,0:T(8,128)S(1)} %get-tuple-element.385), channel_id=1, source_target_pairs={{0,4},{4,0},{8,12},{12,8},{16,20},{20,16},{24,28},{28,24},{1,5},{5... | collective-permute-start | bytes 786440 | tf_op jit(solution)/shard_map/ppermute | solution.py:17
  202.2 8.1 %collective-permute-start.39 = (f32[512,128]{1,0:T(8,128)S(1)}, f32[512,128]{1,0:T(8,128)S(1)}, u32[]{:S(2)}, u32[]{:S(2)}) collective-permute-start(f32[512,128]{1,0:T(8,128)S(1)} %get-tuple-element.386), channel_id=1, source_target_pairs={{0,8},{4,12},{8,0},{12,4},{16,24},{20,28},{24,16},{28,20},{1,9},{5... | collective-permute-start | bytes 786440 | tf_op jit(solution)/shard_map/ppermute | solution.py:17
  210.3 7.3 %collective-permute-start.40 = (f32[512,128]{1,0:T(8,128)S(1)}, f32[512,128]{1,0:T(8,128)S(1)}, u32[]{:S(2)}, u32[]{:S(2)}) collective-permute-start(f32[512,128]{1,0:T(8,128)S(1)} %add.249), channel_id=1, source_target_pairs={{0,8},{4,12},{8,0},{12,4},{16,24},{20,28},{24,16},{28,20},{1,9},{5... | collective-permute-start | bytes 786440 | tf_op jit(solution)/shard_map/ppermute | solution.py:17
  211.6 6.9 %collective-permute-start.41 = (f32[512,128]{1,0:T(8,128)S(1)}, f32[512,128]{1,0:T(8,128)S(1)}, u32[]{:S(2)}, u32[]{:S(2)}) collective-permute-start(f32[512,128]{1,0:T(8,128)S(1)} %add.250), channel_id=1, source_target_pairs={{0,4},{4,0},{8,12},{12,8},{16,20},{20,16},{24,28},{28,24},{1,5},{5... | collective-permute-start | bytes 786440 | tf_op jit(solution)/shard_map/ppermute | solution.py:17
  220.9 8.5 %collective-permute-start.43 = (f32[512,128]{1,0:T(8,128)S(1)}, f32[512,128]{1,0:T(8,128)S(1)}, u32[]{:S(2)}, u32[]{:S(2)}) collective-permute-start(f32[512,128]{1,0:T(8,128)S(1)} %add.254), channel_id=1, source_target_pairs={{0,2},{1,3},{2,0},{3,1},{4,6},{5,7},{6,4},{7,5},{8,10},{9,11},{10,... | collective-permute-start | bytes 786440 | tf_op jit(solution)/shard_map/ppermute | solution.py:17
  221.9 7.5 %collective-permute-start.44 = (f32[8,128]{1,0:T(8,128)S(1)}, f32[8,128]{1,0:T(8,128)S(1)}, u32[]{:S(2)}, u32[]{:S(2)}) collective-permute-start(f32[8,128]{1,0:T(8,128)S(1)} %add.247), channel_id=1, source_target_pairs={{0,2},{1,3},{2,0},{3,1},{4,6},{5,7},{6,4},{7,5},{8,10},{9,11},{10,... | collective-permute-start | bytes 12296 | tf_op jit(solution)/shard_map/ppermute | solution.py:17
  232.3 5.6 %collective-permute-start.46 = (f32[256,128]{1,0:T(8,128)S(1)}, f32[256,128]{1,0:T(8,128)S(1)}, u32[]{:S(2)}, u32[]{:S(2)}) collective-permute-start(f32[256,128]{1,0:T(8,128)S(1)} %get-tuple-element.420), channel_id=1, source_target_pairs={{0,4},{4,0},{8,12},{12,8},{16,20},{20,16},{24,28},{28,24},{1,5},{5... | collective-permute-start | bytes 393224 | tf_op jit(solution)/shard_map/ppermute | solution.py:17
  233.8 6.4 %collective-permute-start.47 = (f32[256,128]{1,0:T(8,128)S(1)}, f32[256,128]{1,0:T(8,128)S(1)}, u32[]{:S(2)}, u32[]{:S(2)}) collective-permute-start(f32[256,128]{1,0:T(8,128)S(1)} %get-tuple-element.421), channel_id=1, source_target_pairs={{0,8},{4,12},{8,0},{12,4},{16,24},{20,28},{24,16},{28,20},{1,9},{5... | collective-permute-start | bytes 393224 | tf_op jit(solution)/shard_map/ppermute | solution.py:17
  234.1 7.8 %collective-permute-start.48 = (f32[256,128]{1,0:T(8,128)S(1)}, f32[256,128]{1,0:T(8,128)S(1)}, u32[]{:S(2)}, u32[]{:S(2)}) collective-permute-start(f32[256,128]{1,0:T(8,128)S(1)} %get-tuple-element.422), channel_id=1, source_target_pairs={{0,12},{4,8},{8,4},{12,0},{16,28},{20,24},{24,20},{28,16},{1,13},{... | collective-permute-start | bytes 393224 | tf_op jit(solution)/shard_map/ppermute | solution.py:17
  241.9 8.2 %collective-permute-start.49 = (f32[256,128]{1,0:T(8,128)S(1)}, f32[256,128]{1,0:T(8,128)S(1)}, u32[]{:S(2)}, u32[]{:S(2)}) collective-permute-start(f32[256,128]{1,0:T(8,128)S(1)} %add_add_fusion), channel_id=1, source_target_pairs={{0,16},{4,20},{8,24},{12,28},{16,0},{20,4},{24,8},{28,12},{1,17},{... | collective-permute-start | bytes 393224 | tf_op jit(solution)/shard_map/ppermute | solution.py:17
  250.1 6.3 %collective-permute-start.51 = (f32[256,128]{1,0:T(8,128)S(1)}, f32[256,128]{1,0:T(8,128)S(1)}, u32[]{:S(2)}, u32[]{:S(2)}) collective-permute-start(f32[256,128]{1,0:T(8,128)S(1)} %add.260), channel_id=1, source_target_pairs={{0,8},{4,12},{8,0},{12,4},{16,24},{20,28},{24,16},{28,20},{1,9},{5... | collective-permute-start | bytes 393224 | tf_op jit(solution)/shard_map/ppermute | solution.py:17
  250.4 8.3 %collective-permute-start.52 = (f32[256,128]{1,0:T(8,128)S(1)}, f32[256,128]{1,0:T(8,128)S(1)}, u32[]{:S(2)}, u32[]{:S(2)}) collective-permute-start(f32[256,128]{1,0:T(8,128)S(1)} %add.260), channel_id=1, source_target_pairs={{0,12},{4,8},{8,4},{12,0},{16,28},{20,24},{24,20},{28,16},{1,13},{... | collective-permute-start | bytes 393224 | tf_op jit(solution)/shard_map/ppermute | solution.py:17
  252.9 7.1 %collective-permute-start.50 = (f32[256,128]{1,0:T(8,128)S(1)}, f32[256,128]{1,0:T(8,128)S(1)}, u32[]{:S(2)}, u32[]{:S(2)}) collective-permute-start(f32[256,128]{1,0:T(8,128)S(1)} %add.260), channel_id=1, source_target_pairs={{0,4},{4,0},{8,12},{12,8},{16,20},{20,16},{24,28},{28,24},{1,5},{5... | collective-permute-start | bytes 393224 | tf_op jit(solution)/shard_map/ppermute | solution.py:17
  261.9 5.6 %collective-permute-start.54 = (f32[256,128]{1,0:T(8,128)S(1)}, f32[256,128]{1,0:T(8,128)S(1)}, u32[]{:S(2)}, u32[]{:S(2)}) collective-permute-start(f32[256,128]{1,0:T(8,128)S(1)} %add.262), channel_id=1, source_target_pairs={{0,2},{1,3},{2,0},{3,1},{4,6},{5,7},{6,4},{7,5},{8,10},{9,11},{10,... | collective-permute-start | bytes 393224 | tf_op jit(solution)/shard_map/ppermute | solution.py:17
  (9 other events, 24.4 us)
